TPU v7x, 256 devices: a whole 4x4x8 slice. The times are simulated.
256 devices in a mesh: section: 8 (over x, y_hi), dp: 32 (over y_lo, z, core).
Axes of the slice: x: 4, y: 4 (y_hi: 2, y_lo: 2; y = y_hi * 2 + y_lo), z: 8, core: 2. Of those that a mesh axis runs over, the one named last changes fastest.
Arguments:
- latent: bfloat16 [8192, 1536], P('dp'), may hold values from -6 to 6
- target: bfloat16 [8192, 1536], P('dp'), may hold values from -6 to 6
- camera_of_token: int32 [8192], P('dp'), may hold values from 0 to 5
- timestep_indices: int32 [2], replicated, may hold values from 0 to 49
- camera_embedding_table: bfloat16 [6, 1536], replicated, may hold values from -3 to 3
- timestep_embedding_table: bfloat16 [50, 1536], replicated, may hold values from -2.5 to 2.5
- layer_norm_gain: float32 [8, 1536], P('section'), may hold values from 0.25 to 1.75
- frozen_weight: bfloat16 [8, 1536, 1536], P('section', 'dp'), may hold values from -0.15625 to 0.15625
- adapter_down_weight: bfloat16 [8, 64, 1536], P('section'), may hold values from -0.15625 to 0.15625
- adapter_up_weight: bfloat16 [8, 64, 1536], P('section'), may hold values from -0.75 to 0.75
Outputs:
- grad_down: float32 [8, 64, 1536], P('section', None, 'dp')
- grad_up: float32 [8, 64, 1536], P('section', None, 'dp')
Inputs may be any that keep to these rules, and one draw needn't show every extreme that they name: `timestep_indices`: indices of rows of timestep_embedding_table.
All inputs are finite; a program needn't handle non-finite values.
Results may differ from a plain program's by a relative error of at most 0.024.
Values may be sent and summed in bfloat16 or wider, within the bound.
No kernel may reach another device: no remote copies, remote signals or barrier semaphores. Data moves between devices by JAX's collectives and lax.ppermute only.
A program may use at most 64 MiB of HBM per device.

v0:
```python
import math

import jax
import jax.numpy as jnp
from jax import lax
from jax.sharding import PartitionSpec as P

MICRO = 4


BLEND = 0.5
ADAPTER_SCALE = 0.5
EPSILON = 1e-06


def from_behind(block, axis, distance):
    devices = range(lax.axis_size(axis))
    route = [((i - distance) % len(devices), i) for i in devices]
    return lax.ppermute(block, axis, route)


def in_one_piece(arrays, axis, dim, along):
    widths = [a.shape[along] for a in arrays]
    both = jnp.concatenate(arrays, axis=along)
    out = lax.psum_scatter(both, axis, scatter_dimension=dim, tiled=True)
    return tuple(jnp.split(out, [sum(widths[:k]) for k in range(1, len(widths))], axis=along))


def forward_layer_pass(
    hidden_state, layer_weight, down_weight_rows, up_weight_rows, gain_row, modulate_row
):
    hidden_float = hidden_state.astype(jnp.float32)
    inverse_rms = lax.rsqrt(jnp.mean(hidden_float * hidden_float, axis=-1, keepdims=True) + EPSILON)
    normalized_hidden = (hidden_float * inverse_rms * (gain_row * modulate_row)).astype(
        jnp.bfloat16
    )
    low_rank_hidden = lax.dot_general(
        normalized_hidden,
        down_weight_rows,
        (((1,), (1,)), ((), ())),
        preferred_element_type=jnp.float32,
    ).astype(jnp.bfloat16)
    preactivation = jnp.dot(
        normalized_hidden, layer_weight, preferred_element_type=jnp.float32
    ) + ADAPTER_SCALE * jnp.dot(low_rank_hidden, up_weight_rows, preferred_element_type=jnp.float32)
    output = (hidden_float + jax.nn.silu(preactivation)).astype(jnp.bfloat16)
    return (output, normalized_hidden, low_rank_hidden, preactivation)


def backward_layer_pass(
    hidden_state,
    normalized_hidden,
    low_rank_hidden,
    preactivation,
    output_gradient,
    layer_weight,
    down_weight_rows,
    up_weight_rows,
    gain_row,
    modulate_row,
):
    sigmoid_value = jax.nn.sigmoid(preactivation)
    preactivation_gradient = (
        output_gradient * sigmoid_value * (1.0 + preactivation * (1.0 - sigmoid_value))
    ).astype(jnp.bfloat16)
    low_rank_gradient = (
        ADAPTER_SCALE
        * lax.dot_general(
            preactivation_gradient,
            up_weight_rows,
            (((1,), (1,)), ((), ())),
            preferred_element_type=jnp.float32,
        )
    ).astype(jnp.bfloat16)
    norm_grad = lax.dot_general(
        preactivation_gradient,
        layer_weight,
        (((1,), (1,)), ((), ())),
        preferred_element_type=jnp.float32,
    ) + jnp.dot(low_rank_gradient, down_weight_rows, preferred_element_type=jnp.float32)
    up_gradient_term = ADAPTER_SCALE * lax.dot_general(
        low_rank_hidden,
        preactivation_gradient,
        (((0,), (0,)), ((), ())),
        preferred_element_type=jnp.float32,
    )
    down_gradient_term = lax.dot_general(
        low_rank_gradient,
        normalized_hidden,
        (((0,), (0,)), ((), ())),
        preferred_element_type=jnp.float32,
    )
    hidden_float = hidden_state.astype(jnp.float32)
    inverse_rms = lax.rsqrt(jnp.mean(hidden_float * hidden_float, axis=-1, keepdims=True) + EPSILON)
    scaled = hidden_float * inverse_rms
    scaled_grad = norm_grad * (gain_row * modulate_row)
    hidden_gradient = output_gradient + inverse_rms * (
        scaled_grad - scaled * jnp.mean(scaled_grad * scaled, axis=-1, keepdims=True)
    )
    return (hidden_gradient, down_gradient_term, up_gradient_term)


def pick_block(store, first_index, second_index):
    anchor = jnp.zeros((), jnp.int32)
    starts = (first_index, second_index) + (anchor,) * (store.ndim - 2)
    piece = lax.dynamic_slice(store, starts, (1, 1) + store.shape[2:])
    return piece[0, 0]


def place_block(store, value, first_index, second_index):
    anchor = jnp.zeros((), jnp.int32)
    starts = (first_index, second_index) + (anchor,) * (store.ndim - 2)
    return lax.dynamic_update_slice(store, value[None, None], starts)


def local(
    latent,
    target,
    camera_of_token,
    timestep_indices,
    camera_embedding_table,
    timestep_embedding_table,
    layer_norm_gain,
    frozen_weight,
    adapter_down_weight,
    adapter_up_weight,
):
    sections = lax.axis_size("section")
    position = lax.axis_index("section")
    layer_weight = lax.all_gather(frozen_weight[0], "dp", axis=0, tiled=True)
    down_weight_rows = adapter_down_weight[0]
    up_weight_rows = adapter_up_weight[0]
    gain_row = layer_norm_gain[0]
    feature_width = latent.shape[1]
    rank_width = down_weight_rows.shape[0]
    scale_factor = 1.0 / math.sqrt(latent.shape[0] * lax.axis_size("dp"))
    camera_rows = jnp.dot(
        jax.nn.one_hot(camera_of_token, camera_embedding_table.shape[0], dtype=jnp.bfloat16),
        camera_embedding_table,
        preferred_element_type=jnp.float32,
    )
    timestep_modulation = 1.0 + jnp.dot(
        jax.nn.one_hot(timestep_indices, timestep_embedding_table.shape[0], dtype=jnp.bfloat16),
        timestep_embedding_table,
        preferred_element_type=jnp.float32,
    )
    block_count = MICRO
    block_rows = latent.shape[0] // block_count
    latent_blocks = latent.reshape(block_count, block_rows, feature_width)
    target_blocks = target.reshape(block_count, block_rows, feature_width)
    camera_blocks = camera_rows.reshape(block_count, block_rows, feature_width)
    is_first = position == 0
    is_last = position == sections - 1
    tick_total = 2 * sections + block_count - 1
    zero_index = jnp.zeros((), jnp.int32)

    def forward_tick(tick_index, carry):
        offset = tick_index - position
        round_index = (offset >= sections).astype(jnp.int32)
        block_index = offset - round_index * sections
        active = (offset >= 0) & (block_index < block_count)
        safe_block = jnp.clip(block_index, 0, block_count - 1)

        def forward_compute(current):
            (
                received,
                hidden_store,
                normed_store,
                low_store,
                pre_store,
                blend_store,
                adjoint_store,
            ) = current
            latent_block = lax.dynamic_index_in_dim(
                latent_blocks, safe_block, 0, keepdims=False
            ).astype(jnp.float32)
            camera_block = lax.dynamic_index_in_dim(camera_blocks, safe_block, 0, keepdims=False)
            target_block = lax.dynamic_index_in_dim(
                target_blocks, safe_block, 0, keepdims=False
            ).astype(jnp.float32)
            starting = jnp.where(round_index == 0, latent_block, received.astype(jnp.float32))
            first_hidden = (starting + camera_block).astype(jnp.bfloat16)
            hidden_state = jnp.where(is_first, first_hidden, received)
            modulate_row = jnp.where(
                round_index == 0, timestep_modulation[0], timestep_modulation[1]
            )
            output, normalized_hidden, low_rank_hidden, preactivation = forward_layer_pass(
                hidden_state, layer_weight, down_weight_rows, up_weight_rows, gain_row, modulate_row
            )
            hidden_store = place_block(hidden_store, hidden_state, round_index, safe_block)
            normed_store = place_block(normed_store, normalized_hidden, round_index, safe_block)
            low_store = place_block(low_store, low_rank_hidden, round_index, safe_block)
            pre_store = place_block(pre_store, preactivation, round_index, safe_block)
            previous_blend = lax.dynamic_index_in_dim(blend_store, safe_block, 0, keepdims=False)
            previous = jnp.where(round_index == 0, latent_block, previous_blend.astype(jnp.float32))
            blended = BLEND * (previous + output.astype(jnp.float32))
            blend_rounded = blended.astype(jnp.bfloat16)
            keep_blend = jnp.where(round_index == 0, blend_rounded, previous_blend)
            blend_store = lax.dynamic_update_slice(
                blend_store, keep_blend[None], (safe_block, zero_index, zero_index)
            )
            squashed = jnp.tanh(blended)
            adjoint = target_block * (1.0 - squashed * squashed) * scale_factor
            previous_adjoint = lax.dynamic_index_in_dim(
                adjoint_store, safe_block, 0, keepdims=False
            )
            keep_adjoint = jnp.where(round_index == 1, adjoint, previous_adjoint)
            adjoint_store = lax.dynamic_update_slice(
                adjoint_store, keep_adjoint[None], (safe_block, zero_index, zero_index)
            )
            outgoing = jnp.where(is_last, blend_rounded, output)
            return (
                outgoing,
                (hidden_store, normed_store, low_store, pre_store, blend_store, adjoint_store),
            )

        def forward_skip_block(current):
            return (jnp.zeros_like(current[0]), tuple(current[1:]))

        outgoing, stores = lax.cond(active, forward_compute, forward_skip_block, carry)
        incoming = from_behind(outgoing, "section", 1)
        return (incoming,) + tuple(stores)

    forward_start = (
        jnp.zeros((block_rows, feature_width), jnp.bfloat16),
        jnp.zeros((2, block_count, block_rows, feature_width), jnp.bfloat16),
        jnp.zeros((2, block_count, block_rows, feature_width), jnp.bfloat16),
        jnp.zeros((2, block_count, block_rows, rank_width), jnp.bfloat16),
        jnp.zeros((2, block_count, block_rows, feature_width), jnp.float32),
        jnp.zeros((block_count, block_rows, feature_width), jnp.bfloat16),
        jnp.zeros((block_count, block_rows, feature_width), jnp.float32),
    )
    forward_end = lax.fori_loop(0, tick_total, forward_tick, forward_start)
    hidden_store, normed_store, low_store, pre_store, blend_store, adjoint_store = forward_end[1:]
    back_position = sections - 1 - position

    def backward_tick(tick_index, carry):
        offset = tick_index - back_position
        round_back = (offset >= sections).astype(jnp.int32)
        block_index = offset - round_back * sections
        active = (offset >= 0) & (block_index < block_count)
        safe_block = jnp.clip(block_index, 0, block_count - 1)
        forward_round = 1 - round_back

        def backward_compute(current):
            received, down_sum, up_sum = current
            adjoint_block = lax.dynamic_index_in_dim(adjoint_store, safe_block, 0, keepdims=False)
            received_float = received.astype(jnp.float32)
            last_cotangent = jnp.where(
                round_back == 0,
                BLEND * adjoint_block,
                BLEND * (BLEND * adjoint_block + received_float),
            )
            output_gradient = jnp.where(is_last, last_cotangent, received_float)
            hidden_state = pick_block(hidden_store, forward_round, safe_block)
            normalized_hidden = pick_block(normed_store, forward_round, safe_block)
            low_rank_hidden = pick_block(low_store, forward_round, safe_block)
            preactivation = pick_block(pre_store, forward_round, safe_block)
            modulate_row = jnp.where(
                forward_round == 0, timestep_modulation[0], timestep_modulation[1]
            )
            hidden_gradient, down_gradient_term, up_gradient_term = backward_layer_pass(
                hidden_state,
                normalized_hidden,
                low_rank_hidden,
                preactivation,
                output_gradient,
                layer_weight,
                down_weight_rows,
                up_weight_rows,
                gain_row,
                modulate_row,
            )
            return (
                hidden_gradient.astype(jnp.bfloat16),
                down_sum + down_gradient_term,
                up_sum + up_gradient_term,
            )

        def backward_skip_block(current):
            return (jnp.zeros_like(current[0]), current[1], current[2])

        outgoing, down_sum, up_sum = lax.cond(active, backward_compute, backward_skip_block, carry)
        incoming = from_behind(outgoing, "section", -1)
        return (incoming, down_sum, up_sum)

    backward_start = (
        jnp.zeros((block_rows, feature_width), jnp.bfloat16),
        jnp.zeros((rank_width, feature_width), jnp.float32),
        jnp.zeros((rank_width, feature_width), jnp.float32),
    )
    backward_end = lax.fori_loop(0, tick_total, backward_tick, backward_start)
    down_part, up_part = in_one_piece((backward_end[1], backward_end[2]), "dp", 1, 0)
    return (down_part[None], up_part[None])


def solution(mesh):
    in_specs = (
        P("dp", None),
        P("dp", None),
        P("dp"),
        P(),
        P(),
        P(),
        P("section", None),
        P("section", "dp", None),
        P("section", None, None),
        P("section", None, None),
    )
    out_specs = (P("section", None, "dp"), P("section", None, "dp"))
    return jax.shard_map(local, mesh=mesh, in_specs=in_specs, out_specs=out_specs, check_vma=False)
```

profile of v0, /device:TPU:32, one launch (start us, length us, event | category | flops | bytes accessed | tf_op | source)
XLA Modules:
  0.0 964.8 jit_solution(15846906296157261650)
XLA Ops:
  12.0 67.5 %all-gather.3.cloned.1.call-done = bf16[1,1536,1536]{2,1,0:T(8,128)(2,1)} async-done(((bf16[1,48,1536]{2,1,0:T(8,128)(2,1)}), bf16[1,1536,1536]{2,1,0:T(8,128)(2,1)}) %all-gather.3.cloned.1.call-update) | async-done | bytes 4718608 | tf_op jit(solution)/shard_map/all_gather | solution.py:130
  85.4 399.7 %while.42 = (s32[]{:T(128)}, bf16[64,1536]{1,0:T(8,128)(2,1)}, bf16[2,4,64,1536]{3,2,1,0:T(8,128)(2,1)S(1)}, bf16[2,4,64,1536]{3,2,1,0:T(8,128)(2,1)}, bf16[2,4,...) while((s32[]{:T(128)}, bf16[64,1536]{1,0:T(8,128)(2,1)}, ...), condition=%wide.region_4.5_spmd, body=%wide.region_0.4_spmd.sunk | while | flops 332176448 | bytes 21725468 | solution.py:233
  85.4 13.7 %conditional.4 = (bf16[64,1536]{1,0:T(8,128)(2,1)}, bf16[2,4,64,1536]{3,2,1,0:T(8,128)(2,1)S(1)}, bf16[2,4,64,1536]{3,2,1,0:T(8,128)(2,1)}, bf16[2,4,64,64]{3,2,...) conditional(s32[]{:T(128)} %convert_element_type.177, ...), branch_computations={%region_1.1_spmd, %region_2.3_spmd} | conditional | flops 332176448 | bytes 20152056 | solution.py:220
  110.7 13.7 %conditional.4 = (bf16[64,1536]{1,0:T(8,128)(2,1)}, bf16[2,4,64,1536]{3,2,1,0:T(8,128)(2,1)S(1)}, bf16[2,4,64,1536]{3,2,1,0:T(8,128)(2,1)}, bf16[2,4,64,64]{3,2,...) conditional(s32[]{:T(128)} %convert_element_type.177, ...), branch_computations={%region_1.1_spmd, %region_2.3_spmd} | conditional | flops 332176448 | bytes 20152056 | solution.py:220
  135.2 13.7 %conditional.4 = (bf16[64,1536]{1,0:T(8,128)(2,1)}, bf16[2,4,64,1536]{3,2,1,0:T(8,128)(2,1)S(1)}, bf16[2,4,64,1536]{3,2,1,0:T(8,128)(2,1)}, bf16[2,4,64,64]{3,2,...) conditional(s32[]{:T(128)} %convert_element_type.177, ...), branch_computations={%region_1.1_spmd, %region_2.3_spmd} | conditional | flops 332176448 | bytes 20152056 | solution.py:220
  159.0 13.7 %conditional.4 = (bf16[64,1536]{1,0:T(8,128)(2,1)}, bf16[2,4,64,1536]{3,2,1,0:T(8,128)(2,1)S(1)}, bf16[2,4,64,1536]{3,2,1,0:T(8,128)(2,1)}, bf16[2,4,64,64]{3,2,...) conditional(s32[]{:T(128)} %convert_element_type.177, ...), branch_computations={%region_1.1_spmd, %region_2.3_spmd} | conditional | flops 332176448 | bytes 20152056 | solution.py:220
  210.2 11.8 %collective-permute-start = (bf16[64,1536]{1,0:T(8,128)(2,1)}, bf16[64,1536]{1,0:T(8,128)(2,1)S(1)}, u32[]{:S(2)}, u32[]{:S(2)}) collective-permute-start(bf16[64,1536]{1,0:T(8,128)(2,1)} %get-tuple-element.1111), channel_id=1, source_target_pairs={{224,0},{0,32},{32,64},{64,96},{96,128},{128,160},{160,192},{192,2... | collective-permute-start | bytes 589832 | tf_op jit(solution)/shard_map/while/body/eval_jaxpr/ppermute | solution.py:19
  231.7 19.0 %collective-permute-done = bf16[64,1536]{1,0:T(8,128)(2,1)S(1)} collective-permute-done((bf16[64,1536]{1,0:T(8,128)(2,1)}, bf16[64,1536]{1,0:T(8,128)(2,1)S(1)}, u32[]{:S(2)}, u32[]{:S(2)}) %collective-permute-start) | collective-permute-done | bytes 196640 | tf_op jit(solution)/shard_map/while/body/eval_jaxpr/ppermute | solution.py:19
  251.3 13.7 %conditional.4 = (bf16[64,1536]{1,0:T(8,128)(2,1)}, bf16[2,4,64,1536]{3,2,1,0:T(8,128)(2,1)S(1)}, bf16[2,4,64,1536]{3,2,1,0:T(8,128)(2,1)}, bf16[2,4,64,64]{3,2,...) conditional(s32[]{:T(128)} %convert_element_type.177, ...), branch_computations={%region_1.1_spmd, %region_2.3_spmd} | conditional | flops 332176448 | bytes 20152056 | solution.py:220
  275.2 13.7 %conditional.4 = (bf16[64,1536]{1,0:T(8,128)(2,1)}, bf16[2,4,64,1536]{3,2,1,0:T(8,128)(2,1)S(1)}, bf16[2,4,64,1536]{3,2,1,0:T(8,128)(2,1)}, bf16[2,4,64,64]{3,2,...) conditional(s32[]{:T(128)} %convert_element_type.177, ...), branch_computations={%region_1.1_spmd, %region_2.3_spmd} | conditional | flops 332176448 | bytes 20152056 | solution.py:220
  299.0 13.7 %conditional.4 = (bf16[64,1536]{1,0:T(8,128)(2,1)}, bf16[2,4,64,1536]{3,2,1,0:T(8,128)(2,1)S(1)}, bf16[2,4,64,1536]{3,2,1,0:T(8,128)(2,1)}, bf16[2,4,64,64]{3,2,...) conditional(s32[]{:T(128)} %convert_element_type.177, ...), branch_computations={%region_1.1_spmd, %region_2.3_spmd} | conditional | flops 332176448 | bytes 20152056 | solution.py:220
  322.9 13.7 %conditional.4 = (bf16[64,1536]{1,0:T(8,128)(2,1)}, bf16[2,4,64,1536]{3,2,1,0:T(8,128)(2,1)S(1)}, bf16[2,4,64,1536]{3,2,1,0:T(8,128)(2,1)}, bf16[2,4,64,64]{3,2,...) conditional(s32[]{:T(128)} %convert_element_type.177, ...), branch_computations={%region_1.1_spmd, %region_2.3_spmd} | conditional | flops 332176448 | bytes 20152056 | solution.py:220
  395.5 17.3 %collective-permute-done = bf16[64,1536]{1,0:T(8,128)(2,1)S(1)} collective-permute-done((bf16[64,1536]{1,0:T(8,128)(2,1)}, bf16[64,1536]{1,0:T(8,128)(2,1)S(1)}, u32[]{:S(2)}, u32[]{:S(2)}) %collective-permute-start) | collective-permute-done | bytes 196640 | tf_op jit(solution)/shard_map/while/body/eval_jaxpr/ppermute | solution.py:19
  414.2 22.5 %collective-permute-done = bf16[64,1536]{1,0:T(8,128)(2,1)S(1)} collective-permute-done((bf16[64,1536]{1,0:T(8,128)(2,1)}, bf16[64,1536]{1,0:T(8,128)(2,1)S(1)}, u32[]{:S(2)}, u32[]{:S(2)}) %collective-permute-start) | collective-permute-done | bytes 196640 | tf_op jit(solution)/shard_map/while/body/eval_jaxpr/ppermute | solution.py:19
  438.1 22.5 %collective-permute-done = bf16[64,1536]{1,0:T(8,128)(2,1)S(1)} collective-permute-done((bf16[64,1536]{1,0:T(8,128)(2,1)}, bf16[64,1536]{1,0:T(8,128)(2,1)S(1)}, u32[]{:S(2)}, u32[]{:S(2)}) %collective-permute-start) | collective-permute-done | bytes 196640 | tf_op jit(solution)/shard_map/while/body/eval_jaxpr/ppermute | solution.py:19
  462.0 22.4 %collective-permute-done = bf16[64,1536]{1,0:T(8,128)(2,1)S(1)} collective-permute-done((bf16[64,1536]{1,0:T(8,128)(2,1)}, bf16[64,1536]{1,0:T(8,128)(2,1)S(1)}, u32[]{:S(2)}, u32[]{:S(2)}) %collective-permute-start) | collective-permute-done | bytes 196640 | tf_op jit(solution)/shard_map/while/body/eval_jaxpr/ppermute | solution.py:19
  486.4 358.3 %while.43 = (s32[]{:T(128)}, bf16[64,1536]{1,0:T(8,128)(2,1)S(1)}, f32[64,1536]{1,0:T(8,128)S(1)}, f32[64,1536]{1,0:T(8,128)S(1)}, s32[]{:T(128)}, /*index=5*/pr...) while((s32[]{:T(128)}, bf16[64,1536]{1,0:T(8,128)(2,1)S(1)}, ...), condition=%wide.region_10.11_spmd, body=%wide.region_5.10_spmd.sunk | while | flops 356265024 | bytes 13259635 | solution.py:292
  487.2 14.7 %collective-permute-start.1 = (bf16[64,1536]{1,0:T(8,128)(2,1)}, bf16[64,1536]{1,0:T(8,128)(2,1)S(1)}, u32[]{:S(2)}, u32[]{:S(2)}) collective-permute-start(bf16[64,1536]{1,0:T(8,128)(2,1)} %get-tuple-element.1134), channel_id=1, source_target_pairs={{32,0},{64,32},{96,64},{128,96},{160,128},{192,160},{224,192},{0,2... | collective-permute-start | bytes 589832 | tf_op jit(solution)/shard_map/while/body/eval_jaxpr/ppermute | solution.py:19
  506.1 17.2 %collective-permute-start.1 = (bf16[64,1536]{1,0:T(8,128)(2,1)}, bf16[64,1536]{1,0:T(8,128)(2,1)S(1)}, u32[]{:S(2)}, u32[]{:S(2)}) collective-permute-start(bf16[64,1536]{1,0:T(8,128)(2,1)} %get-tuple-element.1134), channel_id=1, source_target_pairs={{32,0},{64,32},{96,64},{128,96},{160,128},{192,160},{224,192},{0,2... | collective-permute-start | bytes 589832 | tf_op jit(solution)/shard_map/while/body/eval_jaxpr/ppermute | solution.py:19
  527.9 17.2 %collective-permute-start.1 = (bf16[64,1536]{1,0:T(8,128)(2,1)}, bf16[64,1536]{1,0:T(8,128)(2,1)S(1)}, u32[]{:S(2)}, u32[]{:S(2)}) collective-permute-start(bf16[64,1536]{1,0:T(8,128)(2,1)} %get-tuple-element.1134), channel_id=1, source_target_pairs={{32,0},{64,32},{96,64},{128,96},{160,128},{192,160},{224,192},{0,2... | collective-permute-start | bytes 589832 | tf_op jit(solution)/shard_map/while/body/eval_jaxpr/ppermute | solution.py:19
  550.9 17.2 %collective-permute-start.1 = (bf16[64,1536]{1,0:T(8,128)(2,1)}, bf16[64,1536]{1,0:T(8,128)(2,1)S(1)}, u32[]{:S(2)}, u32[]{:S(2)}) collective-permute-start(bf16[64,1536]{1,0:T(8,128)(2,1)} %get-tuple-element.1134), channel_id=1, source_target_pairs={{32,0},{64,32},{96,64},{128,96},{160,128},{192,160},{224,192},{0,2... | collective-permute-start | bytes 589832 | tf_op jit(solution)/shard_map/while/body/eval_jaxpr/ppermute | solution.py:19
  601.7 15.1 %collective-permute-done.1 = bf16[64,1536]{1,0:T(8,128)(2,1)S(1)} collective-permute-done((bf16[64,1536]{1,0:T(8,128)(2,1)}, bf16[64,1536]{1,0:T(8,128)(2,1)S(1)}, u32[]{:S(2)}, u32[]{:S(2)}) %collective-permute-start.1) | collective-permute-done | bytes 196640 | tf_op jit(solution)/shard_map/while/body/eval_jaxpr/ppermute | solution.py:19
  701.6 13.2 %collective-permute-start.1 = (bf16[64,1536]{1,0:T(8,128)(2,1)}, bf16[64,1536]{1,0:T(8,128)(2,1)S(1)}, u32[]{:S(2)}, u32[]{:S(2)}) collective-permute-start(bf16[64,1536]{1,0:T(8,128)(2,1)} %get-tuple-element.1134), channel_id=1, source_target_pairs={{32,0},{64,32},{96,64},{128,96},{160,128},{192,160},{224,192},{0,2... | collective-permute-start | bytes 589832 | tf_op jit(solution)/shard_map/while/body/eval_jaxpr/ppermute | solution.py:19
  846.5 110.0 %reduce-scatter.2.cloned.1.call-done = f32[128,48]{0,1:T(8,128)} async-done(((f32[128,1536]{0,1:T(8,128)}), f32[128,48]{0,1:T(8,128)}) %reduce-scatter.2.cloned.1.call-update) | async-done | bytes 24592 | tf_op jit(solution)/shard_map/reduce_scatter | solution.py:25
  (427 shorter events, 671.3 us)
Async XLA Ops:
  7.2 72.3 %all-gather.3.cloned.1.call-start = ((), (), s32[]{:S(2)}) async-start(), calls=%async_computation.2 | async-start | bytes 4866048 | tf_op jit(solution)/shard_map/all_gather | solution.py:130
  7.9 948.6 %reduce-scatter.2.cloned.1.call-start = ((), (), s32[]{:S(2)}) async-start(), calls=%async_computation.1 | async-start | bytes 811008 | tf_op jit(solution)/shard_map/reduce_scatter | solution.py:25
  99.1 10.9 %collective-permute-start = (bf16[64,1536]{1,0:T(8,128)(2,1)}, bf16[64,1536]{1,0:T(8,128)(2,1)S(1)}, u32[]{:S(2)}, u32[]{:S(2)}) collective-permute-start(bf16[64,1536]{1,0:T(8,128)(2,1)} %get-tuple-element.1111), channel_id=1, source_target_pairs={{224,0},{0,32},{32,64},{64,96},{96,128},{128,160},{160,192},{192,2... | collective-permute-start | bytes 589832 | tf_op jit(solution)/shard_map/while/body/eval_jaxpr/ppermute | solution.py:19
  124.4 10.1 %collective-permute-start = (bf16[64,1536]{1,0:T(8,128)(2,1)}, bf16[64,1536]{1,0:T(8,128)(2,1)S(1)}, u32[]{:S(2)}, u32[]{:S(2)}) collective-permute-start(bf16[64,1536]{1,0:T(8,128)(2,1)} %get-tuple-element.1111), channel_id=1, source_target_pairs={{224,0},{0,32},{32,64},{64,96},{96,128},{128,160},{160,192},{192,2... | collective-permute-start | bytes 589832 | tf_op jit(solution)/shard_map/while/body/eval_jaxpr/ppermute | solution.py:19
  183.6 14.4 %collective-permute-start = (bf16[64,1536]{1,0:T(8,128)(2,1)}, bf16[64,1536]{1,0:T(8,128)(2,1)S(1)}, u32[]{:S(2)}, u32[]{:S(2)}) collective-permute-start(bf16[64,1536]{1,0:T(8,128)(2,1)} %get-tuple-element.1111), channel_id=1, source_target_pairs={{224,0},{0,32},{32,64},{64,96},{96,128},{128,160},{160,192},{192,2... | collective-permute-start | bytes 589832 | tf_op jit(solution)/shard_map/while/body/eval_jaxpr/ppermute | solution.py:19
  210.2 15.3 %collective-permute-start = (bf16[64,1536]{1,0:T(8,128)(2,1)}, bf16[64,1536]{1,0:T(8,128)(2,1)S(1)}, u32[]{:S(2)}, u32[]{:S(2)}) collective-permute-start(bf16[64,1536]{1,0:T(8,128)(2,1)} %get-tuple-element.1111), channel_id=1, source_target_pairs={{224,0},{0,32},{32,64},{64,96},{96,128},{128,160},{160,192},{192,2... | collective-permute-start | bytes 589832 | tf_op jit(solution)/shard_map/while/body/eval_jaxpr/ppermute | solution.py:19
  226.9 23.8 %collective-permute-start = (bf16[64,1536]{1,0:T(8,128)(2,1)}, bf16[64,1536]{1,0:T(8,128)(2,1)S(1)}, u32[]{:S(2)}, u32[]{:S(2)}) collective-permute-start(bf16[64,1536]{1,0:T(8,128)(2,1)} %get-tuple-element.1111), channel_id=1, source_target_pairs={{224,0},{0,32},{32,64},{64,96},{96,128},{128,160},{160,192},{192,2... | collective-permute-start | bytes 589832 | tf_op jit(solution)/shard_map/while/body/eval_jaxpr/ppermute | solution.py:19
  336.6 11.1 %collective-permute-start = (bf16[64,1536]{1,0:T(8,128)(2,1)}, bf16[64,1536]{1,0:T(8,128)(2,1)S(1)}, u32[]{:S(2)}, u32[]{:S(2)}) collective-permute-start(bf16[64,1536]{1,0:T(8,128)(2,1)} %get-tuple-element.1111), channel_id=1, source_target_pairs={{224,0},{0,32},{32,64},{64,96},{96,128},{128,160},{160,192},{192,2... | collective-permute-start | bytes 589832 | tf_op jit(solution)/shard_map/while/body/eval_jaxpr/ppermute | solution.py:19
  349.0 12.8 %collective-permute-start = (bf16[64,1536]{1,0:T(8,128)(2,1)}, bf16[64,1536]{1,0:T(8,128)(2,1)S(1)}, u32[]{:S(2)}, u32[]{:S(2)}) collective-permute-start(bf16[64,1536]{1,0:T(8,128)(2,1)} %get-tuple-element.1111), channel_id=1, source_target_pairs={{224,0},{0,32},{32,64},{64,96},{96,128},{128,160},{160,192},{192,2... | collective-permute-start | bytes 589832 | tf_op jit(solution)/shard_map/while/body/eval_jaxpr/ppermute | solution.py:19
  374.0 15.3 %collective-permute-start = (bf16[64,1536]{1,0:T(8,128)(2,1)}, bf16[64,1536]{1,0:T(8,128)(2,1)S(1)}, u32[]{:S(2)}, u32[]{:S(2)}) collective-permute-start(bf16[64,1536]{1,0:T(8,128)(2,1)} %get-tuple-element.1111), channel_id=1, source_target_pairs={{224,0},{0,32},{32,64},{64,96},{96,128},{128,160},{160,192},{192,2... | collective-permute-start | bytes 589832 | tf_op jit(solution)/shard_map/while/body/eval_jaxpr/ppermute | solution.py:19
  390.7 22.1 %collective-permute-start = (bf16[64,1536]{1,0:T(8,128)(2,1)}, bf16[64,1536]{1,0:T(8,128)(2,1)S(1)}, u32[]{:S(2)}, u32[]{:S(2)}) collective-permute-start(bf16[64,1536]{1,0:T(8,128)(2,1)} %get-tuple-element.1111), channel_id=1, source_target_pairs={{224,0},{0,32},{32,64},{64,96},{96,128},{128,160},{160,192},{192,2... | collective-permute-start | bytes 589832 | tf_op jit(solution)/shard_map/while/body/eval_jaxpr/ppermute | solution.py:19
  414.2 22.5 %collective-permute-start = (bf16[64,1536]{1,0:T(8,128)(2,1)}, bf16[64,1536]{1,0:T(8,128)(2,1)S(1)}, u32[]{:S(2)}, u32[]{:S(2)}) collective-permute-start(bf16[64,1536]{1,0:T(8,128)(2,1)} %get-tuple-element.1111), channel_id=1, source_target_pairs={{224,0},{0,32},{32,64},{64,96},{96,128},{128,160},{160,192},{192,2... | collective-permute-start | bytes 589832 | tf_op jit(solution)/shard_map/while/body/eval_jaxpr/ppermute | solution.py:19
  438.1 22.5 %collective-permute-start = (bf16[64,1536]{1,0:T(8,128)(2,1)}, bf16[64,1536]{1,0:T(8,128)(2,1)S(1)}, u32[]{:S(2)}, u32[]{:S(2)}) collective-permute-start(bf16[64,1536]{1,0:T(8,128)(2,1)} %get-tuple-element.1111), channel_id=1, source_target_pairs={{224,0},{0,32},{32,64},{64,96},{96,128},{128,160},{160,192},{192,2... | collective-permute-start | bytes 589832 | tf_op jit(solution)/shard_map/while/body/eval_jaxpr/ppermute | solution.py:19
  462.0 22.4 %collective-permute-start = (bf16[64,1536]{1,0:T(8,128)(2,1)}, bf16[64,1536]{1,0:T(8,128)(2,1)S(1)}, u32[]{:S(2)}, u32[]{:S(2)}) collective-permute-start(bf16[64,1536]{1,0:T(8,128)(2,1)} %get-tuple-element.1111), channel_id=1, source_target_pairs={{224,0},{0,32},{32,64},{64,96},{96,128},{128,160},{160,192},{192,2... | collective-permute-start | bytes 589832 | tf_op jit(solution)/shard_map/while/body/eval_jaxpr/ppermute | solution.py:19
  487.2 18.2 %collective-permute-start.1 = (bf16[64,1536]{1,0:T(8,128)(2,1)}, bf16[64,1536]{1,0:T(8,128)(2,1)S(1)}, u32[]{:S(2)}, u32[]{:S(2)}) collective-permute-start(bf16[64,1536]{1,0:T(8,128)(2,1)} %get-tuple-element.1134), channel_id=1, source_target_pairs={{32,0},{64,32},{96,64},{128,96},{160,128},{192,160},{224,192},{0,2... | collective-permute-start | bytes 589832 | tf_op jit(solution)/shard_map/while/body/eval_jaxpr/ppermute | solution.py:19
  506.1 21.1 %collective-permute-start.1 = (bf16[64,1536]{1,0:T(8,128)(2,1)}, bf16[64,1536]{1,0:T(8,128)(2,1)S(1)}, u32[]{:S(2)}, u32[]{:S(2)}) collective-permute-start(bf16[64,1536]{1,0:T(8,128)(2,1)} %get-tuple-element.1134), channel_id=1, source_target_pairs={{32,0},{64,32},{96,64},{128,96},{160,128},{192,160},{224,192},{0,2... | collective-permute-start | bytes 589832 | tf_op jit(solution)/shard_map/while/body/eval_jaxpr/ppermute | solution.py:19
  527.9 22.3 %collective-permute-start.1 = (bf16[64,1536]{1,0:T(8,128)(2,1)}, bf16[64,1536]{1,0:T(8,128)(2,1)S(1)}, u32[]{:S(2)}, u32[]{:S(2)}) collective-permute-start(bf16[64,1536]{1,0:T(8,128)(2,1)} %get-tuple-element.1134), channel_id=1, source_target_pairs={{32,0},{64,32},{96,64},{128,96},{160,128},{192,160},{224,192},{0,2... | collective-permute-start | bytes 589832 | tf_op jit(solution)/shard_map/while/body/eval_jaxpr/ppermute | solution.py:19
  550.9 22.3 %collective-permute-start.1 = (bf16[64,1536]{1,0:T(8,128)(2,1)}, bf16[64,1536]{1,0:T(8,128)(2,1)S(1)}, u32[]{:S(2)}, u32[]{:S(2)}) collective-permute-start(bf16[64,1536]{1,0:T(8,128)(2,1)} %get-tuple-element.1134), channel_id=1, source_target_pairs={{32,0},{64,32},{96,64},{128,96},{160,128},{192,160},{224,192},{0,2... | collective-permute-start | bytes 589832 | tf_op jit(solution)/shard_map/while/body/eval_jaxpr/ppermute | solution.py:19
  573.9 10.9 %collective-permute-start.1 = (bf16[64,1536]{1,0:T(8,128)(2,1)}, bf16[64,1536]{1,0:T(8,128)(2,1)S(1)}, u32[]{:S(2)}, u32[]{:S(2)}) collective-permute-start(bf16[64,1536]{1,0:T(8,128)(2,1)} %get-tuple-element.1134), channel_id=1, source_target_pairs={{32,0},{64,32},{96,64},{128,96},{160,128},{192,160},{224,192},{0,2... | collective-permute-start | bytes 589832 | tf_op jit(solution)/shard_map/while/body/eval_jaxpr/ppermute | solution.py:19
  595.7 21.1 %collective-permute-start.1 = (bf16[64,1536]{1,0:T(8,128)(2,1)}, bf16[64,1536]{1,0:T(8,128)(2,1)S(1)}, u32[]{:S(2)}, u32[]{:S(2)}) collective-permute-start(bf16[64,1536]{1,0:T(8,128)(2,1)} %get-tuple-element.1134), channel_id=1, source_target_pairs={{32,0},{64,32},{96,64},{128,96},{160,128},{192,160},{224,192},{0,2... | collective-permute-start | bytes 589832 | tf_op jit(solution)/shard_map/while/body/eval_jaxpr/ppermute | solution.py:19
  701.6 16.7 %collective-permute-start.1 = (bf16[64,1536]{1,0:T(8,128)(2,1)}, bf16[64,1536]{1,0:T(8,128)(2,1)S(1)}, u32[]{:S(2)}, u32[]{:S(2)}) collective-permute-start(bf16[64,1536]{1,0:T(8,128)(2,1)} %get-tuple-element.1134), channel_id=1, source_target_pairs={{32,0},{64,32},{96,64},{128,96},{160,128},{192,160},{224,192},{0,2... | collective-permute-start | bytes 589832 | tf_op jit(solution)/shard_map/while/body/eval_jaxpr/ppermute | solution.py:19
  729.1 14.8 %collective-permute-start.1 = (bf16[64,1536]{1,0:T(8,128)(2,1)}, bf16[64,1536]{1,0:T(8,128)(2,1)S(1)}, u32[]{:S(2)}, u32[]{:S(2)}) collective-permute-start(bf16[64,1536]{1,0:T(8,128)(2,1)} %get-tuple-element.1134), channel_id=1, source_target_pairs={{32,0},{64,32},{96,64},{128,96},{160,128},{192,160},{224,192},{0,2... | collective-permute-start | bytes 589832 | tf_op jit(solution)/shard_map/while/body/eval_jaxpr/ppermute | solution.py:19
  744.6 14.5 %collective-permute-start.1 = (bf16[64,1536]{1,0:T(8,128)(2,1)}, bf16[64,1536]{1,0:T(8,128)(2,1)S(1)}, u32[]{:S(2)}, u32[]{:S(2)}) collective-permute-start(bf16[64,1536]{1,0:T(8,128)(2,1)} %get-tuple-element.1134), channel_id=1, source_target_pairs={{32,0},{64,32},{96,64},{128,96},{160,128},{192,160},{224,192},{0,2... | collective-permute-start | bytes 589832 | tf_op jit(solution)/shard_map/while/body/eval_jaxpr/ppermute | solution.py:19
  814.3 11.2 %collective-permute-start.1 = (bf16[64,1536]{1,0:T(8,128)(2,1)}, bf16[64,1536]{1,0:T(8,128)(2,1)S(1)}, u32[]{:S(2)}, u32[]{:S(2)}) collective-permute-start(bf16[64,1536]{1,0:T(8,128)(2,1)} %get-tuple-element.1134), channel_id=1, source_target_pairs={{32,0},{64,32},{96,64},{128,96},{160,128},{192,160},{224,192},{0,2... | collective-permute-start | bytes 589832 | tf_op jit(solution)/shard_map/while/body/eval_jaxpr/ppermute | solution.py:19
  (61 other events, 226.8 us)
Sparse Core Ops, SparseCore 0:
  9.9 69.5 all-gather.2
  846.6 109.8 reduce-scatter.1
where the time goes:
time: 972 us; the launch traced here: 965 us
  waiting for transfers between devices  522 us (54%)
  starting transfers between devices  182 us (19%)
  matrix products  133 us (14%)
  other arithmetic  61.9 us (6%)
  local copies, waits for them, and re-layouts  50.3 us (5%)
  between operations  14.1 us (1%)
    ppermute x38, waiting for transfers between devices, from_behind(): return lax.ppermute(block, axis, route)  344 us
    ppermute x38, starting transfers between devices, from_behind(): return lax.ppermute(block, axis, route)  182 us
    reduce_scatter x1, waiting for transfers between devices, in_one_piece(): out = lax.psum_scatter(both, axis, scatter_dimension=dim, tiled=True)  110 us
    all_gather x1, waiting for transfers between devices, local(): layer_weight = lax.all_gather(frozen_weight[0], 'dp', axis=0, tiled=True)  67.5 us
    dot_general x8, matrix products, forward_layer_pass(): jnp.dot(normalized_hidden, layer_weight, preferred_element_type=jnp.float32)  32.5 us
    dot_general x8, matrix products, backward_layer_pass(): lax.dot_general(preactivation_gradient, layer_weight, (((1,), (1,)), ((),...  31.2 us
  transfers between devices with their start and end apart: 40, of which 40 were waited for; matrix products, arithmetic and copies ran while one was open for 0% of the time, Pallas kernels for 0%

commit v1 on v0

v1 whole, which is shorter than its diff:
```python
import math

import jax
import jax.numpy as jnp
from jax import lax
from jax.experimental import pallas as pl
from jax.experimental.pallas import tpu as pltpu
from jax.sharding import PartitionSpec as P

BLEND = 0.5
ADAPTER_SCALE = 0.5
EPSILON = 1e-06
EXTRA = 8
F32 = jnp.float32
BF16 = jnp.bfloat16


def dot_nn(a, b):
    return lax.dot_general(a, b, (((1,), (0,)), ((), ())), preferred_element_type=F32)


def dot_nt(a, b):
    return lax.dot_general(a, b, (((1,), (1,)), ((), ())), preferred_element_type=F32)


def dot_tn(a, b):
    return lax.dot_general(a, b, (((0,), (0,)), ((), ())), preferred_element_type=F32)


def rows_kernel(
    layers,
    dp_size,
    part_rows,
    rank,
    scale_factor,
    latent_ref,
    target_ref,
    camera_ref,
    modulation_ref,
    pack_ref,
    grad_ref,
    weights,
    adapters,
    gains,
    hidden_store,
    normed_store,
    low_store,
    pre_store,
    grad_store,
    lowgrad_store,
    adjoint,
    sem,
):
    rows, width = latent_ref.shape
    adapter_blocks = 2 * rank // EXTRA

    def copies(layer):
        first = layer * dp_size
        return (
            pltpu.make_async_copy(
                pack_ref.at[pl.ds(first, dp_size), pl.ds(0, part_rows)],
                weights.at[layer],
                sem.at[0, layer],
            ),
            pltpu.make_async_copy(
                pack_ref.at[pl.ds(first, adapter_blocks), pl.ds(part_rows, EXTRA)],
                adapters.at[layer],
                sem.at[1, layer],
            ),
            pltpu.make_async_copy(
                pack_ref.at[pl.ds(first + adapter_blocks, 1), pl.ds(part_rows, EXTRA)],
                gains.at[layer],
                sem.at[2, layer],
            ),
        )

    for layer in range(layers):
        for one in copies(layer):
            one.start()

    def weight(layer):
        return weights[layer].reshape(width, width)

    def adapter(layer):
        both = adapters[layer].reshape(2 * rank, width)
        return both[:rank], both[rank:]

    def scale_row(layer, step):
        parts = gains[layer, 0].astype(F32)
        gain = (parts[0:1] + parts[1:2]) + parts[2:3]
        return gain * modulation_ref[pl.ds(step, 1), :]

    def forward(step, layer, hidden):
        slot = step * layers + layer
        hidden_store[slot] = hidden
        down, up = adapter(layer)
        hf = hidden.astype(F32)
        inverse = lax.rsqrt(jnp.mean(hf * hf, axis=-1, keepdims=True) + EPSILON)
        normed = (hf * inverse * scale_row(layer, step)).astype(BF16)
        low = dot_nt(normed, down).astype(BF16)
        pre = dot_nn(normed, weight(layer)) + ADAPTER_SCALE * dot_nn(low, up)
        normed_store[slot] = normed
        low_store[slot] = low
        pre_store[slot] = pre
        return (hf + pre * jax.nn.sigmoid(pre)).astype(BF16)

    def first_pass(layer, hidden):
        for one in copies(layer):
            one.wait()
        return forward(0, layer, hidden)

    latent = latent_ref[...].astype(F32)
    camera = camera_ref[...]
    hidden = lax.fori_loop(0, layers, first_pass, (latent + camera).astype(BF16))
    middle = (BLEND * (latent + hidden.astype(F32))).astype(BF16).astype(F32)
    hidden = lax.fori_loop(
        0, layers, lambda layer, h: forward(1, layer, h), (middle + camera).astype(BF16)
    )
    squashed = jnp.tanh(BLEND * (middle + hidden.astype(F32)))
    adjoint[...] = target_ref[...].astype(F32) * (1.0 - squashed * squashed) * scale_factor

    def backward(step, layer, cotangent):
        slot = step * layers + layer
        down, up = adapter(layer)
        pre = pre_store[slot]
        s = jax.nn.sigmoid(pre)
        pre_grad = (cotangent * s * (1.0 + pre * (1.0 - s))).astype(BF16)
        low_grad = (ADAPTER_SCALE * dot_nt(pre_grad, up)).astype(BF16)
        norm_grad = dot_nt(pre_grad, weight(layer)) + dot_nn(low_grad, down)
        hf = hidden_store[slot].astype(F32)
        inverse = lax.rsqrt(jnp.mean(hf * hf, axis=-1, keepdims=True) + EPSILON)
        y = hf * inverse
        g = norm_grad * scale_row(layer, step)
        result = cotangent + inverse * (g - y * jnp.mean(g * y, axis=-1, keepdims=True))
        return pre_grad, low_grad, result.astype(BF16).astype(F32)

    def last_step(i, cotangent):
        layer = layers - 1 - i
        pre_grad, low_grad, result = backward(1, layer, cotangent)
        grad_store[layer] = pre_grad
        lowgrad_store[layer] = low_grad
        return result

    def first_step(i, cotangent):
        layer = layers - 1 - i
        pre_grad, low_grad, result = backward(0, layer, cotangent)
        both = layers + layer
        pre_both = jnp.concatenate([pre_grad, grad_store[layer]], axis=0)
        lg_both = jnp.concatenate([low_grad, lowgrad_store[layer]], axis=0)
        low_both = jnp.concatenate([low_store[layer], low_store[both]], axis=0)
        normed_both = jnp.concatenate([normed_store[layer], normed_store[both]], axis=0)
        grad_ref[layer, :, 0:rank] = dot_tn(normed_both, lg_both).astype(grad_ref.dtype)
        grad_ref[layer, :, rank:] = (ADAPTER_SCALE * dot_tn(pre_both, low_both)).astype(grad_ref.dtype)
        return result

    entering = lax.fori_loop(0, layers, last_step, BLEND * adjoint[...])
    lax.fori_loop(0, layers, first_step, BLEND * (BLEND * adjoint[...] + entering))


def row_gradients(latent, target, camera, modulation, pack, layers, dp_size, rank, scale_factor, dtype):
    rows, width = latent.shape
    part_rows = width // dp_size
    vmem = pl.BlockSpec(memory_space=pltpu.VMEM)

    def body(*refs):
        rows_kernel(layers, dp_size, part_rows, rank, scale_factor, *refs)

    return pl.pallas_call(
        body,
        out_shape=jax.ShapeDtypeStruct((layers, width, 2 * rank), dtype),
        in_specs=[vmem, vmem, vmem, vmem, pl.BlockSpec(memory_space=pl.ANY)],
        out_specs=vmem,
        scratch_shapes=[
            pltpu.VMEM((layers, dp_size, part_rows, width), BF16),
            pltpu.VMEM((layers, 2 * rank // EXTRA, EXTRA, width), BF16),
            pltpu.VMEM((layers, 1, EXTRA, width), BF16),
            pltpu.VMEM((2 * layers, rows, width), BF16),
            pltpu.VMEM((2 * layers, rows, width), BF16),
            pltpu.VMEM((2 * layers, rows, rank), BF16),
            pltpu.VMEM((2 * layers, rows, width), F32),
            pltpu.VMEM((layers, rows, width), BF16),
            pltpu.VMEM((layers, rows, rank), BF16),
            pltpu.VMEM((rows, width), F32),
            pltpu.SemaphoreType.DMA((3, layers)),
        ],
        compiler_params=pltpu.CompilerParams(vmem_limit_bytes=61 * 1024 * 1024),
        name="row_gradients",
    )(latent, target, camera, modulation, pack)


def exchange_and_add(parts, axis):
    count = lax.axis_size(axis)
    parts = parts.reshape(count, -1, parts.shape[-1])
    return lax.all_to_all(parts, axis, 0, 0, tiled=True).astype(F32).sum(0)


def local(
    latent,
    target,
    camera_of_token,
    timestep_indices,
    camera_embedding_table,
    timestep_embedding_table,
    layer_norm_gain,
    frozen_weight,
    adapter_down_weight,
    adapter_up_weight,
):
    sections = lax.axis_size("section")
    dp_size = lax.axis_size("dp")
    section = lax.axis_index("section")
    lane = lax.axis_index("dp")
    rank, width = adapter_down_weight.shape[1:]
    rows = latent.shape[0] // sections
    scale_factor = 1.0 / math.sqrt(latent.shape[0] * dp_size)
    adapter_rows = jnp.concatenate([adapter_down_weight[0], adapter_up_weight[0]], axis=0)
    adapter_blocks = 2 * rank // EXTRA
    mine = lax.dynamic_slice(
        adapter_rows, (EXTRA * jnp.minimum(lane, adapter_blocks - 1), 0), (EXTRA, width)
    )
    gain = layer_norm_gain
    high = lax.reduce_precision(gain, 8, 7)
    middle = lax.reduce_precision(gain - high, 8, 7)
    lowest = gain - high - middle
    gain_rows = jnp.concatenate(
        [high, middle, lowest, jnp.zeros((EXTRA - 3, width), F32)], axis=0
    ).astype(BF16)
    extra = jnp.where(lane < adapter_blocks, mine, gain_rows)
    own = jnp.concatenate([frozen_weight[0], extra], axis=0)
    pack = lax.all_gather(own, ("section", "dp"), axis=0, tiled=False)

    def my_rows(a):
        return lax.dynamic_slice_in_dim(a, section * rows, rows, 0)

    camera_rows = jnp.dot(
        jax.nn.one_hot(my_rows(camera_of_token), camera_embedding_table.shape[0], dtype=BF16),
        camera_embedding_table,
        preferred_element_type=F32,
    )
    modulation = 1.0 + jnp.dot(
        jax.nn.one_hot(timestep_indices, timestep_embedding_table.shape[0], dtype=BF16),
        timestep_embedding_table,
        preferred_element_type=F32,
    )
    grads = row_gradients(
        my_rows(latent),
        my_rows(target),
        camera_rows,
        modulation,
        pack,
        sections,
        dp_size,
        rank,
        scale_factor,
        BF16,
    )
    over_sections = exchange_and_add(grads, "section")
    summed = exchange_and_add(over_sections.astype(BF16), "dp")
    turned = summed.T
    return turned[None, :rank], turned[None, rank:]


def solution(mesh):
    in_specs = (
        P("dp", None),
        P("dp", None),
        P("dp"),
        P(),
        P(),
        P(),
        P("section", None),
        P("section", "dp", None),
        P("section", None, None),
        P("section", None, None),
    )
    out_specs = (P("section", None, "dp"), P("section", None, "dp"))
    return jax.shard_map(local, mesh=mesh, in_specs=in_specs, out_specs=out_specs, check_vma=False)
```

time: 972 us -> 314 us (0.32)
  waiting for transfers between devices: 522 us -> 167 us
  starting transfers between devices: 182 us -> 0.04 us
  matrix products: 133 us -> 3.08 us
  blocking collectives: 0 us -> 66.7 us
  other arithmetic: 61.9 us -> 4.48 us
  Pallas kernels: 0 us -> 55.1 us
  local copies, waits for them, and re-layouts: 50.3 us -> 3.18 us
    ppermute x38 -> x0, waiting for transfers between devices: 344 us -> none  [from_behind(): return lax.ppermute(block, axis, route)]
    ppermute x38 -> x0, starting transfers between devices: 182 us -> none  [from_behind(): return lax.ppermute(block, axis, route)]
    dot_general x65 -> x1, matrix products: 132 us -> 1.63 us  [local(): jnp.dot(jax.nn.one_hot(my_rows(camera_of_token), camera_embedding_table.s...]
    reduce_scatter x1 -> x0, waiting for transfers between devices: 110 us -> none  [in_one_piece(): out = lax.psum_scatter(both, axis, scatter_dimension=dim, tiled=True)]
    all_gather x1, waiting for transfers between devices: 67.5 us -> 166 us  [local(): pack = lax.all_gather(own, ('section', 'dp'), axis=0, tiled=False)]
    all_to_all x0 -> x2, blocking collectives: none -> 66.7 us  [exchange_and_add(): return lax.all_to_all(parts, axis, 0, 0, tiled=True).astype(F32).sum(0)]
    pallas_call x0 -> x1, Pallas kernels: none -> 55.1 us  [row_gradients(): pl.pallas_call(body, out_shape=jax.ShapeDtypeStruct((layers, width, 2 * r...]
    dynamic_update_slice x24 -> x0, other arithmetic: 18.5 us -> none  [the longest x16 18.1 us: place_block(): return lax.dynamic_update_slice(store, value[None, None], starts)]
  transfers between devices with their start and end apart: 40 -> 1, of which waited for: 40 -> 1; matrix products, arithmetic and copies ran while one was open for 0% -> 2% of each run, Pallas kernels for 0% -> 0%
where the time goes in v1:
time: 314 us; the launch traced here: 313 us
  waiting for transfers between devices  167 us (53%)
  blocking collectives  66.7 us (21%)
  Pallas kernels  55.1 us (18%)
  between operations  14.1 us (4%)
  other arithmetic  4.48 us (1%)
  local copies, waits for them, and re-layouts  3.18 us (1%)
    all_gather x1, waiting for transfers between devices, local(): pack = lax.all_gather(own, ('section', 'dp'), axis=0, tiled=False)  166 us
    all_to_all x2, blocking collectives, exchange_and_add(): return lax.all_to_all(parts, axis, 0, 0, tiled=True).astype(F32).sum(0)  66.7 us
    pallas_call x1, Pallas kernels, row_gradients(): pl.pallas_call(body, out_shape=jax.ShapeDtypeStruct((layers, width, 2 * r...  55.1 us
  transfers between devices with their start and end apart: 1, of which 1 were waited for; matrix products, arithmetic and copies ran while one was open for 2% of the time, Pallas kernels for 0%

profile of v1, /device:TPU:32, one launch (start us, length us, event | category | flops | bytes accessed | tf_op | source)
XLA Modules:
  0.0 313.1 jit_solution(3750734242461932532)
XLA Ops:
  7.2 0.0 copy-start
  7.2 0.0 all-gather.3.cloned.1.call-start
  7.2 0.7 reduce-precision_convert_fusion.1
  8.0 0.1 pad.5.clone
  8.1 0.8 maximum_select_fusion
  8.9 1.6 pad_maximum_fusion
  10.5 0.0 all-gather.3.cloned.1.call-update
  10.5 0.8 dynamic_slice.14
  11.3 0.0 copy-done
  11.3 1.5 convolution_add_fusion.refs_3_
  12.7 1.6 fusion.1.refs_2_
  14.3 1.6 constant_dynamic-slice_fusion
  16.0 166.5 %all-gather.3.cloned.1.call-done = bf16[14336,1536]{1,0:T(8,128)(2,1)} async-done(((bf16[56,1536]{1,0:T(8,128)(2,1)}), bf16[14336,1536]{1,0:T(8,128)(2,1)}) %all-gather.3.cloned.1.call-update) | async-done | bytes 44040208 | tf_op jit(solution)/shard_map/all_gather | solution.py:230
  182.5 55.1 %row_gradients.1 = bf16[8,1536,128]{2,1,0:T(8,128)(2,1)} custom-call(bf16[32,1536]{1,0:T(8,128)(2,1)} %get-tuple-element.8.refs_0_, bf16[32,1536]{1,0:T(8,128)(2,1)} %get-tuple-element.7.refs_1_, f32[32,1536]{1,0:T(8,128)} %fusion.1.refs_2_, f32[2,1536]{1,0:T(2,128)} %convolution_add_fusion.refs_3_, bf16[256,56,1536]{2,1,0:T(8,128)(2,1)} %bitcast.12), custom_call_target="tpu_custom_call" | custom-call | tf_op jit(solution)/shard_map/row_gradients/pallas_call | solution.py:168
  237.6 44.9 %all_to_all.10 = bf16[8,1536,128]{2,1,0:T(8,128)(2,1)S(1)} all-to-all(bf16[8,1536,128]{2,1,0:T(8,128)(2,1)} %row_gradients.1), channel_id=1, replica_groups=mesh['section'=8,'dp'=32] {'section'}, dimensions={0} | all-to-all | bytes 6291456 | tf_op jit(solution)/shard_map/all_to_all | solution.py:194
  282.5 1.3 reduce_sum.21
  283.7 21.7 %all_to_all.11 = bf16[32,48,128]{2,1,0:T(8,128)(2,1)S(1)} all-to-all(bf16[32,48,128]{2,1,0:T(8,128)(2,1)} %bitcast.13), channel_id=1, replica_groups=mesh['section'=8,'dp'=32] {'dp'}, dimensions={0} | all-to-all | bytes 786432 | tf_op jit(solution)/shard_map/all_to_all | solution.py:194
  305.5 0.1 convert_reduce_fusion
  305.6 0.7 slice_bitcast_fusion
  (1 shorter events, 0.0 us)
Async XLA Ops:
  7.2 4.1 %copy-start = (bf16[50,1536]{1,0:T(8,128)(2,1)S(1)}, bf16[50,1536]{1,0:T(8,128)(2,1)}, u32[]{:S(2)}) copy-start(bf16[50,1536]{1,0:T(8,128)(2,1)} %param.15) | copy-start | bytes 460804
  7.2 175.3 %all-gather.3.cloned.1.call-start = ((), (), s32[]{:S(2)}) async-start(), calls=%async_computation.2 | async-start | bytes 44212224 | tf_op jit(solution)/shard_map/all_gather | solution.py:230
Sparse Core Ops, SparseCore 0:
  11.9 170.5 all-gather.2

commit v2 on v1

v2 whole, which is shorter than its diff:
```python
import math

import jax
import jax.numpy as jnp
from jax import lax
from jax.experimental import pallas as pl
from jax.experimental.pallas import tpu as pltpu
from jax.sharding import PartitionSpec as P

BLEND = 0.5
ADAPTER_SCALE = 0.5
EPSILON = 1e-06
EXTRA = 8
EVERYWHERE = ("section", "dp")
SIZES = {"x": 4, "y": 4, "z": 8}
PART = 16
F32 = jnp.float32
BF16 = jnp.bfloat16


def dot_nn(a, b):
    return lax.dot_general(a, b, (((1,), (0,)), ((), ())), preferred_element_type=F32)


def dot_nt(a, b):
    return lax.dot_general(a, b, (((1,), (1,)), ((), ())), preferred_element_type=F32)


def dot_tn(a, b):
    return lax.dot_general(a, b, (((0,), (0,)), ((), ())), preferred_element_type=F32)


def ring_offsets(count):
    offsets = [0]
    for distance in range(1, count // 2 + 1):
        offsets.append(distance)
        if 2 * distance < count:
            offsets.append(-distance)
    return offsets


def rows_kernel(
    layers,
    rank,
    scale_factor,
    place_ref,
    latent_ref,
    target_ref,
    camera_ref,
    modulation_ref,
    *refs,
):
    piece_total = 2 * (SIZES["x"] + SIZES["y"])
    sides = refs[:2]
    last = refs[2]
    refs = refs[3:]
    pieces = refs[:piece_total]
    keep_ref, send_ref = refs[piece_total : piece_total + 2]
    run_rows(
        layers,
        rank,
        scale_factor,
        place_ref,
        latent_ref,
        target_ref,
        camera_ref,
        modulation_ref,
        sides,
        last,
        pieces,
        keep_ref,
        send_ref,
        *refs[piece_total + 2 :],
    )


def run_rows(
    layers,
    rank,
    scale_factor,
    place_ref,
    latent_ref,
    target_ref,
    camera_ref,
    modulation_ref,
    sides,
    last,
    pieces,
    keep_ref,
    send_ref,
    weights,
    side,
    hidden_store,
    normed_store,
    low_store,
    pre_store,
    grad_store,
    lowgrad_store,
    adjoint,
    sem,
    side_sem,
):
    rows, width = latent_ref.shape
    core = place_ref[3]

    copies = []
    number = 0
    for axis, name in enumerate(("x", "y")):
        count = SIZES[name]
        for half in range(2):
            owner = core if half == 0 else 1 - core
            sense = 1 - 2 * owner
            for offset in ring_offsets(count):
                at = lax.rem(place_ref[axis] - sense * offset + 2 * count, count)
                if name == "x":
                    home = weights.at[at, :, :, :, owner, pl.ds(0, PART)]
                else:
                    home = weights.at[:, at // 2, lax.rem(at, 2), :, owner, pl.ds(PART, PART)]
                copies.append(pltpu.make_async_copy(pieces[number], home, sem.at[number]))
                number += 1
    for z in range(SIZES["z"]):
        for owner in range(2):
            home = weights.at[:, :, :, z, owner, pl.ds(2 * PART, PART)]
            copies.append(pltpu.make_async_copy(last.at[2 * z + owner], home, sem.at[number]))
            number += 1
    for half in range(2):
        owner = core if half == 0 else 1 - core
        copies.append(pltpu.make_async_copy(sides[half], side.at[owner], side_sem.at[half]))
    for one in copies:
        one.start()
    for one in copies:
        one.wait()

    def weight(layer):
        return weights[layer // 2, lax.rem(layer, 2)].reshape(width, width)

    def adapter(layer):
        x, h = layer // 2, lax.rem(layer, 2)
        return side[0, x, h, 0:rank], side[1, x, h, 0:rank]

    def scale_row(layer, step):
        parts = side[0, layer // 2, lax.rem(layer, 2), rank:].astype(F32)
        gain = (parts[0:1] + parts[1:2]) + parts[2:3]
        return gain * modulation_ref[pl.ds(step, 1), :]

    def forward(step, layer, hidden):
        slot = step * layers + layer
        hidden_store[slot] = hidden
        down, up = adapter(layer)
        hf = hidden.astype(F32)
        inverse = lax.rsqrt(jnp.mean(hf * hf, axis=-1, keepdims=True) + EPSILON)
        normed = (hf * inverse * scale_row(layer, step)).astype(BF16)
        low = dot_nt(normed, down).astype(BF16)
        pre = dot_nn(normed, weight(layer)) + ADAPTER_SCALE * dot_nn(low, up)
        normed_store[slot] = normed
        low_store[slot] = low
        pre_store[slot] = pre
        return (hf + pre * jax.nn.sigmoid(pre)).astype(BF16)

    latent = latent_ref[...].astype(F32)
    camera = camera_ref[...]
    hidden = lax.fori_loop(
        0, layers, lambda layer, h: forward(0, layer, h), (latent + camera).astype(BF16)
    )
    middle = (BLEND * (latent + hidden.astype(F32))).astype(BF16).astype(F32)
    hidden = lax.fori_loop(
        0, layers, lambda layer, h: forward(1, layer, h), (middle + camera).astype(BF16)
    )
    squashed = jnp.tanh(BLEND * (middle + hidden.astype(F32)))
    adjoint[...] = target_ref[...].astype(F32) * (1.0 - squashed * squashed) * scale_factor

    def backward(step, layer, cotangent):
        slot = step * layers + layer
        down, up = adapter(layer)
        pre = pre_store[slot]
        s = jax.nn.sigmoid(pre)
        pre_grad = (cotangent * s * (1.0 + pre * (1.0 - s))).astype(BF16)
        low_grad = (ADAPTER_SCALE * dot_nt(pre_grad, up)).astype(BF16)
        norm_grad = dot_nt(pre_grad, weight(layer)) + dot_nn(low_grad, down)
        hf = hidden_store[slot].astype(F32)
        inverse = lax.rsqrt(jnp.mean(hf * hf, axis=-1, keepdims=True) + EPSILON)
        y = hf * inverse
        g = norm_grad * scale_row(layer, step)
        result = cotangent + inverse * (g - y * jnp.mean(g * y, axis=-1, keepdims=True))
        return pre_grad, low_grad, result.astype(BF16).astype(F32)

    def last_step(i, cotangent):
        layer = layers - 1 - i
        pre_grad, low_grad, result = backward(1, layer, cotangent)
        grad_store[layer] = pre_grad
        lowgrad_store[layer] = low_grad
        return result

    def first_step(i, cotangent):
        layer = layers - 1 - i
        pre_grad, low_grad, result = backward(0, layer, cotangent)
        both = layers + layer
        pre_both = jnp.concatenate([pre_grad, grad_store[layer]], axis=0)
        lg_both = jnp.concatenate([low_grad, lowgrad_store[layer]], axis=0)
        low_both = jnp.concatenate([low_store[layer], low_store[both]], axis=0)
        normed_both = jnp.concatenate([normed_store[layer], normed_store[both]], axis=0)
        for first, term in (
            (0, dot_tn(normed_both, lg_both)),
            (rank, ADAPTER_SCALE * dot_tn(pre_both, low_both)),
        ):
            columns = term.reshape(-1, 2, keep_ref.shape[2], rank)
            here = core == 0
            keep_ref[layer, :, :, first : first + rank] = jnp.where(here, columns[:, 0], columns[:, 1])
            send_ref[layer, :, :, first : first + rank] = jnp.where(
                here, columns[:, 1], columns[:, 0]
            ).astype(BF16)
        return result

    entering = lax.fori_loop(0, layers, last_step, BLEND * adjoint[...])
    lax.fori_loop(0, layers, first_step, BLEND * (BLEND * adjoint[...] + entering))


def row_gradients(
    place, latent, target, camera, modulation, sides, last, pieces, layers, rank, chunk, scale_factor
):
    rows, width = latent.shape
    vmem = pl.BlockSpec(memory_space=pltpu.VMEM)
    hbm = pl.BlockSpec(memory_space=pltpu.HBM)
    half = (layers, width // (2 * chunk), chunk, 2 * rank)

    def body(*refs):
        rows_kernel(layers, rank, scale_factor, *refs)

    return pl.pallas_call(
        body,
        out_shape=(jax.ShapeDtypeStruct(half, F32), jax.ShapeDtypeStruct(half, BF16)),
        in_specs=[pl.BlockSpec(memory_space=pltpu.SMEM)] + [vmem] * 4 + [hbm] * (3 + len(pieces)),
        out_specs=(vmem, vmem),
        scratch_shapes=[
            pltpu.VMEM((4, 2, 2, 8, 2, 3 * PART, width), BF16),
            pltpu.VMEM((2,) + sides[0].shape, BF16),
            pltpu.VMEM((2 * layers, rows, width), BF16),
            pltpu.VMEM((2 * layers, rows, width), BF16),
            pltpu.VMEM((2 * layers, rows, rank), BF16),
            pltpu.VMEM((2 * layers, rows, width), F32),
            pltpu.VMEM((layers, rows, width), BF16),
            pltpu.VMEM((layers, rows, rank), BF16),
            pltpu.VMEM((rows, width), F32),
            pltpu.SemaphoreType.DMA((len(pieces) + last.shape[0],)),
            pltpu.SemaphoreType.DMA((2,)),
        ],
        compiler_params=pltpu.CompilerParams(vmem_limit_bytes=61 * 1024 * 1024),
        name="row_gradients",
    )(place, latent, target, camera, modulation, *sides, last, *pieces)


def device_number(x, y, z, core):
    return (x * 2 + y // 2) * 32 + (y % 2) * 16 + z * 2 + core


def route(axis, sign):
    pairs = []
    for x in range(SIZES["x"]):
        for y in range(SIZES["y"]):
            for z in range(SIZES["z"]):
                for core in range(2):
                    to = {"x": x, "y": y, "z": z}
                    step = sign if core == 0 else -sign
                    if axis == "half":
                        to["y"] = (y + 2) % SIZES["y"]
                    else:
                        to[axis] = (to[axis] + step) % SIZES[axis]
                    pairs.append((device_number(x, y, z, core), device_number(core=core, **to)))
    return pairs


def other_core(block):
    pairs = [(i, i ^ 1) for i in range(256)]
    return lax.ppermute(block, EVERYWHERE, pairs)


def together(*arrays):
    return lax.optimization_barrier(arrays)


def onwards(block, axis):
    return lax.ppermute(block, EVERYWHERE, route(axis, 1))


def back(block, axis):
    return lax.ppermute(block, EVERYWHERE, route(axis, -1))


def ring_blocks(block, axis):
    a = onwards(block, axis)
    return [block, a, back(block, axis), onwards(a, axis)]


def in_line(blocks, place, axis, before=0, split=1):
    count = len(blocks)
    rows = blocks[0].shape[-2] // split
    shape = blocks[0].shape[:-2] + (rows, blocks[0].shape[-1])
    shape = shape[:before] + (count,) + shape[before:]

    def body(place_ref, *refs):
        for i, offset in enumerate(ring_offsets(count)):
            if axis == "half":
                at = lax.rem(place_ref[1] // 2 + offset, 2)
            else:
                sense = 1 - 2 * place_ref[3]
                at = place_ref[list(SIZES).index(axis)] - sense * offset
                at = lax.rem(at + 2 * count, count)
            for half in range(split):
                block = refs[i][..., half * rows : (half + 1) * rows, :]
                out = refs[count + half]
                if before == 0:
                    out[at] = block
                else:
                    out[:, at] = block

    vmem = pl.BlockSpec(memory_space=pltpu.VMEM)
    out_shape = (jax.ShapeDtypeStruct(shape, blocks[0].dtype),) * split
    return pl.pallas_call(
        body,
        out_shape=out_shape,
        in_specs=[pl.BlockSpec(memory_space=pltpu.SMEM)] + [vmem] * count,
        out_specs=(vmem,) * split,
        compiler_params=pltpu.CompilerParams(vmem_limit_bytes=8 * 1024 * 1024),
        name="in_line_" + axis,
    )(place, *blocks)


def gathered_rows(rows, place):
    width = rows.shape[1]
    c, ab = rows[2 * PART :], rows[: 2 * PART]
    c1, c2, z1, y1 = onwards(c, "y"), back(c, "y"), onwards(ab, "z"), back(ab, "z")
    c1, c2, z1, y1 = together(c1, c2, z1, y1)
    c3, z2, y2 = together(onwards(c1, "y"), onwards(z1, "z"), back(y1, "z"))
    c = in_line([c, c1, c2, c3], place, "y")[0]
    c1, c2, z3, y3 = together(onwards(c, "x"), back(c, "x"), onwards(z2, "z"), back(y2, "z"))
    c3, z4 = together(onwards(c1, "x"), onwards(z3, "z"))
    c = in_line([c, c1, c2, c3], place, "x")[0]
    same_line = [[16 * low + i for i in range(16)] for low in range(2)]
    last = lax.all_gather(
        c.reshape(4, 2, 2, PART, width), "dp", axis=0, tiled=False, axis_index_groups=same_line
    )
    a, b = in_line([ab, z1, y1, z2, y2, z3, y3, z4], place, "z", split=2)
    a = in_line(ring_blocks(a, "y"), place, "y")[0].reshape(2, 2, 8, PART, width)
    b = in_line(ring_blocks(b, "x"), place, "x")[0]
    a1, b1 = onwards(a, "x"), onwards(b, "y")
    a2, b2 = back(a, "x"), back(b, "y")
    a, a1 = together(a, a1)
    b, b1 = together(b, b1)
    a3, b3 = onwards(a1, "x"), onwards(b1, "y")
    pieces = []
    for mine in ([a, a1, a2, a3], [b, b1, b2, b3]):
        pieces += mine + [other_core(piece) for piece in mine]
    return last, pieces


def gathered_sides(own, place):
    both = in_line([own, lax.ppermute(own, EVERYWHERE, route("half", 1))], place, "half")[0]
    mine = in_line(ring_blocks(both, "x"), place, "x")[0]
    return mine, other_core(mine)


def exchange_and_add(parts, axis, groups=None):
    received = lax.all_to_all(parts, axis, 0, 0, axis_index_groups=groups, tiled=True)
    return received.astype(F32).sum(0)


def local(
    latent,
    target,
    camera_of_token,
    timestep_indices,
    camera_embedding_table,
    timestep_embedding_table,
    layer_norm_gain,
    frozen_weight,
    adapter_down_weight,
    adapter_up_weight,
):
    sections = lax.axis_size("section")
    dp_size = lax.axis_size("dp")
    section = lax.axis_index("section")
    lane = lax.axis_index("dp")
    rank, width = adapter_down_weight.shape[1:]
    rows = latent.shape[0] // sections
    scale_factor = 1.0 / math.sqrt(latent.shape[0] * dp_size)
    place = jnp.stack(
        [section // 2, lax.rem(section, 2) * 2 + lane // 16, lax.rem(lane // 2, 8), lax.rem(lane, 2)]
    ).astype(jnp.int32)
    last, pieces = gathered_rows(frozen_weight[0], place)
    gain = layer_norm_gain
    high = lax.reduce_precision(gain, 8, 7)
    middle = lax.reduce_precision(gain - high, 8, 7)
    lowest = gain - high - middle
    gain_rows = jnp.concatenate([high, middle, lowest, jnp.zeros((EXTRA - 3, width), F32)], axis=0)
    adapter = jnp.where(place[3] == 0, adapter_down_weight[0], adapter_up_weight[0])
    sides = gathered_sides(jnp.concatenate([adapter, gain_rows.astype(BF16)], axis=0), place)

    def my_rows(a):
        return lax.dynamic_slice_in_dim(a, section * rows, rows, 0)

    camera_rows = jnp.dot(
        jax.nn.one_hot(my_rows(camera_of_token), camera_embedding_table.shape[0], dtype=BF16),
        camera_embedding_table,
        preferred_element_type=F32,
    )
    modulation = 1.0 + jnp.dot(
        jax.nn.one_hot(timestep_indices, timestep_embedding_table.shape[0], dtype=BF16),
        timestep_embedding_table,
        preferred_element_type=F32,
    )
    keep, send = row_gradients(
        place,
        my_rows(latent),
        my_rows(target),
        camera_rows,
        modulation,
        sides,
        last,
        pieces,
        sections,
        rank,
        width // dp_size,
        scale_factor,
    )
    on_chip = (keep + other_core(send).astype(F32)).astype(BF16)
    over_sections = exchange_and_add(on_chip, "section")
    same_core = [[i for i in range(32) if i % 2 == core] for core in range(2)]
    summed = exchange_and_add(over_sections.astype(BF16), "dp", same_core)
    turned = summed.T
    return turned[None, :rank], turned[None, rank:]


def solution(mesh):
    in_specs = (
        P("dp", None),
        P("dp", None),
        P("dp"),
        P(),
        P(),
        P(),
        P("section", None),
        P("section", "dp", None),
        P("section", None, None),
        P("section", None, None),
    )
    out_specs = (P("section", None, "dp"), P("section", None, "dp"))
    return jax.shard_map(local, mesh=mesh, in_specs=in_specs, out_specs=out_specs, check_vma=False)
```

time: 314 us -> 271 us (0.86)
  waiting for transfers between devices: 167 us -> 94.4 us
  starting transfers between devices: 0.04 us -> 41.9 us
  blocking collectives: 66.7 us -> 41.3 us
  Pallas kernels: 55.1 us -> 69.7 us
    all_gather x1, waiting for transfers between devices: 166 us -> 0.01 us  [gathered_rows(): lax.all_gather(c.reshape(4, 2, 2, PART, width), 'dp', axis=0, tiled=False...]
    ppermute x0 -> x39, waiting for transfers between devices: none -> 94.4 us  [the longest x18 75.1 us: onwards(): return lax.ppermute(block, EVERYWHERE, route(axis, 1))]
    ppermute x0 -> x39, starting transfers between devices: none -> 41.9 us  [the longest x10 25.2 us: back(): return lax.ppermute(block, EVERYWHERE, route(axis, -1))]
    all_to_all x2, blocking collectives: 66.7 us -> 41.3 us  [exchange_and_add(): lax.all_to_all(parts, axis, 0, 0, axis_index_groups=groups, tiled=True)]
    pallas_call x1 -> x8, Pallas kernels: 55.1 us -> 69.7 us  [the longest x1 63.4 us: row_gradients(): pl.pallas_call(body, out_shape=(jax.ShapeDtypeStruct(half, F32), jax.Shap...]
  transfers between devices with their start and end apart: 1 -> 40, of which waited for: 1 -> 22; matrix products, arithmetic and copies ran while one was open for 2% -> 2% of each run, Pallas kernels for 0% -> 2%
where the time goes in v2:
time: 271 us
  waiting for transfers between devices  94.4 us (35%)
  Pallas kernels  69.7 us (26%)
  starting transfers between devices  41.9 us (15%)
  blocking collectives  41.3 us (15%)
  between operations  14.4 us (5%)
  local copies, waits for them, and re-layouts  4.45 us (2%)
    ppermute x18, waiting for transfers between devices, onwards(): return lax.ppermute(block, EVERYWHERE, route(axis, 1))  75.1 us
    pallas_call x1, Pallas kernels, row_gradients(): pl.pallas_call(body, out_shape=(jax.ShapeDtypeStruct(half, F32), jax.Shap...  63.4 us
    all_to_all x2, blocking collectives, exchange_and_add(): lax.all_to_all(parts, axis, 0, 0, axis_index_groups=groups, tiled=True)  41.3 us
    ppermute x10, starting transfers between devices, back(): return lax.ppermute(block, EVERYWHERE, route(axis, -1))  25.2 us
    ppermute x18, starting transfers between devices, onwards(): return lax.ppermute(block, EVERYWHERE, route(axis, 1))  12.2 us
    ppermute x10, waiting for transfers between devices, other_core(): return lax.ppermute(block, EVERYWHERE, pairs)  8.61 us
    pallas_call x7, Pallas kernels, in_line(): pl.pallas_call(body, out_shape=out_shape, in_specs=[pl.BlockSpec(memory_s...  6.37 us
    ppermute x10, waiting for transfers between devices, back(): return lax.ppermute(block, EVERYWHERE, route(axis, -1))  5.54 us
  transfers between devices with their start and end apart: 40, of which 22 were waited for; matrix products, arithmetic and copies ran while one was open for 2% of the time, Pallas kernels for 2%

profile of v2, /device:TPU:32, one launch (start us, length us, event | category | flops | bytes accessed | tf_op | source)
XLA Modules:
  0.0 270.6 jit_solution(2816859324850524991)
XLA Ops:
  11.1 3.0 %collective-permute-start.6 = (bf16[16,1536]{1,0:T(8,128)(2,1)S(1)}, bf16[16,1536]{1,0:T(8,128)(2,1)S(1)}, u32[]{:S(2)}, u32[]{:S(2)}) collective-permute-start(bf16[16,1536]{1,0:T(8,128)(2,1)S(1)} %slice_bitcast_fusion.1.refs_0_), channel_id=1, source_target_pairs={{0,48},{1,17},{2,50},{3,19},{4,52},{5,21},{6,54},{7,23},{8,56},{9,... | collective-permute-start | bytes 147464 | tf_op jit(solution)/shard_map/ppermute | solution.py:286
  15.9 3.5 %collective-permute-done.5.refs_1_ = bf16[16,1536]{1,0:T(8,128)(2,1)S(1)} collective-permute-done((bf16[16,1536]{1,0:T(8,128)(2,1)S(1)}, bf16[16,1536]{1,0:T(8,128)(2,1)S(1)}, u32[]{:S(2)}, u32[]{:S(2)}) %collective-permute-start.5) | collective-permute-done | bytes 49184 | tf_op jit(solution)/shard_map/ppermute | solution.py:282
  27.7 2.8 %collective-permute-start.13 = (bf16[4,16,1536]{2,1,0:T(8,128)(2,1)S(1)}, bf16[4,16,1536]{2,1,0:T(8,128)(2,1)S(1)}, u32[]{:S(2)}, u32[]{:S(2)}) collective-permute-start(bf16[4,16,1536]{2,1,0:T(8,128)(2,1)S(1)} %in_line_y.2.refs_0_), channel_id=1, source_target_pairs={{0,192},{1,65},{2,194},{3,67},{4,196},{5,69},{6,198},{7,71},{8,200... | collective-permute-start | bytes 589832 | tf_op jit(solution)/shard_map/ppermute | solution.py:286
  32.7 2.7 collective-permute-done.14.refs_5_
  35.4 2.9 %collective-permute-done.15.refs_6_ = bf16[32,1536]{1,0:T(8,128)(2,1)S(1)} collective-permute-done((bf16[32,1536]{1,0:T(8,128)(2,1)S(1)}, bf16[32,1536]{1,0:T(8,128)(2,1)S(1)}, u32[]{:S(2)}, u32[]{:S(2)}) %collective-permute-start.15) | collective-permute-done | bytes 98336 | tf_op jit(solution)/shard_map/ppermute | solution.py:286
  41.2 2.7 collective-permute-done.17.refs_7_
  47.0 2.4 collective-permute-start
  49.3 5.2 %collective-permute-done.refs_1_ = bf16[72,1536]{1,0:T(8,128)(2,1)S(1)} collective-permute-done((bf16[72,1536]{1,0:T(8,128)(2,1)S(1)}, bf16[72,1536]{1,0:T(8,128)(2,1)S(1)}, u32[]{:S(2)}, u32[]{:S(2)}) %collective-permute-start) | collective-permute-done | bytes 221216 | tf_op jit(solution)/shard_map/ppermute | solution.py:357
  55.8 2.6 collective-permute-start.2
  61.3 5.6 %collective-permute-done.1.refs_1_ = bf16[2,72,1536]{2,1,0:T(8,128)(2,1)S(1)} collective-permute-done((bf16[2,72,1536]{2,1,0:T(8,128)(2,1)S(1)}, bf16[2,72,1536]{2,1,0:T(8,128)(2,1)S(1)}, u32[]{:S(2)}, u32[]{:S(2)}) %collective-permute-start.1) | collective-permute-done | bytes 442400 | tf_op jit(solution)/shard_map/ppermute | solution.py:282
  66.9 3.2 %collective-permute-start.29 = (bf16[8,16,1536]{2,1,0:T(8,128)(2,1)S(1)}, bf16[8,16,1536]{2,1,0:T(8,128)(2,1)S(1)}, u32[]{:S(2)}, u32[]{:S(2)}) collective-permute-start(bf16[8,16,1536]{2,1,0:T(8,128)(2,1)S(1)} %get-tuple-element.39.refs_0_), channel_id=1, source_target_pairs={{0,192},{1,65},{2,194},{3,67},{4,196},{5,69},{6,198},{7,71},{8,200... | collective-permute-start | bytes 1179656 | tf_op jit(solution)/shard_map/ppermute | solution.py:286
  70.1 3.0 %collective-permute-done.28.refs_1_ = bf16[8,16,1536]{2,1,0:T(8,128)(2,1)S(1)} collective-permute-done((bf16[8,16,1536]{2,1,0:T(8,128)(2,1)S(1)}, bf16[8,16,1536]{2,1,0:T(8,128)(2,1)S(1)}, u32[]{:S(2)}, u32[]{:S(2)}) %collective-permute-start.28) | collective-permute-done | bytes 393248 | tf_op jit(solution)/shard_map/ppermute | solution.py:282
  73.1 3.6 %collective-permute-start.19 = (bf16[8,16,1536]{2,1,0:T(8,128)(2,1)S(1)}, bf16[8,16,1536]{2,1,0:T(8,128)(2,1)S(1)}, u32[]{:S(2)}, u32[]{:S(2)}) collective-permute-start(bf16[8,16,1536]{2,1,0:T(8,128)(2,1)S(1)} %get-tuple-element.36.refs_0_), channel_id=1, source_target_pairs={{0,48},{1,17},{2,50},{3,19},{4,52},{5,21},{6,54},{7,23},{8,56},{9,... | collective-permute-start | bytes 1179656 | tf_op jit(solution)/shard_map/ppermute | solution.py:286
  78.6 3.5 %collective-permute-done.30.refs_3_ = bf16[8,16,1536]{2,1,0:T(8,128)(2,1)S(1)} collective-permute-done((bf16[8,16,1536]{2,1,0:T(8,128)(2,1)S(1)}, bf16[8,16,1536]{2,1,0:T(8,128)(2,1)S(1)}, u32[]{:S(2)}, u32[]{:S(2)}) %collective-permute-start.30) | collective-permute-done | bytes 393248 | tf_op jit(solution)/shard_map/ppermute | solution.py:282
  84.5 2.6 collective-permute-start.32
  88.9 3.2 %collective-permute-start.22 = (bf16[2,2,8,16,1536]{4,3,2,1,0:T(8,128)(2,1)}, bf16[2,2,8,16,1536]{4,3,2,1,0:T(8,128)(2,1)}, u32[]{:S(2)}, u32[]{:S(2)}) collective-permute-start(bf16[2,2,8,16,1536]{4,3,2,1,0:T(8,128)(2,1)} %bitcast.8.refs_8_), channel_id=1, source_target_pairs={{0,192},{1,65},{2,194},{3,67},{4,196},{5,69},{6,198},{7,71},{8,200... | collective-permute-start | bytes 4718600 | tf_op jit(solution)/shard_map/ppermute | solution.py:286
  92.2 29.1 %collective-permute-done.31.refs_17_ = bf16[4,8,16,1536]{3,2,1,0:T(8,128)(2,1)S(1)} collective-permute-done((bf16[4,8,16,1536]{3,2,1,0:T(8,128)(2,1)S(1)}, bf16[4,8,16,1536]{3,2,1,0:T(8,128)(2,1)S(1)}, u32[]{:S(2)}, u32[]{:S(2)}) %collective-permute-start.31) | collective-permute-done | bytes 1572896 | tf_op jit(solution)/shard_map/ppermute | solution.py:282
  121.8 2.5 collective-permute-done.21.refs_9_
  129.4 16.7 %collective-permute-done.33.refs_19_ = bf16[4,8,16,1536]{3,2,1,0:T(8,128)(2,1)S(1)} collective-permute-done((bf16[4,8,16,1536]{3,2,1,0:T(8,128)(2,1)S(1)}, bf16[4,8,16,1536]{3,2,1,0:T(8,128)(2,1)S(1)}, u32[]{:S(2)}, u32[]{:S(2)}) %collective-permute-start.33) | collective-permute-done | bytes 1572896 | tf_op jit(solution)/shard_map/ppermute | solution.py:282
  152.1 63.4 %row_gradients.1 = (f32[8,16,48,128]{3,2,1,0:T(8,128)}, bf16[8,16,48,128]{3,2,1,0:T(8,128)(2,1)}) custom-call(s32[4]{0:T(128)} %copy-done.3, bf16[32,1536]{1,0:T(8,128)(2,1)} %get-tuple-element.50.refs_1_, bf16[32,1536]{1,0:T(8,128)(2,1)} %get-tuple-element.49.refs_2_, f32[32,1536]{1,0:T(8,128)} %fusion.refs_3_, f32[2,1536]{1,0:T(2,128)} %convolution_add_fusion.refs_4_, ...), custom_call_target="tpu_custom_call" | custom-call | tf_op jit(solution)/shard_map/row_gradients/pallas_call | solution.py:229
  215.7 3.5 %collective-permute-done.38 = bf16[8,16,48,128]{3,2,1,0:T(8,128)(2,1)S(1)} collective-permute-done((bf16[8,16,48,128]{3,2,1,0:T(8,128)(2,1)}, bf16[8,16,48,128]{3,2,1,0:T(8,128)(2,1)S(1)}, u32[]{:S(2)}, u32[]{:S(2)}) %collective-permute-start.38) | collective-permute-done | bytes 1572896 | tf_op jit(solution)/shard_map/ppermute | solution.py:274
  219.2 2.3 add_convert_fusion
  221.5 26.5 %all_to_all.10 = bf16[8,16,48,128]{3,2,1,0:T(8,128)(2,1)S(1)} all-to-all(bf16[8,16,48,128]{3,2,1,0:T(8,128)(2,1)S(1)} %add_convert_fusion), channel_id=1, replica_groups=mesh['section'=8,'dp'=32] {'section'}, dimensions={0} | all-to-all | bytes 3145728 | tf_op jit(solution)/shard_map/all_to_all | solution.py:363
  248.2 14.9 %all_to_all.11 = bf16[16,48,128]{2,1,0:T(8,128)(2,1)S(1)} all-to-all(bf16[16,48,128]{2,1,0:T(8,128)(2,1)S(1)} %reduce_sum.21), channel_id=1, replica_groups={{0,2,4,6,8,10,12,14,16,18,20,22,24,26,28,30},{1,3,5,7,9,11,13,15,17,19,..., dimensions={0} | all-to-all | bytes 393216 | tf_op jit(solution)/shard_map/all_to_all | solution.py:363
  (116 shorter events, 44.9 us)
Async XLA Ops:
  7.2 144.9 %all-gather.2.cloned.1.call-start = ((), (), s32[]{:S(2)}) async-start(), calls=%async_computation.2 | async-start | bytes 13369344 | tf_op jit(solution)/shard_map/all_gather | solution.py:339
  8.3 11.1 %collective-permute-start.8 = (bf16[32,1536]{1,0:T(8,128)(2,1)S(1)}, bf16[32,1536]{1,0:T(8,128)(2,1)S(1)}, u32[]{:S(2)}, u32[]{:S(2)}) collective-permute-start(bf16[32,1536]{1,0:T(8,128)(2,1)S(1)} %slice_bitcast_fusion.refs_0_), channel_id=1, source_target_pairs={{0,14},{1,3},{2,0},{3,5},{4,2},{5,7},{6,4},{7,9},{8,6},{9,11},{10,... | collective-permute-start | bytes 294920 | tf_op jit(solution)/shard_map/ppermute | solution.py:286
  10.1 9.3 %collective-permute-start.7 = (bf16[32,1536]{1,0:T(8,128)(2,1)S(1)}, bf16[32,1536]{1,0:T(8,128)(2,1)S(1)}, u32[]{:S(2)}, u32[]{:S(2)}) collective-permute-start(bf16[32,1536]{1,0:T(8,128)(2,1)S(1)} %slice_bitcast_fusion.refs_0_), channel_id=1, source_target_pairs={{0,2},{1,15},{2,4},{3,1},{4,6},{5,3},{6,8},{7,5},{8,10},{9,7},{10,... | collective-permute-start | bytes 294920 | tf_op jit(solution)/shard_map/ppermute | solution.py:282
  27.7 10.6 %collective-permute-start.13 = (bf16[4,16,1536]{2,1,0:T(8,128)(2,1)S(1)}, bf16[4,16,1536]{2,1,0:T(8,128)(2,1)S(1)}, u32[]{:S(2)}, u32[]{:S(2)}) collective-permute-start(bf16[4,16,1536]{2,1,0:T(8,128)(2,1)S(1)} %in_line_y.2.refs_0_), channel_id=1, source_target_pairs={{0,192},{1,65},{2,194},{3,67},{4,196},{5,69},{6,198},{7,71},{8,200... | collective-permute-start | bytes 589832 | tf_op jit(solution)/shard_map/ppermute | solution.py:286
  30.6 7.8 %collective-permute-start.12 = (bf16[4,16,1536]{2,1,0:T(8,128)(2,1)S(1)}, bf16[4,16,1536]{2,1,0:T(8,128)(2,1)S(1)}, u32[]{:S(2)}, u32[]{:S(2)}) collective-permute-start(bf16[4,16,1536]{2,1,0:T(8,128)(2,1)S(1)} %in_line_y.2.refs_0_), channel_id=1, source_target_pairs={{0,64},{1,193},{2,66},{3,195},{4,68},{5,197},{6,70},{7,199},{8,72}... | collective-permute-start | bytes 589832 | tf_op jit(solution)/shard_map/ppermute | solution.py:282
  55.1 11.8 %collective-permute-start.1 = (bf16[2,72,1536]{2,1,0:T(8,128)(2,1)S(1)}, bf16[2,72,1536]{2,1,0:T(8,128)(2,1)S(1)}, u32[]{:S(2)}, u32[]{:S(2)}) collective-permute-start(bf16[2,72,1536]{2,1,0:T(8,128)(2,1)S(1)} %in_line_half.1.refs_0_), channel_id=1, source_target_pairs={{0,64},{1,193},{2,66},{3,195},{4,68},{5,197},{6,70},{7,199},{8,72}... | collective-permute-start | bytes 1327112 | tf_op jit(solution)/shard_map/ppermute | solution.py:282
  55.8 17.3 %collective-permute-start.2 = (bf16[2,72,1536]{2,1,0:T(8,128)(2,1)S(1)}, bf16[2,72,1536]{2,1,0:T(8,128)(2,1)S(1)}, u32[]{:S(2)}, u32[]{:S(2)}) collective-permute-start(bf16[2,72,1536]{2,1,0:T(8,128)(2,1)S(1)} %in_line_half.1.refs_0_), channel_id=1, source_target_pairs={{0,192},{1,65},{2,194},{3,67},{4,196},{5,69},{6,198},{7,71},{8,200... | collective-permute-start | bytes 1327112 | tf_op jit(solution)/shard_map/ppermute | solution.py:286
  59.0 14.1 %collective-permute-start.28 = (bf16[8,16,1536]{2,1,0:T(8,128)(2,1)S(1)}, bf16[8,16,1536]{2,1,0:T(8,128)(2,1)S(1)}, u32[]{:S(2)}, u32[]{:S(2)}) collective-permute-start(bf16[8,16,1536]{2,1,0:T(8,128)(2,1)S(1)} %get-tuple-element.39.refs_0_), channel_id=1, source_target_pairs={{0,64},{1,193},{2,66},{3,195},{4,68},{5,197},{6,70},{7,199},{8,72}... | collective-permute-start | bytes 1179656 | tf_op jit(solution)/shard_map/ppermute | solution.py:282
  59.1 17.6 %collective-permute-start.18 = (bf16[8,16,1536]{2,1,0:T(8,128)(2,1)S(1)}, bf16[8,16,1536]{2,1,0:T(8,128)(2,1)S(1)}, u32[]{:S(2)}, u32[]{:S(2)}) collective-permute-start(bf16[8,16,1536]{2,1,0:T(8,128)(2,1)S(1)} %get-tuple-element.36.refs_0_), channel_id=1, source_target_pairs={{0,16},{1,49},{2,18},{3,51},{4,20},{5,53},{6,22},{7,55},{8,24},{9,... | collective-permute-start | bytes 1179656 | tf_op jit(solution)/shard_map/ppermute | solution.py:282
  66.8 11.0 %collective-permute-start.3 = (bf16[2,72,1536]{2,1,0:T(8,128)(2,1)S(1)}, bf16[2,72,1536]{2,1,0:T(8,128)(2,1)S(1)}, u32[]{:S(2)}, u32[]{:S(2)}) collective-permute-start(bf16[2,72,1536]{2,1,0:T(8,128)(2,1)S(1)} %collective-permute-done.1.refs_1_), channel_id=1, source_target_pairs={{0,64},{1,193},{2,66},{3,195},{4,68},{5,197},{6,70},{7,199},{8,72}... | collective-permute-start | bytes 1327112 | tf_op jit(solution)/shard_map/ppermute | solution.py:282
  66.9 11.8 %collective-permute-start.29 = (bf16[8,16,1536]{2,1,0:T(8,128)(2,1)S(1)}, bf16[8,16,1536]{2,1,0:T(8,128)(2,1)S(1)}, u32[]{:S(2)}, u32[]{:S(2)}) collective-permute-start(bf16[8,16,1536]{2,1,0:T(8,128)(2,1)S(1)} %get-tuple-element.39.refs_0_), channel_id=1, source_target_pairs={{0,192},{1,65},{2,194},{3,67},{4,196},{5,69},{6,198},{7,71},{8,200... | collective-permute-start | bytes 1179656 | tf_op jit(solution)/shard_map/ppermute | solution.py:286
  73.1 9.0 %collective-permute-start.30 = (bf16[8,16,1536]{2,1,0:T(8,128)(2,1)S(1)}, bf16[8,16,1536]{2,1,0:T(8,128)(2,1)S(1)}, u32[]{:S(2)}, u32[]{:S(2)}) collective-permute-start(bf16[8,16,1536]{2,1,0:T(8,128)(2,1)S(1)} %collective-permute-done.28.refs_1_), channel_id=1, source_target_pairs={{0,64},{1,193},{2,66},{3,195},{4,68},{5,197},{6,70},{7,199},{8,72}... | collective-permute-start | bytes 1179656 | tf_op jit(solution)/shard_map/ppermute | solution.py:282
  73.1 14.0 %collective-permute-start.19 = (bf16[8,16,1536]{2,1,0:T(8,128)(2,1)S(1)}, bf16[8,16,1536]{2,1,0:T(8,128)(2,1)S(1)}, u32[]{:S(2)}, u32[]{:S(2)}) collective-permute-start(bf16[8,16,1536]{2,1,0:T(8,128)(2,1)S(1)} %get-tuple-element.36.refs_0_), channel_id=1, source_target_pairs={{0,48},{1,17},{2,50},{3,19},{4,52},{5,21},{6,54},{7,23},{8,56},{9,... | collective-permute-start | bytes 1179656 | tf_op jit(solution)/shard_map/ppermute | solution.py:286
  76.7 10.4 %collective-permute-start.20 = (bf16[8,16,1536]{2,1,0:T(8,128)(2,1)S(1)}, bf16[8,16,1536]{2,1,0:T(8,128)(2,1)S(1)}, u32[]{:S(2)}, u32[]{:S(2)}) collective-permute-start(bf16[8,16,1536]{2,1,0:T(8,128)(2,1)S(1)} %collective-permute-done.18.refs_1_), channel_id=1, source_target_pairs={{0,16},{1,49},{2,18},{3,51},{4,20},{5,53},{6,22},{7,55},{8,24},{9,... | collective-permute-start | bytes 1179656 | tf_op jit(solution)/shard_map/ppermute | solution.py:282
  78.5 45.8 %collective-permute-start.4 = (bf16[4,2,72,1536]{3,2,1,0:T(8,128)(2,1)S(1)}, bf16[4,2,72,1536]{3,2,1,0:T(8,128)(2,1)S(1)}, u32[]{:S(2)}, u32[]{:S(2)}) collective-permute-start(bf16[4,2,72,1536]{3,2,1,0:T(8,128)(2,1)S(1)} %in_line_x.3.refs_5_), channel_id=1, source_target_pairs={{0,1},{1,0},{2,3},{3,2},{4,5},{5,4},{6,7},{7,6},{8,9},{9,8},{10,11... | collective-permute-start | bytes 5308424 | tf_op jit(solution)/shard_map/ppermute | solution.py:274
  82.8 38.5 %collective-permute-start.31 = (bf16[4,8,16,1536]{3,2,1,0:T(8,128)(2,1)S(1)}, bf16[4,8,16,1536]{3,2,1,0:T(8,128)(2,1)S(1)}, u32[]{:S(2)}, u32[]{:S(2)}) collective-permute-start(bf16[4,8,16,1536]{3,2,1,0:T(8,128)(2,1)S(1)} %in_line_x.5.refs_16_), channel_id=1, source_target_pairs={{0,16},{1,49},{2,18},{3,51},{4,20},{5,53},{6,22},{7,55},{8,24},{9,... | collective-permute-start | bytes 4718600 | tf_op jit(solution)/shard_map/ppermute | solution.py:282
  84.5 36.8 %collective-permute-start.32 = (bf16[4,8,16,1536]{3,2,1,0:T(8,128)(2,1)S(1)}, bf16[4,8,16,1536]{3,2,1,0:T(8,128)(2,1)S(1)}, u32[]{:S(2)}, u32[]{:S(2)}) collective-permute-start(bf16[4,8,16,1536]{3,2,1,0:T(8,128)(2,1)S(1)} %in_line_x.5.refs_16_), channel_id=1, source_target_pairs={{0,48},{1,17},{2,50},{3,19},{4,52},{5,21},{6,54},{7,23},{8,56},{9,... | collective-permute-start | bytes 4718600 | tf_op jit(solution)/shard_map/ppermute | solution.py:286
  88.9 35.4 %collective-permute-start.21 = (bf16[2,2,8,16,1536]{4,3,2,1,0:T(8,128)(2,1)}, bf16[2,2,8,16,1536]{4,3,2,1,0:T(8,128)(2,1)}, u32[]{:S(2)}, u32[]{:S(2)}) collective-permute-start(bf16[2,2,8,16,1536]{4,3,2,1,0:T(8,128)(2,1)} %bitcast.8.refs_8_), channel_id=1, source_target_pairs={{0,64},{1,193},{2,66},{3,195},{4,68},{5,197},{6,70},{7,199},{8,72}... | collective-permute-start | bytes 4718600 | tf_op jit(solution)/shard_map/ppermute | solution.py:282
  88.9 35.5 %collective-permute-start.22 = (bf16[2,2,8,16,1536]{4,3,2,1,0:T(8,128)(2,1)}, bf16[2,2,8,16,1536]{4,3,2,1,0:T(8,128)(2,1)}, u32[]{:S(2)}, u32[]{:S(2)}) collective-permute-start(bf16[2,2,8,16,1536]{4,3,2,1,0:T(8,128)(2,1)} %bitcast.8.refs_8_), channel_id=1, source_target_pairs={{0,192},{1,65},{2,194},{3,67},{4,196},{5,69},{6,198},{7,71},{8,200... | collective-permute-start | bytes 4718600 | tf_op jit(solution)/shard_map/ppermute | solution.py:286
  124.4 21.7 %collective-permute-start.33 = (bf16[4,8,16,1536]{3,2,1,0:T(8,128)(2,1)S(1)}, bf16[4,8,16,1536]{3,2,1,0:T(8,128)(2,1)S(1)}, u32[]{:S(2)}, u32[]{:S(2)}) collective-permute-start(bf16[4,8,16,1536]{3,2,1,0:T(8,128)(2,1)S(1)} %collective-permute-done.31.refs_17_), channel_id=1, source_target_pairs={{0,16},{1,49},{2,18},{3,51},{4,20},{5,53},{6,22},{7,55},{8,24},{9,... | collective-permute-start | bytes 4718600 | tf_op jit(solution)/shard_map/ppermute | solution.py:282
  124.5 22.2 %collective-permute-start.23 = (bf16[2,2,8,16,1536]{4,3,2,1,0:T(8,128)(2,1)}, bf16[2,2,8,16,1536]{4,3,2,1,0:T(8,128)(2,1)}, u32[]{:S(2)}, u32[]{:S(2)}) collective-permute-start(bf16[2,2,8,16,1536]{4,3,2,1,0:T(8,128)(2,1)} %collective-permute-done.21.refs_9_), channel_id=1, source_target_pairs={{0,64},{1,193},{2,66},{3,195},{4,68},{5,197},{6,70},{7,199},{8,72}... | collective-permute-start | bytes 4718600 | tf_op jit(solution)/shard_map/ppermute | solution.py:282
  127.0 23.6 %collective-permute-start.25 = (bf16[2,2,8,16,1536]{4,3,2,1,0:T(8,128)(2,1)}, bf16[2,2,8,16,1536]{4,3,2,1,0:T(8,128)(2,1)}, u32[]{:S(2)}, u32[]{:S(2)}) collective-permute-start(bf16[2,2,8,16,1536]{4,3,2,1,0:T(8,128)(2,1)} %collective-permute-done.21.refs_9_), channel_id=1, source_target_pairs={{0,1},{1,0},{2,3},{3,2},{4,5},{5,4},{6,7},{7,6},{8,9},{9,8},{10,11... | collective-permute-start | bytes 4718600 | tf_op jit(solution)/shard_map/ppermute | solution.py:274
  127.7 22.9 %collective-permute-start.24 = (bf16[2,2,8,16,1536]{4,3,2,1,0:T(8,128)(2,1)}, bf16[2,2,8,16,1536]{4,3,2,1,0:T(8,128)(2,1)}, u32[]{:S(2)}, u32[]{:S(2)}) collective-permute-start(bf16[2,2,8,16,1536]{4,3,2,1,0:T(8,128)(2,1)} %bitcast.8.refs_8_), channel_id=1, source_target_pairs={{0,1},{1,0},{2,3},{3,2},{4,5},{5,4},{6,7},{7,6},{8,9},{9,8},{10,11... | collective-permute-start | bytes 4718600 | tf_op jit(solution)/shard_map/ppermute | solution.py:274
  129.2 21.4 %collective-permute-start.26 = (bf16[2,2,8,16,1536]{4,3,2,1,0:T(8,128)(2,1)}, bf16[2,2,8,16,1536]{4,3,2,1,0:T(8,128)(2,1)}, u32[]{:S(2)}, u32[]{:S(2)}) collective-permute-start(bf16[2,2,8,16,1536]{4,3,2,1,0:T(8,128)(2,1)} %collective-permute-done.22.refs_10_), channel_id=1, source_target_pairs={{0,1},{1,0},{2,3},{3,2},{4,5},{5,4},{6,7},{7,6},{8,9},{9,8},{10,11... | collective-permute-start | bytes 4718600 | tf_op jit(solution)/shard_map/ppermute | solution.py:274
  (33 other events, 743.2 us)
Sparse Core Ops, SparseCore 0:
  46.9 73.9 all-gather.1

commit v3 on v2

--- a/solution.py
+++ b/solution.py
@@ -14,6 +14,7 @@
 EVERYWHERE = ("section", "dp")
 SIZES = {"x": 4, "y": 4, "z": 8}
 PART = 16
+CHUNK = 512
 F32 = jnp.float32
 BF16 = jnp.bfloat16
 
@@ -93,9 +94,10 @@
     hidden_store,
     normed_store,
     low_store,
-    pre_store,
+    slope_store,
     grad_store,
     lowgrad_store,
+    inverse_store,
     adjoint,
     sem,
     side_sem,
@@ -103,33 +105,37 @@
     rows, width = latent_ref.shape
     core = place_ref[3]
 
-    copies = []
-    number = 0
-    for axis, name in enumerate(("x", "y")):
-        count = SIZES[name]
-        for half in range(2):
-            owner = core if half == 0 else 1 - core
-            sense = 1 - 2 * owner
-            for offset in ring_offsets(count):
-                at = lax.rem(place_ref[axis] - sense * offset + 2 * count, count)
-                if name == "x":
-                    home = weights.at[at, :, :, :, owner, pl.ds(0, PART)]
-                else:
-                    home = weights.at[:, at // 2, lax.rem(at, 2), :, owner, pl.ds(PART, PART)]
-                copies.append(pltpu.make_async_copy(pieces[number], home, sem.at[number]))
-                number += 1
-    for z in range(SIZES["z"]):
-        for owner in range(2):
-            home = weights.at[:, :, :, z, owner, pl.ds(2 * PART, PART)]
-            copies.append(pltpu.make_async_copy(last.at[2 * z + owner], home, sem.at[number]))
-            number += 1
     for half in range(2):
         owner = core if half == 0 else 1 - core
-        copies.append(pltpu.make_async_copy(sides[half], side.at[owner], side_sem.at[half]))
-    for one in copies:
-        one.start()
-    for one in copies:
-        one.wait()
+        pltpu.make_async_copy(sides[half], side.at[owner], side_sem.at[half]).start()
+    count = SIZES["x"]
+    arrivals = [
+        (half, i, core if half == 0 else 1 - core, offset)
+        for half in range(2)
+        for i, offset in enumerate(ring_offsets(count))
+    ]
+
+    def position(axis, owner, offset):
+        return lax.rem(place_ref[axis] - (1 - 2 * owner) * offset + 2 * count, count)
+
+    def fetch(x):
+        for half, i, owner, offset in arrivals:
+            home = weights.at[x, :, :, :, owner, pl.ds(0, PART)]
+            one = pltpu.make_async_copy(pieces[count * half + i], home, sem.at[x])
+            pl.when(position(0, owner, offset) == x)(one.start)
+            at = position(1, owner, offset)
+            home = weights.at[x, at // 2, lax.rem(at, 2), :, owner, pl.ds(PART, PART)]
+            block = pieces[count * (2 + half) + i]
+            pltpu.make_async_copy(block.at[x], home, sem.at[x]).start()
+        for z in range(SIZES["z"]):
+            for owner in range(2):
+                home = weights.at[x, :, :, z, owner, pl.ds(2 * PART, PART)]
+                pltpu.make_async_copy(last.at[2 * z + owner, x], home, sem.at[x]).start()
+
+    fetch(0)
+
+    def arrive(x):
+        pltpu.make_async_copy(weights.at[x], weights.at[x], sem.at[x]).wait()
 
     def weight(layer):
         return weights[layer // 2, lax.rem(layer, 2)].reshape(width, width)
@@ -149,19 +155,30 @@
         down, up = adapter(layer)
         hf = hidden.astype(F32)
         inverse = lax.rsqrt(jnp.mean(hf * hf, axis=-1, keepdims=True) + EPSILON)
+        inverse_store[slot] = inverse
         normed = (hf * inverse * scale_row(layer, step)).astype(BF16)
         low = dot_nt(normed, down).astype(BF16)
         pre = dot_nn(normed, weight(layer)) + ADAPTER_SCALE * dot_nn(low, up)
         normed_store[slot] = normed
         low_store[slot] = low
-        pre_store[slot] = pre
-        return (hf + pre * jax.nn.sigmoid(pre)).astype(BF16)
+        s = jax.nn.sigmoid(pre)
+        slope_store[slot] = s * (1.0 + pre * (1.0 - s))
+        return (hf + pre * s).astype(BF16)
 
     latent = latent_ref[...].astype(F32)
     camera = camera_ref[...]
-    hidden = lax.fori_loop(
-        0, layers, lambda layer, h: forward(0, layer, h), (latent + camera).astype(BF16)
-    )
+    for half in range(2):
+        owner = core if half == 0 else 1 - core
+        pltpu.make_async_copy(sides[half], side.at[owner], side_sem.at[half]).wait()
+
+    def first_pass(layer, h):
+        x = layer // 2
+        first = lax.rem(layer, 2) == 0
+        pl.when(first)(lambda: arrive(x))
+        pl.when(first & (x + 1 < count))(lambda: fetch(x + 1))
+        return forward(0, layer, h)
+
+    hidden = lax.fori_loop(0, layers, first_pass, (latent + camera).astype(BF16))
     middle = (BLEND * (latent + hidden.astype(F32))).astype(BF16).astype(F32)
     hidden = lax.fori_loop(
         0, layers, lambda layer, h: forward(1, layer, h), (middle + camera).astype(BF16)
@@ -172,13 +189,18 @@
     def backward(step, layer, cotangent):
         slot = step * layers + layer
         down, up = adapter(layer)
-        pre = pre_store[slot]
-        s = jax.nn.sigmoid(pre)
-        pre_grad = (cotangent * s * (1.0 + pre * (1.0 - s))).astype(BF16)
+        pre_grad = (cotangent * slope_store[slot]).astype(BF16)
         low_grad = (ADAPTER_SCALE * dot_nt(pre_grad, up)).astype(BF16)
-        norm_grad = dot_nt(pre_grad, weight(layer)) + dot_nn(low_grad, down)
+        w = weight(layer)
+        norm_grad = jnp.concatenate(
+            [
+                dot_nt(pre_grad, w[j : j + CHUNK]) + dot_nn(low_grad, down[:, j : j + CHUNK])
+                for j in range(0, width, CHUNK)
+            ],
+            axis=1,
+        )
         hf = hidden_store[slot].astype(F32)
-        inverse = lax.rsqrt(jnp.mean(hf * hf, axis=-1, keepdims=True) + EPSILON)
+        inverse = inverse_store[slot]
         y = hf * inverse
         g = norm_grad * scale_row(layer, step)
         result = cotangent + inverse * (g - y * jnp.mean(g * y, axis=-1, keepdims=True))
@@ -240,8 +262,9 @@
             pltpu.VMEM((2 * layers, rows, width), F32),
             pltpu.VMEM((layers, rows, width), BF16),
             pltpu.VMEM((layers, rows, rank), BF16),
+            pltpu.VMEM((2 * layers, rows, 1), F32),
             pltpu.VMEM((rows, width), F32),
-            pltpu.SemaphoreType.DMA((len(pieces) + last.shape[0],)),
+            pltpu.SemaphoreType.DMA((SIZES["x"],)),
             pltpu.SemaphoreType.DMA((2,)),
         ],
         compiler_params=pltpu.CompilerParams(vmem_limit_bytes=61 * 1024 * 1024),
@@ -262,7 +285,7 @@
                     to = {"x": x, "y": y, "z": z}
                     step = sign if core == 0 else -sign
                     if axis == "half":
-                        to["y"] = (y + 2) % SIZES["y"]
+                        to["y"] = SIZES["y"] - 1 - y
                     else:
                         to[axis] = (to[axis] + step) % SIZES[axis]
                     pairs.append((device_number(x, y, z, core), device_number(core=core, **to)))
@@ -325,15 +348,17 @@
     )(place, *blocks)
 
 
-def gathered_rows(rows, place):
+def gathered_rows(rows, side, place):
     width = rows.shape[1]
     c, ab = rows[2 * PART :], rows[: 2 * PART]
     c1, c2, z1, y1 = onwards(c, "y"), back(c, "y"), onwards(ab, "z"), back(ab, "z")
     c1, c2, z1, y1 = together(c1, c2, z1, y1)
     c3, z2, y2 = together(onwards(c1, "y"), onwards(z1, "z"), back(y1, "z"))
     c = in_line([c, c1, c2, c3], place, "y")[0]
+    side, z2 = together(side, z2)
+    half = onwards(side, "half")
     c1, c2, z3, y3 = together(onwards(c, "x"), back(c, "x"), onwards(z2, "z"), back(y2, "z"))
-    c3, z4 = together(onwards(c1, "x"), onwards(z3, "z"))
+    c3, z4, half = together(onwards(c1, "x"), onwards(z3, "z"), half)
     c = in_line([c, c1, c2, c3], place, "x")[0]
     same_line = [[16 * low + i for i in range(16)] for low in range(2)]
     last = lax.all_gather(
@@ -342,21 +367,16 @@
     a, b = in_line([ab, z1, y1, z2, y2, z3, y3, z4], place, "z", split=2)
     a = in_line(ring_blocks(a, "y"), place, "y")[0].reshape(2, 2, 8, PART, width)
     b = in_line(ring_blocks(b, "x"), place, "x")[0]
+    side = in_line(ring_blocks(in_line([side, half], place, "half")[0], "x"), place, "x")[0]
     a1, b1 = onwards(a, "x"), onwards(b, "y")
     a2, b2 = back(a, "x"), back(b, "y")
-    a, a1 = together(a, a1)
-    b, b1 = together(b, b1)
+    small = onwards(a[0, 0, 0], "x")
+    a0, b0, side, _ = together(a, b, side, small)
     a3, b3 = onwards(a1, "x"), onwards(b1, "y")
     pieces = []
-    for mine in ([a, a1, a2, a3], [b, b1, b2, b3]):
+    for mine in ([a0, a1, a2, a3], [b0, b1, b2, b3]):
         pieces += mine + [other_core(piece) for piece in mine]
-    return last, pieces
-
-
-def gathered_sides(own, place):
-    both = in_line([own, lax.ppermute(own, EVERYWHERE, route("half", 1))], place, "half")[0]
-    mine = in_line(ring_blocks(both, "x"), place, "x")[0]
-    return mine, other_core(mine)
+    return last, pieces, (side, other_core(side))
 
 
 def exchange_and_add(parts, axis, groups=None):
@@ -386,14 +406,14 @@
     place = jnp.stack(
         [section // 2, lax.rem(section, 2) * 2 + lane // 16, lax.rem(lane // 2, 8), lax.rem(lane, 2)]
     ).astype(jnp.int32)
-    last, pieces = gathered_rows(frozen_weight[0], place)
     gain = layer_norm_gain
     high = lax.reduce_precision(gain, 8, 7)
     middle = lax.reduce_precision(gain - high, 8, 7)
     lowest = gain - high - middle
     gain_rows = jnp.concatenate([high, middle, lowest, jnp.zeros((EXTRA - 3, width), F32)], axis=0)
     adapter = jnp.where(place[3] == 0, adapter_down_weight[0], adapter_up_weight[0])
-    sides = gathered_sides(jnp.concatenate([adapter, gain_rows.astype(BF16)], axis=0), place)
+    side = jnp.concatenate([adapter, gain_rows.astype(BF16)], axis=0)
+    last, pieces, sides = gathered_rows(frozen_weight[0], side, place)
 
     def my_rows(a):
         return lax.dynamic_slice_in_dim(a, section * rows, rows, 0)

time: 271 us -> 255 us (0.941)
  waiting for transfers between devices: 94.4 us -> 83.8 us
  Pallas kernels: 69.7 us -> 63.8 us
    ppermute x18 -> x19, waiting for transfers between devices: 75.1 us -> 51.5 us  [onwards(): return lax.ppermute(block, EVERYWHERE, route(axis, 1))]
    ppermute x10, waiting for transfers between devices: 5.54 us -> 26.9 us  [back(): return lax.ppermute(block, EVERYWHERE, route(axis, -1))]
    ppermute x1 -> x0, waiting for transfers between devices: 5.15 us -> none  [gathered_sides(): lax.ppermute(own, EVERYWHERE, route('half', 1))]
    pallas_call x1, Pallas kernels: 63.4 us -> 58.6 us  [row_gradients(): pl.pallas_call(body, out_shape=(jax.ShapeDtypeStruct(half, F32), jax.Shap...]
    ppermute x18 -> x19, starting transfers between devices: 12.2 us -> 16.7 us  [onwards(): return lax.ppermute(block, EVERYWHERE, route(axis, 1))]
    ppermute x10, starting transfers between devices: 25.2 us -> 20.9 us  [back(): return lax.ppermute(block, EVERYWHERE, route(axis, -1))]
    ppermute x10, waiting for transfers between devices: 8.61 us -> 5.39 us  [other_core(): return lax.ppermute(block, EVERYWHERE, pairs)]
  transfers between devices with their start and end apart: 40 -> 40, of which waited for: 22 -> 22; matrix products, arithmetic and copies ran while one was open for 2% -> 2% of each run, Pallas kernels for 2% -> 1%
where the time goes in v3:
time: 255 us; the launch traced here: 254 us
  waiting for transfers between devices  83.8 us (33%)
  Pallas kernels  63.8 us (25%)
  blocking collectives  41.6 us (16%)
  starting transfers between devices  39.2 us (15%)
  between operations  14.3 us (6%)
  local copies, waits for them, and re-layouts  5.62 us (2%)
  other arithmetic  4.29 us (2%)
    pallas_call x1, Pallas kernels, row_gradients(): pl.pallas_call(body, out_shape=(jax.ShapeDtypeStruct(half, F32), jax.Shap...  58.6 us
    ppermute x19, waiting for transfers between devices, onwards(): return lax.ppermute(block, EVERYWHERE, route(axis, 1))  51.5 us
    all_to_all x2, blocking collectives, exchange_and_add(): lax.all_to_all(parts, axis, 0, 0, axis_index_groups=groups, tiled=True)  41.6 us
    ppermute x10, waiting for transfers between devices, back(): return lax.ppermute(block, EVERYWHERE, route(axis, -1))  26.9 us
    ppermute x10, starting transfers between devices, back(): return lax.ppermute(block, EVERYWHERE, route(axis, -1))  20.9 us
    ppermute x19, starting transfers between devices, onwards(): return lax.ppermute(block, EVERYWHERE, route(axis, 1))  16.7 us
    ppermute x10, waiting for transfers between devices, other_core(): return lax.ppermute(block, EVERYWHERE, pairs)  5.39 us
    pallas_call x7, Pallas kernels, in_line(): pl.pallas_call(body, out_shape=out_shape, in_specs=[pl.BlockSpec(memory_s...  5.19 us
  transfers between devices with their start and end apart: 40, of which 22 were waited for; matrix products, arithmetic and copies ran while one was open for 2% of the time, Pallas kernels for 1%

profile of v3, /device:TPU:32, one launch (start us, length us, event | category | flops | bytes accessed | tf_op | source)
XLA Modules:
  0.0 254.3 jit_solution(466361429178301131)
XLA Ops:
  8.1 3.0 %collective-permute-start.1 = (bf16[16,1536]{1,0:T(8,128)(2,1)S(1)}, bf16[16,1536]{1,0:T(8,128)(2,1)S(1)}, u32[]{:S(2)}, u32[]{:S(2)}) collective-permute-start(bf16[16,1536]{1,0:T(8,128)(2,1)S(1)} %slice_bitcast_fusion.1.refs_0_), channel_id=1, source_target_pairs={{0,48},{1,17},{2,50},{3,19},{4,52},{5,21},{6,54},{7,23},{8,56},{9,... | collective-permute-start | bytes 147464 | tf_op jit(solution)/shard_map/ppermute | solution.py:309
  17.3 3.2 %collective-permute-done.2.refs_1_ = bf16[32,1536]{1,0:T(8,128)(2,1)S(1)} collective-permute-done((bf16[32,1536]{1,0:T(8,128)(2,1)S(1)}, bf16[32,1536]{1,0:T(8,128)(2,1)S(1)}, u32[]{:S(2)}, u32[]{:S(2)}) %collective-permute-start.2) | collective-permute-done | bytes 98336 | tf_op jit(solution)/shard_map/ppermute | solution.py:305
  21.1 3.2 %collective-permute-start.6 = (bf16[32,1536]{1,0:T(8,128)(2,1)S(1)}, bf16[32,1536]{1,0:T(8,128)(2,1)S(1)}, u32[]{:S(2)}, u32[]{:S(2)}) collective-permute-start(bf16[32,1536]{1,0:T(8,128)(2,1)S(1)} %collective-permute-done.3.refs_2_), channel_id=1, source_target_pairs={{0,14},{1,3},{2,0},{3,5},{4,2},{5,7},{6,4},{7,9},{8,6},{9,11},{10,... | collective-permute-start | bytes 294920 | tf_op jit(solution)/shard_map/ppermute | solution.py:309
  27.5 2.8 %collective-permute-start.8 = (bf16[4,16,1536]{2,1,0:T(8,128)(2,1)S(1)}, bf16[4,16,1536]{2,1,0:T(8,128)(2,1)S(1)}, u32[]{:S(2)}, u32[]{:S(2)}) collective-permute-start(bf16[4,16,1536]{2,1,0:T(8,128)(2,1)S(1)} %in_line_y.2.refs_0_), channel_id=1, source_target_pairs={{0,192},{1,65},{2,194},{3,67},{4,196},{5,69},{6,198},{7,71},{8,200... | collective-permute-start | bytes 589832 | tf_op jit(solution)/shard_map/ppermute | solution.py:309
  31.2 3.3 %collective-permute-start.10 = (bf16[32,1536]{1,0:T(8,128)(2,1)S(1)}, bf16[32,1536]{1,0:T(8,128)(2,1)S(1)}, u32[]{:S(2)}, u32[]{:S(2)}) collective-permute-start(bf16[32,1536]{1,0:T(8,128)(2,1)S(1)} %collective-permute-done.6.refs_4_), channel_id=1, source_target_pairs={{0,14},{1,3},{2,0},{3,5},{4,2},{5,7},{6,4},{7,9},{8,6},{9,11},{10,... | collective-permute-start | bytes 294920 | tf_op jit(solution)/shard_map/ppermute | solution.py:309
  34.5 2.7 %collective-permute-start.13 = (bf16[72,1536]{1,0:T(8,128)(2,1)S(1)}, bf16[72,1536]{1,0:T(8,128)(2,1)S(1)}, u32[]{:S(2)}, u32[]{:S(2)}) collective-permute-start(bf16[72,1536]{1,0:T(8,128)(2,1)S(1)} %concatenate.6.refs_0_), channel_id=1, source_target_pairs={{0,48},{1,49},{2,50},{3,51},{4,52},{5,53},{6,54},{7,55},{8,56},{9,... | collective-permute-start | bytes 663560 | tf_op jit(solution)/shard_map/ppermute | solution.py:305
  37.2 3.2 %collective-permute-done.9.refs_5_ = bf16[32,1536]{1,0:T(8,128)(2,1)S(1)} collective-permute-done((bf16[32,1536]{1,0:T(8,128)(2,1)S(1)}, bf16[32,1536]{1,0:T(8,128)(2,1)S(1)}, u32[]{:S(2)}, u32[]{:S(2)}) %collective-permute-start.9) | collective-permute-done | bytes 98336 | tf_op jit(solution)/shard_map/ppermute | solution.py:305
  41.7 5.3 %collective-permute-done.12.refs_7_ = bf16[32,1536]{1,0:T(8,128)(2,1)S(1)} collective-permute-done((bf16[32,1536]{1,0:T(8,128)(2,1)S(1)}, bf16[32,1536]{1,0:T(8,128)(2,1)S(1)}, u32[]{:S(2)}, u32[]{:S(2)}) %collective-permute-start.12) | collective-permute-done | bytes 98336 | tf_op jit(solution)/shard_map/ppermute | solution.py:305
  51.2 2.7 %collective-permute-start.20 = (bf16[2,72,1536]{2,1,0:T(8,128)(2,1)S(1)}, bf16[2,72,1536]{2,1,0:T(8,128)(2,1)S(1)}, u32[]{:S(2)}, u32[]{:S(2)}) collective-permute-start(bf16[2,72,1536]{2,1,0:T(8,128)(2,1)S(1)} %in_line_half.1.refs_0_), channel_id=1, source_target_pairs={{0,64},{1,193},{2,66},{3,195},{4,68},{5,197},{6,70},{7,199},{8,72}... | collective-permute-start | bytes 1327112 | tf_op jit(solution)/shard_map/ppermute | solution.py:305
  56.3 5.5 %collective-permute-done.17.refs_1_ = bf16[8,16,1536]{2,1,0:T(8,128)(2,1)S(1)} collective-permute-done((bf16[8,16,1536]{2,1,0:T(8,128)(2,1)S(1)}, bf16[8,16,1536]{2,1,0:T(8,128)(2,1)S(1)}, u32[]{:S(2)}, u32[]{:S(2)}) %collective-permute-start.17) | collective-permute-done | bytes 393248 | tf_op jit(solution)/shard_map/ppermute | solution.py:305
  62.7 2.4 collective-permute-start.21
  65.1 4.5 %collective-permute-done.20.refs_1_ = bf16[2,72,1536]{2,1,0:T(8,128)(2,1)S(1)} collective-permute-done((bf16[2,72,1536]{2,1,0:T(8,128)(2,1)S(1)}, bf16[2,72,1536]{2,1,0:T(8,128)(2,1)S(1)}, u32[]{:S(2)}, u32[]{:S(2)}) %collective-permute-start.20) | collective-permute-done | bytes 442400 | tf_op jit(solution)/shard_map/ppermute | solution.py:305
  71.8 2.7 %collective-permute-done.19.refs_3_ = bf16[8,16,1536]{2,1,0:T(8,128)(2,1)S(1)} collective-permute-done((bf16[8,16,1536]{2,1,0:T(8,128)(2,1)S(1)}, bf16[8,16,1536]{2,1,0:T(8,128)(2,1)S(1)}, u32[]{:S(2)}, u32[]{:S(2)}) %collective-permute-start.19) | collective-permute-done | bytes 393248 | tf_op jit(solution)/shard_map/ppermute | solution.py:305
  75.5 6.3 %collective-permute-done.15.refs_2_ = bf16[8,16,1536]{2,1,0:T(8,128)(2,1)S(1)} collective-permute-done((bf16[8,16,1536]{2,1,0:T(8,128)(2,1)S(1)}, bf16[8,16,1536]{2,1,0:T(8,128)(2,1)S(1)}, u32[]{:S(2)}, u32[]{:S(2)}) %collective-permute-start.15) | collective-permute-done | bytes 393248 | tf_op jit(solution)/shard_map/ppermute | solution.py:309
  81.8 1.7 collective-permute-start.31
  84.5 3.3 %collective-permute-start.25 = (bf16[2,2,8,16,1536]{4,3,2,1,0:T(8,128)(2,1)S(1)}, bf16[2,2,8,16,1536]{4,3,2,1,0:T(8,128)(2,1)}, u32[]{:S(2)}, u32[]{:S(2)}) collective-permute-start(bf16[2,2,8,16,1536]{4,3,2,1,0:T(8,128)(2,1)S(1)} %bitcast.19), channel_id=1, source_target_pairs={{0,192},{1,65},{2,194},{3,67},{4,196},{5,69},{6,198},{7,71},{8,200... | collective-permute-start | bytes 4718600 | tf_op jit(solution)/shard_map/ppermute | solution.py:309
  88.7 19.6 %collective-permute-done.32.refs_18_ = bf16[4,8,16,1536]{3,2,1,0:T(8,128)(2,1)S(1)} collective-permute-done((bf16[4,8,16,1536]{3,2,1,0:T(8,128)(2,1)S(1)}, bf16[4,8,16,1536]{3,2,1,0:T(8,128)(2,1)S(1)}, u32[]{:S(2)}, u32[]{:S(2)}) %collective-permute-start.32) | collective-permute-done | bytes 1572896 | tf_op jit(solution)/shard_map/ppermute | solution.py:309
  108.8 3.5 %collective-permute-done.24.refs_9_ = bf16[2,2,8,16,1536]{4,3,2,1,0:T(8,128)(2,1)} collective-permute-done((bf16[2,2,8,16,1536]{4,3,2,1,0:T(8,128)(2,1)S(1)}, bf16[2,2,8,16,1536]{4,3,2,1,0:T(8,128)(2,1)}, u32[]{:S(2)}, u32[]{:S(2)}) %collective-permute-start.24) | collective-permute-done | bytes 1572896 | tf_op jit(solution)/shard_map/ppermute | solution.py:305
  117.1 17.2 %collective-permute-done.33.refs_19_ = bf16[4,8,16,1536]{3,2,1,0:T(8,128)(2,1)} collective-permute-done((bf16[4,8,16,1536]{3,2,1,0:T(8,128)(2,1)}, bf16[4,8,16,1536]{3,2,1,0:T(8,128)(2,1)}, u32[]{:S(2)}, u32[]{:S(2)}) %collective-permute-start.33) | collective-permute-done | bytes 1572896 | tf_op jit(solution)/shard_map/ppermute | solution.py:305
  140.3 58.6 %row_gradients.1 = (f32[8,16,48,128]{3,2,1,0:T(8,128)}, bf16[8,16,48,128]{3,2,1,0:T(8,128)(2,1)}) custom-call(s32[4]{0:T(128)} %copy-done.4, bf16[32,1536]{1,0:T(8,128)(2,1)} %get-tuple-element.54.refs_1_, bf16[32,1536]{1,0:T(8,128)(2,1)} %get-tuple-element.53.refs_2_, f32[32,1536]{1,0:T(8,128)} %fusion.refs_3_, f32[2,1536]{1,0:T(2,128)} %convolution_add_fusion.refs_4_, ...), custom_call_target="tpu_custom_call" | custom-call | tf_op jit(solution)/shard_map/row_gradients/pallas_call | solution.py:251
  199.1 3.5 %collective-permute-done.38 = bf16[8,16,48,128]{3,2,1,0:T(8,128)(2,1)S(1)} collective-permute-done((bf16[8,16,48,128]{3,2,1,0:T(8,128)(2,1)}, bf16[8,16,48,128]{3,2,1,0:T(8,128)(2,1)S(1)}, u32[]{:S(2)}, u32[]{:S(2)}) %collective-permute-start.38) | collective-permute-done | bytes 1572896 | tf_op jit(solution)/shard_map/ppermute | solution.py:297
  202.6 2.3 add_convert_fusion
  204.9 25.5 %all_to_all.10 = bf16[8,16,48,128]{3,2,1,0:T(8,128)(2,1)S(1)} all-to-all(bf16[8,16,48,128]{3,2,1,0:T(8,128)(2,1)S(1)} %add_convert_fusion), channel_id=1, replica_groups=mesh['section'=8,'dp'=32] {'section'}, dimensions={0} | all-to-all | bytes 3145728 | tf_op jit(solution)/shard_map/all_to_all | solution.py:383
  230.6 16.1 %all_to_all.11 = bf16[16,48,128]{2,1,0:T(8,128)(2,1)S(1)} all-to-all(bf16[16,48,128]{2,1,0:T(8,128)(2,1)S(1)} %reduce_sum.21), channel_id=1, replica_groups={{0,2,4,6,8,10,12,14,16,18,20,22,24,26,28,30},{1,3,5,7,9,11,13,15,17,19,..., dimensions={0} | all-to-all | bytes 393216 | tf_op jit(solution)/shard_map/all_to_all | solution.py:383
  (108 shorter events, 37.9 us)
Async XLA Ops:
  7.2 133.1 %all-gather.2.cloned.1.call-start = ((), (), s32[]{:S(2)}) async-start(), calls=%async_computation.2 | async-start | bytes 13369344 | tf_op jit(solution)/shard_map/all_gather | solution.py:364
  12.8 7.7 %collective-permute-start.2 = (bf16[32,1536]{1,0:T(8,128)(2,1)S(1)}, bf16[32,1536]{1,0:T(8,128)(2,1)S(1)}, u32[]{:S(2)}, u32[]{:S(2)}) collective-permute-start(bf16[32,1536]{1,0:T(8,128)(2,1)S(1)} %slice_bitcast_fusion.refs_0_), channel_id=1, source_target_pairs={{0,2},{1,15},{2,4},{3,1},{4,6},{5,3},{6,8},{7,5},{8,10},{9,7},{10,... | collective-permute-start | bytes 294920 | tf_op jit(solution)/shard_map/ppermute | solution.py:305
  27.5 12.8 %collective-permute-start.8 = (bf16[4,16,1536]{2,1,0:T(8,128)(2,1)S(1)}, bf16[4,16,1536]{2,1,0:T(8,128)(2,1)S(1)}, u32[]{:S(2)}, u32[]{:S(2)}) collective-permute-start(bf16[4,16,1536]{2,1,0:T(8,128)(2,1)S(1)} %in_line_y.2.refs_0_), channel_id=1, source_target_pairs={{0,192},{1,65},{2,194},{3,67},{4,196},{5,69},{6,198},{7,71},{8,200... | collective-permute-start | bytes 589832 | tf_op jit(solution)/shard_map/ppermute | solution.py:309
  30.4 10.0 %collective-permute-start.7 = (bf16[4,16,1536]{2,1,0:T(8,128)(2,1)S(1)}, bf16[4,16,1536]{2,1,0:T(8,128)(2,1)S(1)}, u32[]{:S(2)}, u32[]{:S(2)}) collective-permute-start(bf16[4,16,1536]{2,1,0:T(8,128)(2,1)S(1)} %in_line_y.2.refs_0_), channel_id=1, source_target_pairs={{0,64},{1,193},{2,66},{3,195},{4,68},{5,197},{6,70},{7,199},{8,72}... | collective-permute-start | bytes 589832 | tf_op jit(solution)/shard_map/ppermute | solution.py:305
  49.4 12.5 %collective-permute-start.17 = (bf16[8,16,1536]{2,1,0:T(8,128)(2,1)S(1)}, bf16[8,16,1536]{2,1,0:T(8,128)(2,1)S(1)}, u32[]{:S(2)}, u32[]{:S(2)}) collective-permute-start(bf16[8,16,1536]{2,1,0:T(8,128)(2,1)S(1)} %get-tuple-element.39.refs_0_), channel_id=1, source_target_pairs={{0,64},{1,193},{2,66},{3,195},{4,68},{5,197},{6,70},{7,199},{8,72}... | collective-permute-start | bytes 1179656 | tf_op jit(solution)/shard_map/ppermute | solution.py:305
  51.2 18.4 %collective-permute-start.20 = (bf16[2,72,1536]{2,1,0:T(8,128)(2,1)S(1)}, bf16[2,72,1536]{2,1,0:T(8,128)(2,1)S(1)}, u32[]{:S(2)}, u32[]{:S(2)}) collective-permute-start(bf16[2,72,1536]{2,1,0:T(8,128)(2,1)S(1)} %in_line_half.1.refs_0_), channel_id=1, source_target_pairs={{0,64},{1,193},{2,66},{3,195},{4,68},{5,197},{6,70},{7,199},{8,72}... | collective-permute-start | bytes 1327112 | tf_op jit(solution)/shard_map/ppermute | solution.py:305
  53.9 15.9 %collective-permute-start.14 = (bf16[8,16,1536]{2,1,0:T(8,128)(2,1)S(1)}, bf16[8,16,1536]{2,1,0:T(8,128)(2,1)S(1)}, u32[]{:S(2)}, u32[]{:S(2)}) collective-permute-start(bf16[8,16,1536]{2,1,0:T(8,128)(2,1)S(1)} %get-tuple-element.38.refs_0_), channel_id=1, source_target_pairs={{0,16},{1,49},{2,18},{3,51},{4,20},{5,53},{6,22},{7,55},{8,24},{9,... | collective-permute-start | bytes 1179656 | tf_op jit(solution)/shard_map/ppermute | solution.py:305
  55.5 15.1 %collective-permute-start.18 = (bf16[8,16,1536]{2,1,0:T(8,128)(2,1)S(1)}, bf16[8,16,1536]{2,1,0:T(8,128)(2,1)S(1)}, u32[]{:S(2)}, u32[]{:S(2)}) collective-permute-start(bf16[8,16,1536]{2,1,0:T(8,128)(2,1)S(1)} %get-tuple-element.39.refs_0_), channel_id=1, source_target_pairs={{0,192},{1,65},{2,194},{3,67},{4,196},{5,69},{6,198},{7,71},{8,200... | collective-permute-start | bytes 1179656 | tf_op jit(solution)/shard_map/ppermute | solution.py:309
  61.8 12.7 %collective-permute-start.19 = (bf16[8,16,1536]{2,1,0:T(8,128)(2,1)S(1)}, bf16[8,16,1536]{2,1,0:T(8,128)(2,1)S(1)}, u32[]{:S(2)}, u32[]{:S(2)}) collective-permute-start(bf16[8,16,1536]{2,1,0:T(8,128)(2,1)S(1)} %collective-permute-done.17.refs_1_), channel_id=1, source_target_pairs={{0,64},{1,193},{2,66},{3,195},{4,68},{5,197},{6,70},{7,199},{8,72}... | collective-permute-start | bytes 1179656 | tf_op jit(solution)/shard_map/ppermute | solution.py:305
  62.7 25.2 %collective-permute-start.21 = (bf16[2,72,1536]{2,1,0:T(8,128)(2,1)S(1)}, bf16[2,72,1536]{2,1,0:T(8,128)(2,1)S(1)}, u32[]{:S(2)}, u32[]{:S(2)}) collective-permute-start(bf16[2,72,1536]{2,1,0:T(8,128)(2,1)S(1)} %in_line_half.1.refs_0_), channel_id=1, source_target_pairs={{0,192},{1,65},{2,194},{3,67},{4,196},{5,69},{6,198},{7,71},{8,200... | collective-permute-start | bytes 1327112 | tf_op jit(solution)/shard_map/ppermute | solution.py:309
  69.6 18.3 %collective-permute-start.22 = (bf16[2,72,1536]{2,1,0:T(8,128)(2,1)S(1)}, bf16[2,72,1536]{2,1,0:T(8,128)(2,1)S(1)}, u32[]{:S(2)}, u32[]{:S(2)}) collective-permute-start(bf16[2,72,1536]{2,1,0:T(8,128)(2,1)S(1)} %collective-permute-done.20.refs_1_), channel_id=1, source_target_pairs={{0,64},{1,193},{2,66},{3,195},{4,68},{5,197},{6,70},{7,199},{8,72}... | collective-permute-start | bytes 1327112 | tf_op jit(solution)/shard_map/ppermute | solution.py:305
  69.8 12.1 %collective-permute-start.15 = (bf16[8,16,1536]{2,1,0:T(8,128)(2,1)S(1)}, bf16[8,16,1536]{2,1,0:T(8,128)(2,1)S(1)}, u32[]{:S(2)}, u32[]{:S(2)}) collective-permute-start(bf16[8,16,1536]{2,1,0:T(8,128)(2,1)S(1)} %get-tuple-element.38.refs_0_), channel_id=1, source_target_pairs={{0,48},{1,17},{2,50},{3,19},{4,52},{5,21},{6,54},{7,23},{8,56},{9,... | collective-permute-start | bytes 1179656 | tf_op jit(solution)/shard_map/ppermute | solution.py:309
  70.6 13.3 %collective-permute-start.16 = (bf16[8,16,1536]{2,1,0:T(8,128)(2,1)S(1)}, bf16[8,16,1536]{2,1,0:T(8,128)(2,1)S(1)}, u32[]{:S(2)}, u32[]{:S(2)}) collective-permute-start(bf16[8,16,1536]{2,1,0:T(8,128)(2,1)S(1)} %collective-permute-done.14.refs_1_), channel_id=1, source_target_pairs={{0,16},{1,49},{2,18},{3,51},{4,20},{5,53},{6,22},{7,55},{8,24},{9,... | collective-permute-start | bytes 1179656 | tf_op jit(solution)/shard_map/ppermute | solution.py:305
  75.2 33.1 %collective-permute-start.32 = (bf16[4,8,16,1536]{3,2,1,0:T(8,128)(2,1)S(1)}, bf16[4,8,16,1536]{3,2,1,0:T(8,128)(2,1)S(1)}, u32[]{:S(2)}, u32[]{:S(2)}) collective-permute-start(bf16[4,8,16,1536]{3,2,1,0:T(8,128)(2,1)S(1)} %in_line_x.3.refs_16_), channel_id=1, source_target_pairs={{0,48},{1,17},{2,50},{3,19},{4,52},{5,21},{6,54},{7,23},{8,56},{9,... | collective-permute-start | bytes 4718600 | tf_op jit(solution)/shard_map/ppermute | solution.py:309
  81.8 26.4 %collective-permute-start.31 = (bf16[4,8,16,1536]{3,2,1,0:T(8,128)(2,1)S(1)}, bf16[4,8,16,1536]{3,2,1,0:T(8,128)(2,1)}, u32[]{:S(2)}, u32[]{:S(2)}) collective-permute-start(bf16[4,8,16,1536]{3,2,1,0:T(8,128)(2,1)S(1)} %in_line_x.3.refs_16_), channel_id=1, source_target_pairs={{0,16},{1,49},{2,18},{3,51},{4,20},{5,53},{6,22},{7,55},{8,24},{9,... | collective-permute-start | bytes 4718600 | tf_op jit(solution)/shard_map/ppermute | solution.py:305
  84.5 24.2 %collective-permute-start.25 = (bf16[2,2,8,16,1536]{4,3,2,1,0:T(8,128)(2,1)S(1)}, bf16[2,2,8,16,1536]{4,3,2,1,0:T(8,128)(2,1)}, u32[]{:S(2)}, u32[]{:S(2)}) collective-permute-start(bf16[2,2,8,16,1536]{4,3,2,1,0:T(8,128)(2,1)S(1)} %bitcast.19), channel_id=1, source_target_pairs={{0,192},{1,65},{2,194},{3,67},{4,196},{5,69},{6,198},{7,71},{8,200... | collective-permute-start | bytes 4718600 | tf_op jit(solution)/shard_map/ppermute | solution.py:309
  87.9 24.5 %collective-permute-start.24 = (bf16[2,2,8,16,1536]{4,3,2,1,0:T(8,128)(2,1)S(1)}, bf16[2,2,8,16,1536]{4,3,2,1,0:T(8,128)(2,1)}, u32[]{:S(2)}, u32[]{:S(2)}) collective-permute-start(bf16[2,2,8,16,1536]{4,3,2,1,0:T(8,128)(2,1)S(1)} %bitcast.20), channel_id=1, source_target_pairs={{0,64},{1,193},{2,66},{3,195},{4,68},{5,197},{6,70},{7,199},{8,72}... | collective-permute-start | bytes 4718600 | tf_op jit(solution)/shard_map/ppermute | solution.py:305
  88.6 25.3 %collective-permute-start.27 = (bf16[2,2,8,16,1536]{4,3,2,1,0:T(8,128)(2,1)S(1)}, bf16[2,2,8,16,1536]{4,3,2,1,0:T(8,128)(2,1)S(1)}, u32[]{:S(2)}, u32[]{:S(2)}) collective-permute-start(bf16[2,2,8,16,1536]{4,3,2,1,0:T(8,128)(2,1)S(1)} %bitcast.21), channel_id=1, source_target_pairs={{0,1},{1,0},{2,3},{3,2},{4,5},{5,4},{6,7},{7,6},{8,9},{9,8},{10,11... | collective-permute-start | bytes 4718600 | tf_op jit(solution)/shard_map/ppermute | solution.py:297
  108.7 8.2 %collective-permute-start.36 = (bf16[4,8,16,1536]{3,2,1,0:T(8,128)(2,1)S(1)}, bf16[4,8,16,1536]{3,2,1,0:T(8,128)(2,1)S(1)}, u32[]{:S(2)}, u32[]{:S(2)}) collective-permute-start(bf16[4,8,16,1536]{3,2,1,0:T(8,128)(2,1)S(1)} %collective-permute-done.32.refs_18_), channel_id=1, source_target_pairs={{0,1},{1,0},{2,3},{3,2},{4,5},{5,4},{6,7},{7,6},{8,9},{9,8},{10,11... | collective-permute-start | bytes 4718600 | tf_op jit(solution)/shard_map/ppermute | solution.py:297
  112.4 21.9 %collective-permute-start.33 = (bf16[4,8,16,1536]{3,2,1,0:T(8,128)(2,1)}, bf16[4,8,16,1536]{3,2,1,0:T(8,128)(2,1)}, u32[]{:S(2)}, u32[]{:S(2)}) collective-permute-start(bf16[4,8,16,1536]{3,2,1,0:T(8,128)(2,1)} %collective-permute-done.31.refs_17_), channel_id=1, source_target_pairs={{0,16},{1,49},{2,18},{3,51},{4,20},{5,53},{6,22},{7,55},{8,24},{9,... | collective-permute-start | bytes 4718600 | tf_op jit(solution)/shard_map/ppermute | solution.py:305
  113.9 21.9 %collective-permute-start.26 = (bf16[2,2,8,16,1536]{4,3,2,1,0:T(8,128)(2,1)}, bf16[2,2,8,16,1536]{4,3,2,1,0:T(8,128)(2,1)}, u32[]{:S(2)}, u32[]{:S(2)}) collective-permute-start(bf16[2,2,8,16,1536]{4,3,2,1,0:T(8,128)(2,1)} %collective-permute-done.24.refs_9_), channel_id=1, source_target_pairs={{0,64},{1,193},{2,66},{3,195},{4,68},{5,197},{6,70},{7,199},{8,72}... | collective-permute-start | bytes 4718600 | tf_op jit(solution)/shard_map/ppermute | solution.py:305
  114.4 24.8 %collective-permute-start.35 = (bf16[4,8,16,1536]{3,2,1,0:T(8,128)(2,1)}, bf16[4,8,16,1536]{3,2,1,0:T(8,128)(2,1)}, u32[]{:S(2)}, u32[]{:S(2)}) collective-permute-start(bf16[4,8,16,1536]{3,2,1,0:T(8,128)(2,1)} %collective-permute-done.31.refs_17_), channel_id=1, source_target_pairs={{0,1},{1,0},{2,3},{3,2},{4,5},{5,4},{6,7},{7,6},{8,9},{9,8},{10,11... | collective-permute-start | bytes 4718600 | tf_op jit(solution)/shard_map/ppermute | solution.py:297
  115.9 23.3 %collective-permute-start.28 = (bf16[2,2,8,16,1536]{4,3,2,1,0:T(8,128)(2,1)}, bf16[2,2,8,16,1536]{4,3,2,1,0:T(8,128)(2,1)}, u32[]{:S(2)}, u32[]{:S(2)}) collective-permute-start(bf16[2,2,8,16,1536]{4,3,2,1,0:T(8,128)(2,1)} %collective-permute-done.24.refs_9_), channel_id=1, source_target_pairs={{0,1},{1,0},{2,3},{3,2},{4,5},{5,4},{6,7},{7,6},{8,9},{9,8},{10,11... | collective-permute-start | bytes 4718600 | tf_op jit(solution)/shard_map/ppermute | solution.py:297
  117.0 22.2 %collective-permute-start.29 = (bf16[2,2,8,16,1536]{4,3,2,1,0:T(8,128)(2,1)}, bf16[2,2,8,16,1536]{4,3,2,1,0:T(8,128)(2,1)}, u32[]{:S(2)}, u32[]{:S(2)}) collective-permute-start(bf16[2,2,8,16,1536]{4,3,2,1,0:T(8,128)(2,1)} %collective-permute-done.25.refs_10_), channel_id=1, source_target_pairs={{0,1},{1,0},{2,3},{3,2},{4,5},{5,4},{6,7},{7,6},{8,9},{9,8},{10,11... | collective-permute-start | bytes 4718600 | tf_op jit(solution)/shard_map/ppermute | solution.py:297
  (29 other events, 560.3 us)
Sparse Core Ops, SparseCore 0:
  48.9 76.2 all-gather.1

commit v4 on v3

--- a/solution.py
+++ b/solution.py
@@ -14,7 +14,6 @@
 EVERYWHERE = ("section", "dp")
 SIZES = {"x": 4, "y": 4, "z": 8}
 PART = 16
-CHUNK = 512
 F32 = jnp.float32
 BF16 = jnp.bfloat16
 
@@ -158,7 +157,7 @@
         inverse_store[slot] = inverse
         normed = (hf * inverse * scale_row(layer, step)).astype(BF16)
         low = dot_nt(normed, down).astype(BF16)
-        pre = dot_nn(normed, weight(layer)) + ADAPTER_SCALE * dot_nn(low, up)
+        pre = ADAPTER_SCALE * dot_nn(low, up) + dot_nn(normed, weight(layer))
         normed_store[slot] = normed
         low_store[slot] = low
         s = jax.nn.sigmoid(pre)
@@ -191,14 +190,7 @@
         down, up = adapter(layer)
         pre_grad = (cotangent * slope_store[slot]).astype(BF16)
         low_grad = (ADAPTER_SCALE * dot_nt(pre_grad, up)).astype(BF16)
-        w = weight(layer)
-        norm_grad = jnp.concatenate(
-            [
-                dot_nt(pre_grad, w[j : j + CHUNK]) + dot_nn(low_grad, down[:, j : j + CHUNK])
-                for j in range(0, width, CHUNK)
-            ],
-            axis=1,
-        )
+        norm_grad = dot_nn(low_grad, down) + dot_nt(pre_grad, weight(layer))
         hf = hidden_store[slot].astype(F32)
         inverse = inverse_store[slot]
         y = hf * inverse
@@ -227,7 +219,9 @@
         ):
             columns = term.reshape(-1, 2, keep_ref.shape[2], rank)
             here = core == 0
-            keep_ref[layer, :, :, first : first + rank] = jnp.where(here, columns[:, 0], columns[:, 1])
+            keep_ref[layer, :, :, first : first + rank] = jnp.where(
+                here, columns[:, 0], columns[:, 1]
+            ).astype(BF16)
             send_ref[layer, :, :, first : first + rank] = jnp.where(
                 here, columns[:, 1], columns[:, 0]
             ).astype(BF16)
@@ -250,7 +244,7 @@
 
     return pl.pallas_call(
         body,
-        out_shape=(jax.ShapeDtypeStruct(half, F32), jax.ShapeDtypeStruct(half, BF16)),
+        out_shape=(jax.ShapeDtypeStruct(half, BF16), jax.ShapeDtypeStruct(half, BF16)),
         in_specs=[pl.BlockSpec(memory_space=pltpu.SMEM)] + [vmem] * 4 + [hbm] * (3 + len(pieces)),
         out_specs=(vmem, vmem),
         scratch_shapes=[
@@ -370,8 +364,7 @@
     side = in_line(ring_blocks(in_line([side, half], place, "half")[0], "x"), place, "x")[0]
     a1, b1 = onwards(a, "x"), onwards(b, "y")
     a2, b2 = back(a, "x"), back(b, "y")
-    small = onwards(a[0, 0, 0], "x")
-    a0, b0, side, _ = together(a, b, side, small)
+    a0, b0, side = together(a, b, side)
     a3, b3 = onwards(a1, "x"), onwards(b1, "y")
     pieces = []
     for mine in ([a0, a1, a2, a3], [b0, b1, b2, b3]):
@@ -442,7 +435,7 @@
         width // dp_size,
         scale_factor,
     )
-    on_chip = (keep + other_core(send).astype(F32)).astype(BF16)
+    on_chip = (keep.astype(F32) + other_core(send).astype(F32)).astype(BF16)
     over_sections = exchange_and_add(on_chip, "section")
     same_core = [[i for i in range(32) if i % 2 == core] for core in range(2)]
     summed = exchange_and_add(over_sections.astype(BF16), "dp", same_core)

time: 255 us -> 252 us (0.988)
  no operation moved by 1% of the time
where the time goes in v4:
time: 252 us
  waiting for transfers between devices  83.7 us (33%)
  Pallas kernels  61.8 us (25%)
  blocking collectives  41.7 us (17%)
  starting transfers between devices  39.3 us (16%)
  between operations  14.3 us (6%)
  local copies, waits for them, and re-layouts  5.64 us (2%)
  other arithmetic  3.82 us (2%)
    pallas_call x1, Pallas kernels, row_gradients(): pl.pallas_call(body, out_shape=(jax.ShapeDtypeStruct(half, BF16), jax.Sha...  56.6 us
    ppermute x19, waiting for transfers between devices, onwards(): return lax.ppermute(block, EVERYWHERE, route(axis, 1))  51.5 us
    all_to_all x2, blocking collectives, exchange_and_add(): lax.all_to_all(parts, axis, 0, 0, axis_index_groups=groups, tiled=True)  41.7 us
    ppermute x10, waiting for transfers between devices, back(): return lax.ppermute(block, EVERYWHERE, route(axis, -1))  26.9 us
    ppermute x10, starting transfers between devices, back(): return lax.ppermute(block, EVERYWHERE, route(axis, -1))  20.9 us
    ppermute x19, starting transfers between devices, onwards(): return lax.ppermute(block, EVERYWHERE, route(axis, 1))  16.7 us
    ppermute x10, waiting for transfers between devices, other_core(): return lax.ppermute(block, EVERYWHERE, pairs)  5.32 us
    pallas_call x7, Pallas kernels, in_line(): pl.pallas_call(body, out_shape=out_shape, in_specs=[pl.BlockSpec(memory_s...  5.19 us
  transfers between devices with their start and end apart: 40, of which 22 were waited for; matrix products, arithmetic and copies ran while one was open for 2% of the time, Pallas kernels for 1%

profile of v4, /device:TPU:32, one launch (start us, length us, event | category | flops | bytes accessed | tf_op | source)
XLA Modules:
  0.0 252.0 jit_solution(15303915829378526808)
XLA Ops:
  8.1 3.0 %collective-permute-start.1 = (bf16[16,1536]{1,0:T(8,128)(2,1)S(1)}, bf16[16,1536]{1,0:T(8,128)(2,1)S(1)}, u32[]{:S(2)}, u32[]{:S(2)}) collective-permute-start(bf16[16,1536]{1,0:T(8,128)(2,1)S(1)} %slice_bitcast_fusion.1.refs_0_), channel_id=1, source_target_pairs={{0,48},{1,17},{2,50},{3,19},{4,52},{5,21},{6,54},{7,23},{8,56},{9,... | collective-permute-start | bytes 147464 | tf_op jit(solution)/shard_map/ppermute | solution.py:303
  17.3 3.2 %collective-permute-done.2.refs_1_ = bf16[32,1536]{1,0:T(8,128)(2,1)S(1)} collective-permute-done((bf16[32,1536]{1,0:T(8,128)(2,1)S(1)}, bf16[32,1536]{1,0:T(8,128)(2,1)S(1)}, u32[]{:S(2)}, u32[]{:S(2)}) %collective-permute-start.2) | collective-permute-done | bytes 98336 | tf_op jit(solution)/shard_map/ppermute | solution.py:299
  21.1 3.2 %collective-permute-start.6 = (bf16[32,1536]{1,0:T(8,128)(2,1)S(1)}, bf16[32,1536]{1,0:T(8,128)(2,1)S(1)}, u32[]{:S(2)}, u32[]{:S(2)}) collective-permute-start(bf16[32,1536]{1,0:T(8,128)(2,1)S(1)} %collective-permute-done.3.refs_2_), channel_id=1, source_target_pairs={{0,14},{1,3},{2,0},{3,5},{4,2},{5,7},{6,4},{7,9},{8,6},{9,11},{10,... | collective-permute-start | bytes 294920 | tf_op jit(solution)/shard_map/ppermute | solution.py:303
  27.5 2.8 %collective-permute-start.8 = (bf16[4,16,1536]{2,1,0:T(8,128)(2,1)S(1)}, bf16[4,16,1536]{2,1,0:T(8,128)(2,1)S(1)}, u32[]{:S(2)}, u32[]{:S(2)}) collective-permute-start(bf16[4,16,1536]{2,1,0:T(8,128)(2,1)S(1)} %in_line_y.2.refs_0_), channel_id=1, source_target_pairs={{0,192},{1,65},{2,194},{3,67},{4,196},{5,69},{6,198},{7,71},{8,200... | collective-permute-start | bytes 589832 | tf_op jit(solution)/shard_map/ppermute | solution.py:303
  31.2 3.3 %collective-permute-start.10 = (bf16[32,1536]{1,0:T(8,128)(2,1)S(1)}, bf16[32,1536]{1,0:T(8,128)(2,1)S(1)}, u32[]{:S(2)}, u32[]{:S(2)}) collective-permute-start(bf16[32,1536]{1,0:T(8,128)(2,1)S(1)} %collective-permute-done.6.refs_4_), channel_id=1, source_target_pairs={{0,14},{1,3},{2,0},{3,5},{4,2},{5,7},{6,4},{7,9},{8,6},{9,11},{10,... | collective-permute-start | bytes 294920 | tf_op jit(solution)/shard_map/ppermute | solution.py:303
  34.5 2.7 %collective-permute-start.13 = (bf16[72,1536]{1,0:T(8,128)(2,1)S(1)}, bf16[72,1536]{1,0:T(8,128)(2,1)S(1)}, u32[]{:S(2)}, u32[]{:S(2)}) collective-permute-start(bf16[72,1536]{1,0:T(8,128)(2,1)S(1)} %concatenate.6.refs_0_), channel_id=1, source_target_pairs={{0,48},{1,49},{2,50},{3,51},{4,52},{5,53},{6,54},{7,55},{8,56},{9,... | collective-permute-start | bytes 663560 | tf_op jit(solution)/shard_map/ppermute | solution.py:299
  37.2 3.2 %collective-permute-done.9.refs_5_ = bf16[32,1536]{1,0:T(8,128)(2,1)S(1)} collective-permute-done((bf16[32,1536]{1,0:T(8,128)(2,1)S(1)}, bf16[32,1536]{1,0:T(8,128)(2,1)S(1)}, u32[]{:S(2)}, u32[]{:S(2)}) %collective-permute-start.9) | collective-permute-done | bytes 98336 | tf_op jit(solution)/shard_map/ppermute | solution.py:299
  41.7 5.3 %collective-permute-done.12.refs_7_ = bf16[32,1536]{1,0:T(8,128)(2,1)S(1)} collective-permute-done((bf16[32,1536]{1,0:T(8,128)(2,1)S(1)}, bf16[32,1536]{1,0:T(8,128)(2,1)S(1)}, u32[]{:S(2)}, u32[]{:S(2)}) %collective-permute-start.12) | collective-permute-done | bytes 98336 | tf_op jit(solution)/shard_map/ppermute | solution.py:299
  51.2 2.7 %collective-permute-start.20 = (bf16[2,72,1536]{2,1,0:T(8,128)(2,1)S(1)}, bf16[2,72,1536]{2,1,0:T(8,128)(2,1)S(1)}, u32[]{:S(2)}, u32[]{:S(2)}) collective-permute-start(bf16[2,72,1536]{2,1,0:T(8,128)(2,1)S(1)} %in_line_half.1.refs_0_), channel_id=1, source_target_pairs={{0,64},{1,193},{2,66},{3,195},{4,68},{5,197},{6,70},{7,199},{8,72}... | collective-permute-start | bytes 1327112 | tf_op jit(solution)/shard_map/ppermute | solution.py:299
  56.3 5.5 %collective-permute-done.17.refs_1_ = bf16[8,16,1536]{2,1,0:T(8,128)(2,1)S(1)} collective-permute-done((bf16[8,16,1536]{2,1,0:T(8,128)(2,1)S(1)}, bf16[8,16,1536]{2,1,0:T(8,128)(2,1)S(1)}, u32[]{:S(2)}, u32[]{:S(2)}) %collective-permute-start.17) | collective-permute-done | bytes 393248 | tf_op jit(solution)/shard_map/ppermute | solution.py:299
  62.7 2.4 collective-permute-start.21
  65.1 4.5 %collective-permute-done.20.refs_1_ = bf16[2,72,1536]{2,1,0:T(8,128)(2,1)S(1)} collective-permute-done((bf16[2,72,1536]{2,1,0:T(8,128)(2,1)S(1)}, bf16[2,72,1536]{2,1,0:T(8,128)(2,1)S(1)}, u32[]{:S(2)}, u32[]{:S(2)}) %collective-permute-start.20) | collective-permute-done | bytes 442400 | tf_op jit(solution)/shard_map/ppermute | solution.py:299
  71.8 2.7 %collective-permute-done.19.refs_3_ = bf16[8,16,1536]{2,1,0:T(8,128)(2,1)S(1)} collective-permute-done((bf16[8,16,1536]{2,1,0:T(8,128)(2,1)S(1)}, bf16[8,16,1536]{2,1,0:T(8,128)(2,1)S(1)}, u32[]{:S(2)}, u32[]{:S(2)}) %collective-permute-start.19) | collective-permute-done | bytes 393248 | tf_op jit(solution)/shard_map/ppermute | solution.py:299
  75.5 6.3 %collective-permute-done.15.refs_2_ = bf16[8,16,1536]{2,1,0:T(8,128)(2,1)S(1)} collective-permute-done((bf16[8,16,1536]{2,1,0:T(8,128)(2,1)S(1)}, bf16[8,16,1536]{2,1,0:T(8,128)(2,1)S(1)}, u32[]{:S(2)}, u32[]{:S(2)}) %collective-permute-start.15) | collective-permute-done | bytes 393248 | tf_op jit(solution)/shard_map/ppermute | solution.py:303
  81.9 1.7 collective-permute-start.31
  84.5 3.3 %collective-permute-start.25 = (bf16[2,2,8,16,1536]{4,3,2,1,0:T(8,128)(2,1)S(1)}, bf16[2,2,8,16,1536]{4,3,2,1,0:T(8,128)(2,1)}, u32[]{:S(2)}, u32[]{:S(2)}) collective-permute-start(bf16[2,2,8,16,1536]{4,3,2,1,0:T(8,128)(2,1)S(1)} %bitcast.19), channel_id=1, source_target_pairs={{0,192},{1,65},{2,194},{3,67},{4,196},{5,69},{6,198},{7,71},{8,200... | collective-permute-start | bytes 4718600 | tf_op jit(solution)/shard_map/ppermute | solution.py:303
  88.7 19.6 %collective-permute-done.32.refs_18_ = bf16[4,8,16,1536]{3,2,1,0:T(8,128)(2,1)S(1)} collective-permute-done((bf16[4,8,16,1536]{3,2,1,0:T(8,128)(2,1)S(1)}, bf16[4,8,16,1536]{3,2,1,0:T(8,128)(2,1)S(1)}, u32[]{:S(2)}, u32[]{:S(2)}) %collective-permute-start.32) | collective-permute-done | bytes 1572896 | tf_op jit(solution)/shard_map/ppermute | solution.py:303
  108.8 3.5 %collective-permute-done.24.refs_9_ = bf16[2,2,8,16,1536]{4,3,2,1,0:T(8,128)(2,1)} collective-permute-done((bf16[2,2,8,16,1536]{4,3,2,1,0:T(8,128)(2,1)S(1)}, bf16[2,2,8,16,1536]{4,3,2,1,0:T(8,128)(2,1)}, u32[]{:S(2)}, u32[]{:S(2)}) %collective-permute-start.24) | collective-permute-done | bytes 1572896 | tf_op jit(solution)/shard_map/ppermute | solution.py:299
  117.1 17.2 %collective-permute-done.33.refs_19_ = bf16[4,8,16,1536]{3,2,1,0:T(8,128)(2,1)} collective-permute-done((bf16[4,8,16,1536]{3,2,1,0:T(8,128)(2,1)}, bf16[4,8,16,1536]{3,2,1,0:T(8,128)(2,1)}, u32[]{:S(2)}, u32[]{:S(2)}) %collective-permute-start.33) | collective-permute-done | bytes 1572896 | tf_op jit(solution)/shard_map/ppermute | solution.py:299
  140.3 56.6 %row_gradients.1 = (bf16[8,16,48,128]{3,2,1,0:T(8,128)(2,1)}, bf16[8,16,48,128]{3,2,1,0:T(8,128)(2,1)}) custom-call(s32[4]{0:T(128)} %copy-done.4, bf16[32,1536]{1,0:T(8,128)(2,1)} %get-tuple-element.54.refs_1_, bf16[32,1536]{1,0:T(8,128)(2,1)} %get-tuple-element.53.refs_2_, f32[32,1536]{1,0:T(8,128)} %fusion.refs_3_, ...), custom_call_target="tpu_custom_call" | custom-call | tf_op jit(solution)/shard_map/row_gradients/pallas_call | solution.py:245
  197.2 3.5 %collective-permute-done.38 = bf16[8,16,48,128]{3,2,1,0:T(8,128)(2,1)S(1)} collective-permute-done((bf16[8,16,48,128]{3,2,1,0:T(8,128)(2,1)}, bf16[8,16,48,128]{3,2,1,0:T(8,128)(2,1)S(1)}, u32[]{:S(2)}, u32[]{:S(2)}) %collective-permute-start.38) | collective-permute-done | bytes 1572896 | tf_op jit(solution)/shard_map/ppermute | solution.py:291
  200.7 1.8 add_convert_fusion
  202.5 25.5 %all_to_all.10 = bf16[8,16,48,128]{3,2,1,0:T(8,128)(2,1)S(1)} all-to-all(bf16[8,16,48,128]{3,2,1,0:T(8,128)(2,1)S(1)} %add_convert_fusion), channel_id=1, replica_groups=mesh['section'=8,'dp'=32] {'section'}, dimensions={0} | all-to-all | bytes 3145728 | tf_op jit(solution)/shard_map/all_to_all | solution.py:376
  228.2 16.1 %all_to_all.11 = bf16[16,48,128]{2,1,0:T(8,128)(2,1)S(1)} all-to-all(bf16[16,48,128]{2,1,0:T(8,128)(2,1)S(1)} %reduce_sum.21), channel_id=1, replica_groups={{0,2,4,6,8,10,12,14,16,18,20,22,24,26,28,30},{1,3,5,7,9,11,13,15,17,19,..., dimensions={0} | all-to-all | bytes 393216 | tf_op jit(solution)/shard_map/all_to_all | solution.py:376
  (108 shorter events, 38.0 us)
Async XLA Ops:
  7.2 133.1 %all-gather.2.cloned.1.call-start = ((), (), s32[]{:S(2)}) async-start(), calls=%async_computation.2 | async-start | bytes 13369344 | tf_op jit(solution)/shard_map/all_gather | solution.py:358
  12.8 7.7 %collective-permute-start.2 = (bf16[32,1536]{1,0:T(8,128)(2,1)S(1)}, bf16[32,1536]{1,0:T(8,128)(2,1)S(1)}, u32[]{:S(2)}, u32[]{:S(2)}) collective-permute-start(bf16[32,1536]{1,0:T(8,128)(2,1)S(1)} %slice_bitcast_fusion.refs_0_), channel_id=1, source_target_pairs={{0,2},{1,15},{2,4},{3,1},{4,6},{5,3},{6,8},{7,5},{8,10},{9,7},{10,... | collective-permute-start | bytes 294920 | tf_op jit(solution)/shard_map/ppermute | solution.py:299
  27.5 12.8 %collective-permute-start.8 = (bf16[4,16,1536]{2,1,0:T(8,128)(2,1)S(1)}, bf16[4,16,1536]{2,1,0:T(8,128)(2,1)S(1)}, u32[]{:S(2)}, u32[]{:S(2)}) collective-permute-start(bf16[4,16,1536]{2,1,0:T(8,128)(2,1)S(1)} %in_line_y.2.refs_0_), channel_id=1, source_target_pairs={{0,192},{1,65},{2,194},{3,67},{4,196},{5,69},{6,198},{7,71},{8,200... | collective-permute-start | bytes 589832 | tf_op jit(solution)/shard_map/ppermute | solution.py:303
  30.4 10.0 %collective-permute-start.7 = (bf16[4,16,1536]{2,1,0:T(8,128)(2,1)S(1)}, bf16[4,16,1536]{2,1,0:T(8,128)(2,1)S(1)}, u32[]{:S(2)}, u32[]{:S(2)}) collective-permute-start(bf16[4,16,1536]{2,1,0:T(8,128)(2,1)S(1)} %in_line_y.2.refs_0_), channel_id=1, source_target_pairs={{0,64},{1,193},{2,66},{3,195},{4,68},{5,197},{6,70},{7,199},{8,72}... | collective-permute-start | bytes 589832 | tf_op jit(solution)/shard_map/ppermute | solution.py:299
  49.4 12.5 %collective-permute-start.17 = (bf16[8,16,1536]{2,1,0:T(8,128)(2,1)S(1)}, bf16[8,16,1536]{2,1,0:T(8,128)(2,1)S(1)}, u32[]{:S(2)}, u32[]{:S(2)}) collective-permute-start(bf16[8,16,1536]{2,1,0:T(8,128)(2,1)S(1)} %get-tuple-element.39.refs_0_), channel_id=1, source_target_pairs={{0,64},{1,193},{2,66},{3,195},{4,68},{5,197},{6,70},{7,199},{8,72}... | collective-permute-start | bytes 1179656 | tf_op jit(solution)/shard_map/ppermute | solution.py:299
  51.2 18.4 %collective-permute-start.20 = (bf16[2,72,1536]{2,1,0:T(8,128)(2,1)S(1)}, bf16[2,72,1536]{2,1,0:T(8,128)(2,1)S(1)}, u32[]{:S(2)}, u32[]{:S(2)}) collective-permute-start(bf16[2,72,1536]{2,1,0:T(8,128)(2,1)S(1)} %in_line_half.1.refs_0_), channel_id=1, source_target_pairs={{0,64},{1,193},{2,66},{3,195},{4,68},{5,197},{6,70},{7,199},{8,72}... | collective-permute-start | bytes 1327112 | tf_op jit(solution)/shard_map/ppermute | solution.py:299
  53.9 15.9 %collective-permute-start.14 = (bf16[8,16,1536]{2,1,0:T(8,128)(2,1)S(1)}, bf16[8,16,1536]{2,1,0:T(8,128)(2,1)S(1)}, u32[]{:S(2)}, u32[]{:S(2)}) collective-permute-start(bf16[8,16,1536]{2,1,0:T(8,128)(2,1)S(1)} %get-tuple-element.38.refs_0_), channel_id=1, source_target_pairs={{0,16},{1,49},{2,18},{3,51},{4,20},{5,53},{6,22},{7,55},{8,24},{9,... | collective-permute-start | bytes 1179656 | tf_op jit(solution)/shard_map/ppermute | solution.py:299
  55.5 15.1 %collective-permute-start.18 = (bf16[8,16,1536]{2,1,0:T(8,128)(2,1)S(1)}, bf16[8,16,1536]{2,1,0:T(8,128)(2,1)S(1)}, u32[]{:S(2)}, u32[]{:S(2)}) collective-permute-start(bf16[8,16,1536]{2,1,0:T(8,128)(2,1)S(1)} %get-tuple-element.39.refs_0_), channel_id=1, source_target_pairs={{0,192},{1,65},{2,194},{3,67},{4,196},{5,69},{6,198},{7,71},{8,200... | collective-permute-start | bytes 1179656 | tf_op jit(solution)/shard_map/ppermute | solution.py:303
  61.8 12.7 %collective-permute-start.19 = (bf16[8,16,1536]{2,1,0:T(8,128)(2,1)S(1)}, bf16[8,16,1536]{2,1,0:T(8,128)(2,1)S(1)}, u32[]{:S(2)}, u32[]{:S(2)}) collective-permute-start(bf16[8,16,1536]{2,1,0:T(8,128)(2,1)S(1)} %collective-permute-done.17.refs_1_), channel_id=1, source_target_pairs={{0,64},{1,193},{2,66},{3,195},{4,68},{5,197},{6,70},{7,199},{8,72}... | collective-permute-start | bytes 1179656 | tf_op jit(solution)/shard_map/ppermute | solution.py:299
  62.7 25.2 %collective-permute-start.21 = (bf16[2,72,1536]{2,1,0:T(8,128)(2,1)S(1)}, bf16[2,72,1536]{2,1,0:T(8,128)(2,1)S(1)}, u32[]{:S(2)}, u32[]{:S(2)}) collective-permute-start(bf16[2,72,1536]{2,1,0:T(8,128)(2,1)S(1)} %in_line_half.1.refs_0_), channel_id=1, source_target_pairs={{0,192},{1,65},{2,194},{3,67},{4,196},{5,69},{6,198},{7,71},{8,200... | collective-permute-start | bytes 1327112 | tf_op jit(solution)/shard_map/ppermute | solution.py:303
  69.6 18.3 %collective-permute-start.22 = (bf16[2,72,1536]{2,1,0:T(8,128)(2,1)S(1)}, bf16[2,72,1536]{2,1,0:T(8,128)(2,1)S(1)}, u32[]{:S(2)}, u32[]{:S(2)}) collective-permute-start(bf16[2,72,1536]{2,1,0:T(8,128)(2,1)S(1)} %collective-permute-done.20.refs_1_), channel_id=1, source_target_pairs={{0,64},{1,193},{2,66},{3,195},{4,68},{5,197},{6,70},{7,199},{8,72}... | collective-permute-start | bytes 1327112 | tf_op jit(solution)/shard_map/ppermute | solution.py:299
  69.8 12.1 %collective-permute-start.15 = (bf16[8,16,1536]{2,1,0:T(8,128)(2,1)S(1)}, bf16[8,16,1536]{2,1,0:T(8,128)(2,1)S(1)}, u32[]{:S(2)}, u32[]{:S(2)}) collective-permute-start(bf16[8,16,1536]{2,1,0:T(8,128)(2,1)S(1)} %get-tuple-element.38.refs_0_), channel_id=1, source_target_pairs={{0,48},{1,17},{2,50},{3,19},{4,52},{5,21},{6,54},{7,23},{8,56},{9,... | collective-permute-start | bytes 1179656 | tf_op jit(solution)/shard_map/ppermute | solution.py:303
  70.6 13.3 %collective-permute-start.16 = (bf16[8,16,1536]{2,1,0:T(8,128)(2,1)S(1)}, bf16[8,16,1536]{2,1,0:T(8,128)(2,1)S(1)}, u32[]{:S(2)}, u32[]{:S(2)}) collective-permute-start(bf16[8,16,1536]{2,1,0:T(8,128)(2,1)S(1)} %collective-permute-done.14.refs_1_), channel_id=1, source_target_pairs={{0,16},{1,49},{2,18},{3,51},{4,20},{5,53},{6,22},{7,55},{8,24},{9,... | collective-permute-start | bytes 1179656 | tf_op jit(solution)/shard_map/ppermute | solution.py:299
  75.2 33.1 %collective-permute-start.32 = (bf16[4,8,16,1536]{3,2,1,0:T(8,128)(2,1)S(1)}, bf16[4,8,16,1536]{3,2,1,0:T(8,128)(2,1)S(1)}, u32[]{:S(2)}, u32[]{:S(2)}) collective-permute-start(bf16[4,8,16,1536]{3,2,1,0:T(8,128)(2,1)S(1)} %in_line_x.3.refs_16_), channel_id=1, source_target_pairs={{0,48},{1,17},{2,50},{3,19},{4,52},{5,21},{6,54},{7,23},{8,56},{9,... | collective-permute-start | bytes 4718600 | tf_op jit(solution)/shard_map/ppermute | solution.py:303
  81.9 26.4 %collective-permute-start.31 = (bf16[4,8,16,1536]{3,2,1,0:T(8,128)(2,1)S(1)}, bf16[4,8,16,1536]{3,2,1,0:T(8,128)(2,1)}, u32[]{:S(2)}, u32[]{:S(2)}) collective-permute-start(bf16[4,8,16,1536]{3,2,1,0:T(8,128)(2,1)S(1)} %in_line_x.3.refs_16_), channel_id=1, source_target_pairs={{0,16},{1,49},{2,18},{3,51},{4,20},{5,53},{6,22},{7,55},{8,24},{9,... | collective-permute-start | bytes 4718600 | tf_op jit(solution)/shard_map/ppermute | solution.py:299
  84.5 24.2 %collective-permute-start.25 = (bf16[2,2,8,16,1536]{4,3,2,1,0:T(8,128)(2,1)S(1)}, bf16[2,2,8,16,1536]{4,3,2,1,0:T(8,128)(2,1)}, u32[]{:S(2)}, u32[]{:S(2)}) collective-permute-start(bf16[2,2,8,16,1536]{4,3,2,1,0:T(8,128)(2,1)S(1)} %bitcast.19), channel_id=1, source_target_pairs={{0,192},{1,65},{2,194},{3,67},{4,196},{5,69},{6,198},{7,71},{8,200... | collective-permute-start | bytes 4718600 | tf_op jit(solution)/shard_map/ppermute | solution.py:303
  87.9 24.5 %collective-permute-start.24 = (bf16[2,2,8,16,1536]{4,3,2,1,0:T(8,128)(2,1)S(1)}, bf16[2,2,8,16,1536]{4,3,2,1,0:T(8,128)(2,1)}, u32[]{:S(2)}, u32[]{:S(2)}) collective-permute-start(bf16[2,2,8,16,1536]{4,3,2,1,0:T(8,128)(2,1)S(1)} %bitcast.20), channel_id=1, source_target_pairs={{0,64},{1,193},{2,66},{3,195},{4,68},{5,197},{6,70},{7,199},{8,72}... | collective-permute-start | bytes 4718600 | tf_op jit(solution)/shard_map/ppermute | solution.py:299
  88.6 25.3 %collective-permute-start.27 = (bf16[2,2,8,16,1536]{4,3,2,1,0:T(8,128)(2,1)S(1)}, bf16[2,2,8,16,1536]{4,3,2,1,0:T(8,128)(2,1)S(1)}, u32[]{:S(2)}, u32[]{:S(2)}) collective-permute-start(bf16[2,2,8,16,1536]{4,3,2,1,0:T(8,128)(2,1)S(1)} %bitcast.21), channel_id=1, source_target_pairs={{0,1},{1,0},{2,3},{3,2},{4,5},{5,4},{6,7},{7,6},{8,9},{9,8},{10,11... | collective-permute-start | bytes 4718600 | tf_op jit(solution)/shard_map/ppermute | solution.py:291
  108.7 8.2 %collective-permute-start.36 = (bf16[4,8,16,1536]{3,2,1,0:T(8,128)(2,1)S(1)}, bf16[4,8,16,1536]{3,2,1,0:T(8,128)(2,1)S(1)}, u32[]{:S(2)}, u32[]{:S(2)}) collective-permute-start(bf16[4,8,16,1536]{3,2,1,0:T(8,128)(2,1)S(1)} %collective-permute-done.32.refs_18_), channel_id=1, source_target_pairs={{0,1},{1,0},{2,3},{3,2},{4,5},{5,4},{6,7},{7,6},{8,9},{9,8},{10,11... | collective-permute-start | bytes 4718600 | tf_op jit(solution)/shard_map/ppermute | solution.py:291
  112.4 21.9 %collective-permute-start.33 = (bf16[4,8,16,1536]{3,2,1,0:T(8,128)(2,1)}, bf16[4,8,16,1536]{3,2,1,0:T(8,128)(2,1)}, u32[]{:S(2)}, u32[]{:S(2)}) collective-permute-start(bf16[4,8,16,1536]{3,2,1,0:T(8,128)(2,1)} %collective-permute-done.31.refs_17_), channel_id=1, source_target_pairs={{0,16},{1,49},{2,18},{3,51},{4,20},{5,53},{6,22},{7,55},{8,24},{9,... | collective-permute-start | bytes 4718600 | tf_op jit(solution)/shard_map/ppermute | solution.py:299
  113.9 21.9 %collective-permute-start.26 = (bf16[2,2,8,16,1536]{4,3,2,1,0:T(8,128)(2,1)}, bf16[2,2,8,16,1536]{4,3,2,1,0:T(8,128)(2,1)}, u32[]{:S(2)}, u32[]{:S(2)}) collective-permute-start(bf16[2,2,8,16,1536]{4,3,2,1,0:T(8,128)(2,1)} %collective-permute-done.24.refs_9_), channel_id=1, source_target_pairs={{0,64},{1,193},{2,66},{3,195},{4,68},{5,197},{6,70},{7,199},{8,72}... | collective-permute-start | bytes 4718600 | tf_op jit(solution)/shard_map/ppermute | solution.py:299
  114.4 24.8 %collective-permute-start.35 = (bf16[4,8,16,1536]{3,2,1,0:T(8,128)(2,1)}, bf16[4,8,16,1536]{3,2,1,0:T(8,128)(2,1)}, u32[]{:S(2)}, u32[]{:S(2)}) collective-permute-start(bf16[4,8,16,1536]{3,2,1,0:T(8,128)(2,1)} %collective-permute-done.31.refs_17_), channel_id=1, source_target_pairs={{0,1},{1,0},{2,3},{3,2},{4,5},{5,4},{6,7},{7,6},{8,9},{9,8},{10,11... | collective-permute-start | bytes 4718600 | tf_op jit(solution)/shard_map/ppermute | solution.py:291
  115.9 23.3 %collective-permute-start.28 = (bf16[2,2,8,16,1536]{4,3,2,1,0:T(8,128)(2,1)}, bf16[2,2,8,16,1536]{4,3,2,1,0:T(8,128)(2,1)}, u32[]{:S(2)}, u32[]{:S(2)}) collective-permute-start(bf16[2,2,8,16,1536]{4,3,2,1,0:T(8,128)(2,1)} %collective-permute-done.24.refs_9_), channel_id=1, source_target_pairs={{0,1},{1,0},{2,3},{3,2},{4,5},{5,4},{6,7},{7,6},{8,9},{9,8},{10,11... | collective-permute-start | bytes 4718600 | tf_op jit(solution)/shard_map/ppermute | solution.py:291
  117.0 22.3 %collective-permute-start.29 = (bf16[2,2,8,16,1536]{4,3,2,1,0:T(8,128)(2,1)}, bf16[2,2,8,16,1536]{4,3,2,1,0:T(8,128)(2,1)}, u32[]{:S(2)}, u32[]{:S(2)}) collective-permute-start(bf16[2,2,8,16,1536]{4,3,2,1,0:T(8,128)(2,1)} %collective-permute-done.25.refs_10_), channel_id=1, source_target_pairs={{0,1},{1,0},{2,3},{3,2},{4,5},{5,4},{6,7},{7,6},{8,9},{9,8},{10,11... | collective-permute-start | bytes 4718600 | tf_op jit(solution)/shard_map/ppermute | solution.py:291
  (29 other events, 560.4 us)
Sparse Core Ops, SparseCore 0:
  48.9 76.2 all-gather.1

commit v5 on v4

--- a/solution.py
+++ b/solution.py
@@ -364,10 +364,9 @@
     side = in_line(ring_blocks(in_line([side, half], place, "half")[0], "x"), place, "x")[0]
     a1, b1 = onwards(a, "x"), onwards(b, "y")
     a2, b2 = back(a, "x"), back(b, "y")
-    a0, b0, side = together(a, b, side)
     a3, b3 = onwards(a1, "x"), onwards(b1, "y")
     pieces = []
-    for mine in ([a0, a1, a2, a3], [b0, b1, b2, b3]):
+    for mine in ([a, a1, a2, a3], [b, b1, b2, b3]):
         pieces += mine + [other_core(piece) for piece in mine]
     return last, pieces, (side, other_core(side))
 

time: 252 us -> 277 us (1.099)
  waiting for transfers between devices: 83.7 us -> 98.3 us
  blocking collectives: 41.7 us -> 47.4 us
  starting transfers between devices: 39.3 us -> 42.8 us
    ppermute x10, waiting for transfers between devices: 26.9 us -> 59.9 us  [back(): return lax.ppermute(block, EVERYWHERE, route(axis, -1))]
    ppermute x19, waiting for transfers between devices: 51.5 us -> 29 us  [onwards(): return lax.ppermute(block, EVERYWHERE, route(axis, 1))]
    all_to_all x2, blocking collectives: 41.7 us -> 47.4 us  [exchange_and_add(): lax.all_to_all(parts, axis, 0, 0, axis_index_groups=groups, tiled=True)]
    ppermute x10, waiting for transfers between devices: 5.32 us -> 9.38 us  [other_core(): return lax.ppermute(block, EVERYWHERE, pairs)]
  transfers between devices with their start and end apart: 40 -> 40, of which waited for: 22 -> 20; matrix products, arithmetic and copies ran while one was open for 2% -> 2% of each run, Pallas kernels for 1% -> 1%
where the time goes in v5:
time: 277 us
  waiting for transfers between devices  98.3 us (35%)
  Pallas kernels  61.8 us (22%)
  blocking collectives  47.4 us (17%)
  starting transfers between devices  42.8 us (15%)
  between operations  14.4 us (5%)
  local copies, waits for them, and re-layouts  6.57 us (2%)
  other arithmetic  3.82 us (1%)
    ppermute x10, waiting for transfers between devices, back(): return lax.ppermute(block, EVERYWHERE, route(axis, -1))  59.9 us
    pallas_call x1, Pallas kernels, row_gradients(): pl.pallas_call(body, out_shape=(jax.ShapeDtypeStruct(half, BF16), jax.Sha...  56.6 us
    all_to_all x2, blocking collectives, exchange_and_add(): lax.all_to_all(parts, axis, 0, 0, axis_index_groups=groups, tiled=True)  47.4 us
    ppermute x19, waiting for transfers between devices, onwards(): return lax.ppermute(block, EVERYWHERE, route(axis, 1))  29 us
    ppermute x10, starting transfers between devices, back(): return lax.ppermute(block, EVERYWHERE, route(axis, -1))  20.9 us
    ppermute x19, starting transfers between devices, onwards(): return lax.ppermute(block, EVERYWHERE, route(axis, 1))  17.5 us
    ppermute x10, waiting for transfers between devices, other_core(): return lax.ppermute(block, EVERYWHERE, pairs)  9.38 us
  transfers between devices with their start and end apart: 40, of which 20 were waited for; matrix products, arithmetic and copies ran while one was open for 2% of the time, Pallas kernels for 1%

profile of v5, /device:TPU:32, one launch (start us, length us, event | category | flops | bytes accessed | tf_op | source)
XLA Modules:
  0.0 276.8 jit_solution(4485608607949954361)
XLA Ops:
  8.1 3.0 %collective-permute-start.1 = (bf16[16,1536]{1,0:T(8,128)(2,1)S(1)}, bf16[16,1536]{1,0:T(8,128)(2,1)S(1)}, u32[]{:S(2)}, u32[]{:S(2)}) collective-permute-start(bf16[16,1536]{1,0:T(8,128)(2,1)S(1)} %slice_bitcast_fusion.1.refs_0_), channel_id=1, source_target_pairs={{0,48},{1,17},{2,50},{3,19},{4,52},{5,21},{6,54},{7,23},{8,56},{9,... | collective-permute-start | bytes 147464 | tf_op jit(solution)/shard_map/ppermute | solution.py:303
  17.3 3.2 %collective-permute-done.2.refs_1_ = bf16[32,1536]{1,0:T(8,128)(2,1)S(1)} collective-permute-done((bf16[32,1536]{1,0:T(8,128)(2,1)S(1)}, bf16[32,1536]{1,0:T(8,128)(2,1)S(1)}, u32[]{:S(2)}, u32[]{:S(2)}) %collective-permute-start.2) | collective-permute-done | bytes 98336 | tf_op jit(solution)/shard_map/ppermute | solution.py:299
  21.1 3.2 %collective-permute-start.6 = (bf16[32,1536]{1,0:T(8,128)(2,1)S(1)}, bf16[32,1536]{1,0:T(8,128)(2,1)S(1)}, u32[]{:S(2)}, u32[]{:S(2)}) collective-permute-start(bf16[32,1536]{1,0:T(8,128)(2,1)S(1)} %collective-permute-done.3.refs_2_), channel_id=1, source_target_pairs={{0,14},{1,3},{2,0},{3,5},{4,2},{5,7},{6,4},{7,9},{8,6},{9,11},{10,... | collective-permute-start | bytes 294920 | tf_op jit(solution)/shard_map/ppermute | solution.py:303
  27.5 2.8 %collective-permute-start.8 = (bf16[4,16,1536]{2,1,0:T(8,128)(2,1)S(1)}, bf16[4,16,1536]{2,1,0:T(8,128)(2,1)S(1)}, u32[]{:S(2)}, u32[]{:S(2)}) collective-permute-start(bf16[4,16,1536]{2,1,0:T(8,128)(2,1)S(1)} %in_line_y.2.refs_0_), channel_id=1, source_target_pairs={{0,192},{1,65},{2,194},{3,67},{4,196},{5,69},{6,198},{7,71},{8,200... | collective-permute-start | bytes 589832 | tf_op jit(solution)/shard_map/ppermute | solution.py:303
  31.2 3.3 %collective-permute-start.10 = (bf16[32,1536]{1,0:T(8,128)(2,1)S(1)}, bf16[32,1536]{1,0:T(8,128)(2,1)S(1)}, u32[]{:S(2)}, u32[]{:S(2)}) collective-permute-start(bf16[32,1536]{1,0:T(8,128)(2,1)S(1)} %collective-permute-done.6.refs_4_), channel_id=1, source_target_pairs={{0,14},{1,3},{2,0},{3,5},{4,2},{5,7},{6,4},{7,9},{8,6},{9,11},{10,... | collective-permute-start | bytes 294920 | tf_op jit(solution)/shard_map/ppermute | solution.py:303
  34.5 2.7 collective-permute-start.13
  37.2 3.2 %collective-permute-done.9.refs_5_ = bf16[32,1536]{1,0:T(8,128)(2,1)S(1)} collective-permute-done((bf16[32,1536]{1,0:T(8,128)(2,1)S(1)}, bf16[32,1536]{1,0:T(8,128)(2,1)S(1)}, u32[]{:S(2)}, u32[]{:S(2)}) %collective-permute-start.9) | collective-permute-done | bytes 98336 | tf_op jit(solution)/shard_map/ppermute | solution.py:299
  41.7 5.3 %collective-permute-done.12.refs_7_ = bf16[32,1536]{1,0:T(8,128)(2,1)S(1)} collective-permute-done((bf16[32,1536]{1,0:T(8,128)(2,1)S(1)}, bf16[32,1536]{1,0:T(8,128)(2,1)S(1)}, u32[]{:S(2)}, u32[]{:S(2)}) %collective-permute-start.12) | collective-permute-done | bytes 98336 | tf_op jit(solution)/shard_map/ppermute | solution.py:299
  51.2 2.7 collective-permute-start.14
  56.3 5.5 %collective-permute-done.28.refs_1_ = bf16[8,16,1536]{2,1,0:T(8,128)(2,1)S(1)} collective-permute-done((bf16[8,16,1536]{2,1,0:T(8,128)(2,1)S(1)}, bf16[8,16,1536]{2,1,0:T(8,128)(2,1)S(1)}, u32[]{:S(2)}, u32[]{:S(2)}) %collective-permute-start.28) | collective-permute-done | bytes 393248 | tf_op jit(solution)/shard_map/ppermute | solution.py:299
  62.7 2.4 collective-permute-start.15
  65.1 4.5 %collective-permute-done.14.refs_1_ = bf16[2,72,1536]{2,1,0:T(8,128)(2,1)S(1)} collective-permute-done((bf16[2,72,1536]{2,1,0:T(8,128)(2,1)S(1)}, bf16[2,72,1536]{2,1,0:T(8,128)(2,1)S(1)}, u32[]{:S(2)}, u32[]{:S(2)}) %collective-permute-start.14) | collective-permute-done | bytes 442400 | tf_op jit(solution)/shard_map/ppermute | solution.py:299
  71.8 2.0 collective-permute-done.30.refs_3_
  74.6 3.0 %collective-permute-done.19.refs_2_ = bf16[8,16,1536]{2,1,0:T(8,128)(2,1)S(1)} collective-permute-done((bf16[8,16,1536]{2,1,0:T(8,128)(2,1)S(1)}, bf16[8,16,1536]{2,1,0:T(8,128)(2,1)S(1)}, u32[]{:S(2)}, u32[]{:S(2)}) %collective-permute-start.19) | collective-permute-done | bytes 393248 | tf_op jit(solution)/shard_map/ppermute | solution.py:303
  81.5 2.4 collective-permute-start.21
  84.6 2.8 %collective-permute-start.17 = (bf16[4,2,72,1536]{3,2,1,0:T(8,128)(2,1)S(1)}, bf16[4,2,72,1536]{3,2,1,0:T(8,128)(2,1)S(1)}, u32[]{:S(2)}, u32[]{:S(2)}) collective-permute-start(bf16[4,2,72,1536]{3,2,1,0:T(8,128)(2,1)S(1)} %in_line_x.3.refs_5_), channel_id=1, source_target_pairs={{0,1},{1,0},{2,3},{3,2},{4,5},{5,4},{6,7},{7,6},{8,9},{9,8},{10,11... | collective-permute-start | bytes 5308424 | tf_op jit(solution)/shard_map/ppermute | solution.py:291
  87.4 25.2 %collective-permute-done.32.refs_18_ = bf16[4,8,16,1536]{3,2,1,0:T(8,128)(2,1)S(1)} collective-permute-done((bf16[4,8,16,1536]{3,2,1,0:T(8,128)(2,1)S(1)}, bf16[4,8,16,1536]{3,2,1,0:T(8,128)(2,1)S(1)}, u32[]{:S(2)}, u32[]{:S(2)}) %collective-permute-start.32) | collective-permute-done | bytes 1572896 | tf_op jit(solution)/shard_map/ppermute | solution.py:303
  115.9 30.8 %collective-permute-done.22.refs_10_ = bf16[2,2,8,16,1536]{4,3,2,1,0:T(8,128)(2,1)} collective-permute-done((bf16[2,2,8,16,1536]{4,3,2,1,0:T(8,128)(2,1)S(1)}, bf16[2,2,8,16,1536]{4,3,2,1,0:T(8,128)(2,1)}, u32[]{:S(2)}, u32[]{:S(2)}) %collective-permute-start.22) | collective-permute-done | bytes 1572896 | tf_op jit(solution)/shard_map/ppermute | solution.py:303
  155.0 2.2 collective-permute-done.37.refs_23_
  157.2 2.2 collective-permute-done.27.refs_15_
  159.5 56.6 %row_gradients.1 = (bf16[8,16,48,128]{3,2,1,0:T(8,128)(2,1)}, bf16[8,16,48,128]{3,2,1,0:T(8,128)(2,1)}) custom-call(s32[4]{0:T(128)} %copy-done.4, bf16[32,1536]{1,0:T(8,128)(2,1)} %get-tuple-element.48.refs_1_, bf16[32,1536]{1,0:T(8,128)(2,1)} %get-tuple-element.47.refs_2_, f32[32,1536]{1,0:T(8,128)} %fusion.refs_3_, ...), custom_call_target="tpu_custom_call" | custom-call | tf_op jit(solution)/shard_map/row_gradients/pallas_call | solution.py:245
  216.4 3.5 %collective-permute-done.38 = bf16[8,16,48,128]{3,2,1,0:T(8,128)(2,1)S(1)} collective-permute-done((bf16[8,16,48,128]{3,2,1,0:T(8,128)(2,1)}, bf16[8,16,48,128]{3,2,1,0:T(8,128)(2,1)S(1)}, u32[]{:S(2)}, u32[]{:S(2)}) %collective-permute-start.38) | collective-permute-done | bytes 1572896 | tf_op jit(solution)/shard_map/ppermute | solution.py:291
  221.6 28.7 %all_to_all.10 = bf16[8,16,48,128]{3,2,1,0:T(8,128)(2,1)S(1)} all-to-all(bf16[8,16,48,128]{3,2,1,0:T(8,128)(2,1)S(1)} %add_convert_fusion), channel_id=1, replica_groups=mesh['section'=8,'dp'=32] {'section'}, dimensions={0} | all-to-all | bytes 3145728 | tf_op jit(solution)/shard_map/all_to_all | solution.py:375
  250.6 18.7 %all_to_all.11 = bf16[16,48,128]{2,1,0:T(8,128)(2,1)S(1)} all-to-all(bf16[16,48,128]{2,1,0:T(8,128)(2,1)S(1)} %reduce_sum.21), channel_id=1, replica_groups={{0,2,4,6,8,10,12,14,16,18,20,22,24,26,28,30},{1,3,5,7,9,11,13,15,17,19,..., dimensions={0} | all-to-all | bytes 393216 | tf_op jit(solution)/shard_map/all_to_all | solution.py:375
  (108 shorter events, 42.6 us)
Async XLA Ops:
  7.2 152.3 %all-gather.2.cloned.1.call-start = ((), (), s32[]{:S(2)}) async-start(), calls=%async_computation.2 | async-start | bytes 13369344 | tf_op jit(solution)/shard_map/all_gather | solution.py:358
  12.8 7.7 %collective-permute-start.2 = (bf16[32,1536]{1,0:T(8,128)(2,1)S(1)}, bf16[32,1536]{1,0:T(8,128)(2,1)S(1)}, u32[]{:S(2)}, u32[]{:S(2)}) collective-permute-start(bf16[32,1536]{1,0:T(8,128)(2,1)S(1)} %slice_bitcast_fusion.refs_0_), channel_id=1, source_target_pairs={{0,2},{1,15},{2,4},{3,1},{4,6},{5,3},{6,8},{7,5},{8,10},{9,7},{10,... | collective-permute-start | bytes 294920 | tf_op jit(solution)/shard_map/ppermute | solution.py:299
  27.5 12.8 %collective-permute-start.8 = (bf16[4,16,1536]{2,1,0:T(8,128)(2,1)S(1)}, bf16[4,16,1536]{2,1,0:T(8,128)(2,1)S(1)}, u32[]{:S(2)}, u32[]{:S(2)}) collective-permute-start(bf16[4,16,1536]{2,1,0:T(8,128)(2,1)S(1)} %in_line_y.2.refs_0_), channel_id=1, source_target_pairs={{0,192},{1,65},{2,194},{3,67},{4,196},{5,69},{6,198},{7,71},{8,200... | collective-permute-start | bytes 589832 | tf_op jit(solution)/shard_map/ppermute | solution.py:303
  30.4 10.0 %collective-permute-start.7 = (bf16[4,16,1536]{2,1,0:T(8,128)(2,1)S(1)}, bf16[4,16,1536]{2,1,0:T(8,128)(2,1)S(1)}, u32[]{:S(2)}, u32[]{:S(2)}) collective-permute-start(bf16[4,16,1536]{2,1,0:T(8,128)(2,1)S(1)} %in_line_y.2.refs_0_), channel_id=1, source_target_pairs={{0,64},{1,193},{2,66},{3,195},{4,68},{5,197},{6,70},{7,199},{8,72}... | collective-permute-start | bytes 589832 | tf_op jit(solution)/shard_map/ppermute | solution.py:299
  49.4 12.5 %collective-permute-start.28 = (bf16[8,16,1536]{2,1,0:T(8,128)(2,1)S(1)}, bf16[8,16,1536]{2,1,0:T(8,128)(2,1)S(1)}, u32[]{:S(2)}, u32[]{:S(2)}) collective-permute-start(bf16[8,16,1536]{2,1,0:T(8,128)(2,1)S(1)} %get-tuple-element.39.refs_0_), channel_id=1, source_target_pairs={{0,64},{1,193},{2,66},{3,195},{4,68},{5,197},{6,70},{7,199},{8,72}... | collective-permute-start | bytes 1179656 | tf_op jit(solution)/shard_map/ppermute | solution.py:299
  51.2 18.4 %collective-permute-start.14 = (bf16[2,72,1536]{2,1,0:T(8,128)(2,1)S(1)}, bf16[2,72,1536]{2,1,0:T(8,128)(2,1)S(1)}, u32[]{:S(2)}, u32[]{:S(2)}) collective-permute-start(bf16[2,72,1536]{2,1,0:T(8,128)(2,1)S(1)} %in_line_half.1.refs_0_), channel_id=1, source_target_pairs={{0,64},{1,193},{2,66},{3,195},{4,68},{5,197},{6,70},{7,199},{8,72}... | collective-permute-start | bytes 1327112 | tf_op jit(solution)/shard_map/ppermute | solution.py:299
  53.9 15.9 %collective-permute-start.18 = (bf16[8,16,1536]{2,1,0:T(8,128)(2,1)S(1)}, bf16[8,16,1536]{2,1,0:T(8,128)(2,1)S(1)}, u32[]{:S(2)}, u32[]{:S(2)}) collective-permute-start(bf16[8,16,1536]{2,1,0:T(8,128)(2,1)S(1)} %get-tuple-element.38.refs_0_), channel_id=1, source_target_pairs={{0,16},{1,49},{2,18},{3,51},{4,20},{5,53},{6,22},{7,55},{8,24},{9,... | collective-permute-start | bytes 1179656 | tf_op jit(solution)/shard_map/ppermute | solution.py:299
  55.5 15.1 %collective-permute-start.29 = (bf16[8,16,1536]{2,1,0:T(8,128)(2,1)S(1)}, bf16[8,16,1536]{2,1,0:T(8,128)(2,1)S(1)}, u32[]{:S(2)}, u32[]{:S(2)}) collective-permute-start(bf16[8,16,1536]{2,1,0:T(8,128)(2,1)S(1)} %get-tuple-element.39.refs_0_), channel_id=1, source_target_pairs={{0,192},{1,65},{2,194},{3,67},{4,196},{5,69},{6,198},{7,71},{8,200... | collective-permute-start | bytes 1179656 | tf_op jit(solution)/shard_map/ppermute | solution.py:303
  61.8 12.0 %collective-permute-start.30 = (bf16[8,16,1536]{2,1,0:T(8,128)(2,1)S(1)}, bf16[8,16,1536]{2,1,0:T(8,128)(2,1)S(1)}, u32[]{:S(2)}, u32[]{:S(2)}) collective-permute-start(bf16[8,16,1536]{2,1,0:T(8,128)(2,1)S(1)} %collective-permute-done.28.refs_1_), channel_id=1, source_target_pairs={{0,64},{1,193},{2,66},{3,195},{4,68},{5,197},{6,70},{7,199},{8,72}... | collective-permute-start | bytes 1179656 | tf_op jit(solution)/shard_map/ppermute | solution.py:299
  62.7 18.7 %collective-permute-start.15 = (bf16[2,72,1536]{2,1,0:T(8,128)(2,1)S(1)}, bf16[2,72,1536]{2,1,0:T(8,128)(2,1)S(1)}, u32[]{:S(2)}, u32[]{:S(2)}) collective-permute-start(bf16[2,72,1536]{2,1,0:T(8,128)(2,1)S(1)} %in_line_half.1.refs_0_), channel_id=1, source_target_pairs={{0,192},{1,65},{2,194},{3,67},{4,196},{5,69},{6,198},{7,71},{8,200... | collective-permute-start | bytes 1327112 | tf_op jit(solution)/shard_map/ppermute | solution.py:303
  69.6 11.9 %collective-permute-start.16 = (bf16[2,72,1536]{2,1,0:T(8,128)(2,1)S(1)}, bf16[2,72,1536]{2,1,0:T(8,128)(2,1)S(1)}, u32[]{:S(2)}, u32[]{:S(2)}) collective-permute-start(bf16[2,72,1536]{2,1,0:T(8,128)(2,1)S(1)} %collective-permute-done.14.refs_1_), channel_id=1, source_target_pairs={{0,64},{1,193},{2,66},{3,195},{4,68},{5,197},{6,70},{7,199},{8,72}... | collective-permute-start | bytes 1327112 | tf_op jit(solution)/shard_map/ppermute | solution.py:299
  69.8 7.8 %collective-permute-start.19 = (bf16[8,16,1536]{2,1,0:T(8,128)(2,1)S(1)}, bf16[8,16,1536]{2,1,0:T(8,128)(2,1)S(1)}, u32[]{:S(2)}, u32[]{:S(2)}) collective-permute-start(bf16[8,16,1536]{2,1,0:T(8,128)(2,1)S(1)} %get-tuple-element.38.refs_0_), channel_id=1, source_target_pairs={{0,48},{1,17},{2,50},{3,19},{4,52},{5,21},{6,54},{7,23},{8,56},{9,... | collective-permute-start | bytes 1179656 | tf_op jit(solution)/shard_map/ppermute | solution.py:303
  70.6 9.6 %collective-permute-start.20 = (bf16[8,16,1536]{2,1,0:T(8,128)(2,1)S(1)}, bf16[8,16,1536]{2,1,0:T(8,128)(2,1)S(1)}, u32[]{:S(2)}, u32[]{:S(2)}) collective-permute-start(bf16[8,16,1536]{2,1,0:T(8,128)(2,1)S(1)} %collective-permute-done.18.refs_1_), channel_id=1, source_target_pairs={{0,16},{1,49},{2,18},{3,51},{4,20},{5,53},{6,22},{7,55},{8,24},{9,... | collective-permute-start | bytes 1179656 | tf_op jit(solution)/shard_map/ppermute | solution.py:299
  74.5 10.1 %collective-permute-start.34 = (bf16[4,8,16,1536]{3,2,1,0:T(8,128)(2,1)S(1)}, bf16[4,8,16,1536]{3,2,1,0:T(8,128)(2,1)S(1)}, u32[]{:S(2)}, u32[]{:S(2)}) collective-permute-start(bf16[4,8,16,1536]{3,2,1,0:T(8,128)(2,1)S(1)} %in_line_x.5.refs_16_), channel_id=1, source_target_pairs={{0,1},{1,0},{2,3},{3,2},{4,5},{5,4},{6,7},{7,6},{8,9},{9,8},{10,11... | collective-permute-start | bytes 4718600 | tf_op jit(solution)/shard_map/ppermute | solution.py:291
  77.6 35.0 %collective-permute-start.32 = (bf16[4,8,16,1536]{3,2,1,0:T(8,128)(2,1)S(1)}, bf16[4,8,16,1536]{3,2,1,0:T(8,128)(2,1)S(1)}, u32[]{:S(2)}, u32[]{:S(2)}) collective-permute-start(bf16[4,8,16,1536]{3,2,1,0:T(8,128)(2,1)S(1)} %in_line_x.5.refs_16_), channel_id=1, source_target_pairs={{0,48},{1,17},{2,50},{3,19},{4,52},{5,21},{6,54},{7,23},{8,56},{9,... | collective-permute-start | bytes 4718600 | tf_op jit(solution)/shard_map/ppermute | solution.py:303
  80.2 34.2 %collective-permute-start.31 = (bf16[4,8,16,1536]{3,2,1,0:T(8,128)(2,1)S(1)}, bf16[4,8,16,1536]{3,2,1,0:T(8,128)(2,1)}, u32[]{:S(2)}, u32[]{:S(2)}) collective-permute-start(bf16[4,8,16,1536]{3,2,1,0:T(8,128)(2,1)S(1)} %in_line_x.5.refs_16_), channel_id=1, source_target_pairs={{0,16},{1,49},{2,18},{3,51},{4,20},{5,53},{6,22},{7,55},{8,24},{9,... | collective-permute-start | bytes 4718600 | tf_op jit(solution)/shard_map/ppermute | solution.py:299
  81.4 32.9 %collective-permute-start.24 = (bf16[2,2,8,16,1536]{4,3,2,1,0:T(8,128)(2,1)S(1)}, bf16[2,2,8,16,1536]{4,3,2,1,0:T(8,128)(2,1)S(1)}, u32[]{:S(2)}, u32[]{:S(2)}) collective-permute-start(bf16[2,2,8,16,1536]{4,3,2,1,0:T(8,128)(2,1)S(1)} %bitcast.19), channel_id=1, source_target_pairs={{0,1},{1,0},{2,3},{3,2},{4,5},{5,4},{6,7},{7,6},{8,9},{9,8},{10,11... | collective-permute-start | bytes 4718600 | tf_op jit(solution)/shard_map/ppermute | solution.py:291
  81.5 34.4 %collective-permute-start.21 = (bf16[2,2,8,16,1536]{4,3,2,1,0:T(8,128)(2,1)S(1)}, bf16[2,2,8,16,1536]{4,3,2,1,0:T(8,128)(2,1)}, u32[]{:S(2)}, u32[]{:S(2)}) collective-permute-start(bf16[2,2,8,16,1536]{4,3,2,1,0:T(8,128)(2,1)S(1)} %bitcast.20), channel_id=1, source_target_pairs={{0,64},{1,193},{2,66},{3,195},{4,68},{5,197},{6,70},{7,199},{8,72}... | collective-permute-start | bytes 4718600 | tf_op jit(solution)/shard_map/ppermute | solution.py:299
  84.6 62.1 %collective-permute-start.17 = (bf16[4,2,72,1536]{3,2,1,0:T(8,128)(2,1)S(1)}, bf16[4,2,72,1536]{3,2,1,0:T(8,128)(2,1)S(1)}, u32[]{:S(2)}, u32[]{:S(2)}) collective-permute-start(bf16[4,2,72,1536]{3,2,1,0:T(8,128)(2,1)S(1)} %in_line_x.3.refs_5_), channel_id=1, source_target_pairs={{0,1},{1,0},{2,3},{3,2},{4,5},{5,4},{6,7},{7,6},{8,9},{9,8},{10,11... | collective-permute-start | bytes 5308424 | tf_op jit(solution)/shard_map/ppermute | solution.py:291
  112.6 34.1 %collective-permute-start.22 = (bf16[2,2,8,16,1536]{4,3,2,1,0:T(8,128)(2,1)S(1)}, bf16[2,2,8,16,1536]{4,3,2,1,0:T(8,128)(2,1)}, u32[]{:S(2)}, u32[]{:S(2)}) collective-permute-start(bf16[2,2,8,16,1536]{4,3,2,1,0:T(8,128)(2,1)S(1)} %bitcast.21), channel_id=1, source_target_pairs={{0,192},{1,65},{2,194},{3,67},{4,196},{5,69},{6,198},{7,71},{8,200... | collective-permute-start | bytes 4718600 | tf_op jit(solution)/shard_map/ppermute | solution.py:303
  114.3 34.1 %collective-permute-start.36 = (bf16[4,8,16,1536]{3,2,1,0:T(8,128)(2,1)S(1)}, bf16[4,8,16,1536]{3,2,1,0:T(8,128)(2,1)S(1)}, u32[]{:S(2)}, u32[]{:S(2)}) collective-permute-start(bf16[4,8,16,1536]{3,2,1,0:T(8,128)(2,1)S(1)} %collective-permute-done.32.refs_18_), channel_id=1, source_target_pairs={{0,1},{1,0},{2,3},{3,2},{4,5},{5,4},{6,7},{7,6},{8,9},{9,8},{10,11... | collective-permute-start | bytes 4718600 | tf_op jit(solution)/shard_map/ppermute | solution.py:291
  114.4 34.2 %collective-permute-start.33 = (bf16[4,8,16,1536]{3,2,1,0:T(8,128)(2,1)}, bf16[4,8,16,1536]{3,2,1,0:T(8,128)(2,1)}, u32[]{:S(2)}, u32[]{:S(2)}) collective-permute-start(bf16[4,8,16,1536]{3,2,1,0:T(8,128)(2,1)} %collective-permute-done.31.refs_17_), channel_id=1, source_target_pairs={{0,16},{1,49},{2,18},{3,51},{4,20},{5,53},{6,22},{7,55},{8,24},{9,... | collective-permute-start | bytes 4718600 | tf_op jit(solution)/shard_map/ppermute | solution.py:299
  115.9 33.7 %collective-permute-start.23 = (bf16[2,2,8,16,1536]{4,3,2,1,0:T(8,128)(2,1)}, bf16[2,2,8,16,1536]{4,3,2,1,0:T(8,128)(2,1)}, u32[]{:S(2)}, u32[]{:S(2)}) collective-permute-start(bf16[2,2,8,16,1536]{4,3,2,1,0:T(8,128)(2,1)} %collective-permute-done.21.refs_9_), channel_id=1, source_target_pairs={{0,64},{1,193},{2,66},{3,195},{4,68},{5,197},{6,70},{7,199},{8,72}... | collective-permute-start | bytes 4718600 | tf_op jit(solution)/shard_map/ppermute | solution.py:299
  149.6 9.8 %collective-permute-start.27 = (bf16[2,2,8,16,1536]{4,3,2,1,0:T(8,128)(2,1)}, bf16[2,2,8,16,1536]{4,3,2,1,0:T(8,128)(2,1)}, u32[]{:S(2)}, u32[]{:S(2)}) collective-permute-start(bf16[2,2,8,16,1536]{4,3,2,1,0:T(8,128)(2,1)} %collective-permute-done.23.refs_11_), channel_id=1, source_target_pairs={{0,1},{1,0},{2,3},{3,2},{4,5},{5,4},{6,7},{7,6},{8,9},{9,8},{10,11... | collective-permute-start | bytes 4718600 | tf_op jit(solution)/shard_map/ppermute | solution.py:291
  (29 other events, 756.8 us)
Sparse Core Ops, SparseCore 0:
  48.9 75.2 all-gather.1
